TPU v7x, 256 devices: a whole 4x4x8 slice. The times are simulated.
256 devices in a mesh: seq: 64 (over y, z, core), utt: 4 (over x).
Axes of the slice: x: 4, y: 4, z: 8, core: 2. Of those that a mesh axis runs over, the one named last changes fastest.
Arguments:
- features: bfloat16 [4, 16384, 1024], P('utt', 'seq'), may hold values from -6 to 6
- cotangent: bfloat16 [4, 16384, 1024], P('utt', 'seq'), may hold values from -100 to 100
- conv_kernel: float32 [31, 1024], replicated, may hold values from -1 to 1
- norm_gain: float32 [1024], replicated, may hold values from 0.25 to 1.75
- weight_in: bfloat16 [1024, 4096], P('seq', 'utt'), may hold values from -0.1875 to 0.1875
- weight_out: bfloat16 [4096, 1024], P(('utt', 'seq')), may hold values from -0.09375 to 0.09375
- keep_count: int32 [4, 64], P('utt'), may hold values from 0 to 256, as said below
- keep_index: int32 [4, 16384], P('utt', 'seq'), may hold values from 0 to 255, as said below
Outputs:
- grad_features: bfloat16 [4, 16384, 1024], P('utt', 'seq')
- grad_weight_in: float32 [1024, 4096], P('seq', 'utt')
- grad_weight_out: float32 [4096, 1024], P(('utt', 'seq'))
- grad_kernel: float32 [31, 1024], replicated
- grad_gain: float32 [1024], replicated
Inputs may be any that keep to these rules, and one draw needn't show every extreme that they name: keep_count[u, s] counts the kept frames of shard s (frames s * 256 to (s + 1) * 256 - 1) of utterance u. With the blocks of a shard being its count divided by 128 and rounded up, the shards before shard s hold between s * 1 and (s + 1) * 1 blocks, and the 64 shards of an utterance hold exactly 64 blocks. For shard s of utterance u, the entries keep_index[u, s * 256 + j] with j below keep_count[u, s] are distinct frame indices within the shard in rising order; the other entries are 0.
All inputs are finite; a program needn't handle non-finite values.
Results may differ from a plain program's by a relative error of at most 0.0085.
Values may be sent and summed in bfloat16 or wider, within the bound.
No kernel may reach another device: no remote copies, remote signals or barrier semaphores. Data moves between devices by JAX's collectives and lax.ppermute only.
A program may use at most 64 MiB of HBM per device.

v0:
```python
import jax
import jax.numpy as jnp
from jax import lax
from jax.sharding import PartitionSpec as P

norm_eps = 1e-05


def with_halo(cells, sides, width):
    for axis, dim in sides:
        count = lax.axis_size(axis)
        ends = count - 1
        head = lax.slice_in_dim(cells, 0, width, axis=dim)
        tail = lax.slice_in_dim(cells, cells.shape[dim] - width, cells.shape[dim], axis=dim)
        cells = jnp.concatenate(
            [
                lax.ppermute(tail, axis, [(i, (i + 1) % count) for i in range(ends)]),
                cells,
                lax.ppermute(head, axis, [((i + 1) % count, i) for i in range(ends)]),
            ],
            axis=dim,
        )
    return cells


def silu_grad(values):
    sigmoid = jax.nn.sigmoid(values)
    return sigmoid * (1.0 + values * (1.0 - sigmoid))


def depthwise(padded, kernel, length):
    running = jnp.zeros((length, padded.shape[1]), jnp.float32)
    for offset in range(kernel.shape[0]):
        running = running + kernel[offset] * padded[offset : offset + length]
    return running


def per_device(
    features, cotangent, conv_kernel, norm_gain, weight_in, weight_out, keep_count, keep_index
):
    frames = features[0]
    length = frames.shape[0]
    width = frames.shape[1]
    half_width = conv_kernel.shape[0] // 2
    wide_rows = with_halo(frames, (("seq", 0),), half_width)
    wide32 = wide_rows.astype(jnp.float32)
    conv_out = depthwise(wide32, conv_kernel, length)
    hidden = (frames.astype(jnp.float32) + jax.nn.silu(conv_out)).astype(jnp.bfloat16)
    my_shard = lax.axis_index("seq")
    counts = keep_count[0]
    local_index = keep_index[0]
    valid_slot = jnp.arange(length, dtype=jnp.int32) < counts[my_shard]
    zero_bf = jnp.zeros((), jnp.bfloat16)
    picked = jnp.where(valid_slot[:, None], hidden[local_index], zero_bf)
    picked_grad = jnp.where(valid_slot[:, None], cotangent[0][local_index], zero_bf)
    rows32 = picked.astype(jnp.float32)
    row_mean = jnp.mean(rows32, axis=1, keepdims=True)
    centred = rows32 - row_mean
    row_var = jnp.mean(centred * centred, axis=1, keepdims=True)
    inv_scale = lax.rsqrt(row_var + norm_eps)
    normed = centred * inv_scale
    scaled = (normed * norm_gain).astype(jnp.bfloat16)
    scaled_all, grad_all = (
        lax.all_gather(scaled, "utt", axis=0, tiled=True),
        lax.all_gather(picked_grad, "utt", axis=0, tiled=True),
    )
    columns = scaled_all
    pre_act = jnp.dot(
        columns,
        lax.all_gather(weight_in, "seq", axis=0, tiled=True),
        preferred_element_type=jnp.float32,
    )
    activation = jax.nn.silu(pre_act).astype(jnp.bfloat16)
    act_grad = 0.5 * lax.dot_general(
        grad_all,
        lax.all_gather(weight_out, "seq", axis=0, tiled=True),
        (((1,), (1,)), ((), ())),
        preferred_element_type=jnp.float32,
    )
    up_grad = (act_grad * silu_grad(pre_act)).astype(jnp.bfloat16)
    columns = scaled_all
    grad_weight_in = lax.psum_scatter(
        lax.dot_general(
            columns, up_grad, (((0,), (0,)), ((), ())), preferred_element_type=jnp.float32
        ),
        "seq",
        scatter_dimension=0,
        tiled=True,
    )
    columns = activation
    grad_weight_out = lax.psum_scatter(
        0.5
        * lax.dot_general(
            columns, grad_all, (((0,), (0,)), ((), ())), preferred_element_type=jnp.float32
        ),
        "seq",
        scatter_dimension=0,
        tiled=True,
    )
    partial_grad = lax.dot_general(
        up_grad,
        lax.all_gather(weight_in, "seq", axis=0, tiled=True),
        (((1,), (1,)), ((), ())),
        preferred_element_type=jnp.float32,
    )
    norm_grad = lax.psum_scatter(partial_grad, "utt", scatter_dimension=0, tiled=True)
    gain_term = jnp.sum(norm_grad * normed, axis=0)
    gain_grad = norm_grad * norm_gain
    back_term = (
        gain_grad
        - jnp.mean(gain_grad, axis=1, keepdims=True)
        - normed * jnp.mean(gain_grad * normed, axis=1, keepdims=True)
    ) * inv_scale
    row_grad = (picked_grad.astype(jnp.float32) + back_term).astype(jnp.bfloat16)
    local_grad = row_grad.astype(jnp.float32)
    frame_grad = (
        jnp.zeros((length, width), jnp.float32)
        .at[local_index]
        .add(jnp.where(valid_slot[:, None], local_grad, 0.0))
    )
    conv_grad = frame_grad * silu_grad(conv_out)
    grad_wide = with_halo(conv_grad, (("seq", 0),), half_width)
    tap_count = conv_kernel.shape[0]
    transposed = jnp.zeros((length, width), jnp.float32)
    for offset in range(tap_count):
        begin = 2 * half_width - offset
        transposed = transposed + conv_kernel[offset] * grad_wide[begin : begin + length]
    kernel_term = jnp.stack(
        [
            jnp.sum(conv_grad * wide32[offset : offset + length], axis=0)
            for offset in range(tap_count)
        ]
    )
    grad_x = (frame_grad + transposed).astype(jnp.bfloat16)
    kernel_sum, gain_sum = lax.psum((kernel_term, gain_term), ("seq", "utt"))
    return (grad_x[None], grad_weight_in, grad_weight_out, kernel_sum, gain_sum)


def solution(mesh):
    placed = (
        P("utt", "seq", None),
        P("utt", "seq", None),
        P(),
        P(),
        P("seq", "utt"),
        P(("utt", "seq"), None),
        P("utt", None),
        P("utt", "seq"),
    )
    return jax.shard_map(
        per_device,
        mesh=mesh,
        in_specs=placed,
        out_specs=(P("utt", "seq", None), P("seq", "utt"), P(("utt", "seq"), None), P(), P()),
        check_vma=False,
    )
```

profile of v0, /device:TPU:2, one launch (start us, length us, event | category | flops | bytes accessed | tf_op | source)
XLA Modules:
  0.0 873.7 jit_solution(4482847801487876634)
XLA Ops:
  7.2 0.0 copy-start
  7.2 0.0 copy-start.1
  7.2 0.0 all-gather.9.cloned.1.call-start
  7.2 0.9 slice_bitcast_fusion.1
  8.1 1.7 collective-permute-start
  9.9 1.3 collective-permute-start.1
  11.2 1.1 fusion.115
  12.3 1.4 fusion.114
  13.7 0.7 compare_select_fusion
  14.4 1.2 constant_dynamic-slice_fusion
  15.6 0.6 iota_compare_fusion
  16.3 0.0 collective-permute-done
  16.3 0.0 collective-permute-done.1
  16.3 1.2 maximum_convert_fusion
  17.5 5.2 add_convert_fusion
  22.7 1.2 gather_fusion.1
  23.8 0.3 convert_reduce_fusion
  24.1 0.3 fusion.13
  24.4 1.3 fusion.6
  25.7 0.0 all-gather.9.cloned.1.call-update
  25.8 0.0 all-gather.11.cloned.1.call-start
  25.8 0.7 all-gather.11.cloned.1.call-update
  26.5 0.0 all-gather.5.cloned.1.call-start
  26.6 1.2 gather_fusion
  27.7 0.9 broadcast_select_fusion.1
  28.6 0.0 all-gather.5.cloned.1.call-update
  28.7 0.0 all-gather.7.cloned.1.call-start
  28.7 0.5 all-gather.7.cloned.1.call-update
  29.2 0.0 reduce-scatter.4.cloned.1.call-start
  29.3 35.7 %all-gather.9.cloned.1.call-done = bf16[1024,1024]{1,0:T(8,128)(2,1)} async-done(((bf16[256,1024]{1,0:T(8,128)(2,1)}), bf16[1024,1024]{1,0:T(8,128)(2,1)}) %all-gather.9.cloned.1.call-update) | async-done | bytes 2097168 | tf_op jit(solution)/shard_map/all_gather | solution.py:64
  65.0 81.4 %all-gather.11.cloned.1.call-done = bf16[1024,1024]{1,0:T(8,128)(2,1)} async-done(((bf16[16,1024]{1,0:T(8,128)(2,1)}), bf16[1024,1024]{1,0:T(8,128)(2,1)}) %all-gather.11.cloned.1.call-update) | async-done | bytes 2097168 | tf_op jit(solution)/shard_map/all_gather | solution.py:70
  146.4 6.5 fusion.116
  152.9 25.1 %all-gather.5.cloned.1.call-done = bf16[1024,1024]{1,0:T(8,128)(2,1)} async-done(((bf16[256,1024]{1,0:T(8,128)(2,1)}), bf16[1024,1024]{1,0:T(8,128)(2,1)}) %all-gather.5.cloned.1.call-update) | async-done | bytes 2097168 | tf_op jit(solution)/shard_map/all_gather | solution.py:65
  178.0 81.2 %all-gather.7.cloned.1.call-done = bf16[1024,1024]{1,0:T(8,128)(2,1)} async-done(((bf16[16,1024]{1,0:T(8,128)(2,1)}), bf16[1024,1024]{1,0:T(8,128)(2,1)}) %all-gather.7.cloned.1.call-update) | async-done | bytes 2097168 | tf_op jit(solution)/shard_map/all_gather | solution.py:76
  259.2 6.8 multiply_convert_fusion.1
  266.0 0.0 copy-start.4
  266.0 1.3 copy-done.4
  267.3 0.0 copy-done.3
  267.3 4.4 fusion.117
  271.7 0.0 reduce-scatter.4.cloned.1.call-update
  271.7 0.2 reduce-scatter.8.cloned.1.call-start
  271.9 7.2 convolution_multiply_fusion
  279.2 0.0 reduce-scatter.8.cloned.1.call-update
  279.2 0.0 reduce-scatter.6.cloned.1.call-start
  279.3 7.3 fusion.118
  286.6 0.0 reduce-scatter.6.cloned.1.call-update
  286.6 0.0 all-reduce.2.cloned.1.call-start
  286.6 30.8 %reduce-scatter.4.cloned.1.call-done = f32[256,1024]{1,0:T(8,128)} async-done(((f32[1024,1024]{1,0:T(8,128)}), f32[256,1024]{1,0:T(8,128)}) %reduce-scatter.4.cloned.1.call-update) | async-done | bytes 1048592 | tf_op jit(solution)/shard_map/reduce_scatter | solution.py:106
  317.4 1.8 fusion.12
  319.2 4.9 scatter_custom_fusion
  324.1 4.0 multiply_reduce_fusion
  328.1 1.3 collective-permute-start.2
  329.4 3.0 collective-permute-start.3
  332.5 1.8 multiply_reduce_fusion.1
  334.3 2.7 stack.127
  336.9 0.0 all-reduce.2.cloned.1.call-update
  336.9 79.0 %psum.15 = f32[1024]{0:T(1024)} all-reduce(f32[1024]{0:T(1024)S(1)} %get-tuple-element.36), channel_id=1, replica_groups=mesh['seq'=64,'utt'=4] {'seq','utt'}, use_global_device_ids=true, to_apply=%region_41.42 | all-reduce | flops 1024 | bytes 8192 | tf_op jit(solution)/shard_map/psum | solution.py:135
  416.0 0.0 collective-permute-done.2
  416.0 0.0 collective-permute-done.3
  416.0 6.4 fusion.111
  422.4 45.3 %reduce-scatter.8.cloned.1.call-done = f32[16,1024]{1,0:T(8,128)} async-done(((f32[1024,1024]{1,0:T(8,128)}), f32[16,1024]{1,0:T(8,128)}) %reduce-scatter.8.cloned.1.call-update) | async-done | bytes 65552 | tf_op jit(solution)/shard_map/reduce_scatter | solution.py:91
  467.6 147.4 %reduce-scatter.6.cloned.1.call-done = f32[16,1024]{1,0:T(8,128)} async-done(((f32[1024,1024]{1,0:T(8,128)}), f32[16,1024]{1,0:T(8,128)}) %reduce-scatter.6.cloned.1.call-update) | async-done | bytes 65552 | tf_op jit(solution)/shard_map/reduce_scatter | solution.py:82
  615.1 250.2 %all-reduce.2.cloned.1.call-done = f32[31,1024]{1,0:T(8,128)} async-done(((f32[31,1024]{1,0:T(8,128)}), f32[31,1024]{1,0:T(8,128)}) %all-reduce.2.cloned.1.call-update) | async-done | bytes 126992 | tf_op jit(solution)/shard_map/psum | solution.py:135
  865.3 1.6 copy.14
  (10 shorter events, 0.0 us)
Async XLA Ops:
  7.2 19.4 %copy-start = (bf16[1,256,1024]{2,1,0:T(8,128)(2,1)S(1)}, bf16[1,256,1024]{2,1,0:T(8,128)(2,1)}, u32[]{:S(2)}) copy-start(bf16[1,256,1024]{2,1,0:T(8,128)(2,1)} %param.9) | copy-start | bytes 1572868
  7.2 10.3 %copy-start.1 = (bf16[1,256,1024]{2,1,0:T(8,128)(2,1)S(1)}, bf16[1,256,1024]{2,1,0:T(8,128)(2,1)}, u32[]{:S(2)}) copy-start(bf16[1,256,1024]{2,1,0:T(8,128)(2,1)} %param.8) | copy-start | bytes 1572868
  7.2 57.8 %all-gather.9.cloned.1.call-start = ((), (), s32[]{:S(2)}) async-start(), calls=%async_computation.5 | async-start | bytes 2621440 | tf_op jit(solution)/shard_map/all_gather | solution.py:64
  8.1 8.1 collective-permute-start
  9.9 6.4 collective-permute-start.1
  22.7 1.8 copy-start.2
  25.8 120.6 %all-gather.11.cloned.1.call-start = ((), (), s32[]{:S(2)}) async-start(), calls=%async_computation.6 | async-start | bytes 2129920 | tf_op jit(solution)/shard_map/all_gather | solution.py:70
  26.5 151.5 %all-gather.5.cloned.1.call-start = ((), (), s32[]{:S(2)}) async-start(), calls=%async_computation.3 | async-start | bytes 2621440 | tf_op jit(solution)/shard_map/all_gather | solution.py:65
  28.7 230.5 %all-gather.7.cloned.1.call-start = ((), (), s32[]{:S(2)}) async-start(), calls=%async_computation.4 | async-start | bytes 2129920 | tf_op jit(solution)/shard_map/all_gather | solution.py:76
  29.2 288.2 %reduce-scatter.4.cloned.1.call-start = ((), (), s32[]{:S(2)}) async-start(), calls=%async_computation.7 | async-start | bytes 5242880 | tf_op jit(solution)/shard_map/reduce_scatter | solution.py:106
  259.2 8.1 copy-start.3
  266.0 1.4 copy-start.4
  271.7 195.9 %reduce-scatter.8.cloned.1.call-start = ((), (), s32[]{:S(2)}) async-start(), calls=%async_computation.9 | async-start | bytes 4259840 | tf_op jit(solution)/shard_map/reduce_scatter | solution.py:91
  279.2 335.9 %reduce-scatter.6.cloned.1.call-start = ((), (), s32[]{:S(2)}) async-start(), calls=%async_computation.8 | async-start | bytes 4259840 | tf_op jit(solution)/shard_map/reduce_scatter | solution.py:82
  286.6 578.7 %all-reduce.2.cloned.1.call-start = ((), (), s32[]{:S(2)}) async-start(), calls=%async_computation.10 | async-start | bytes 262144 | tf_op jit(solution)/shard_map/psum | solution.py:135
  328.1 87.8 %collective-permute-start.2 = (f32[15,1024]{1,0:T(8,128)S(1)}, f32[15,1024]{1,0:T(8,128)S(1)}, u32[]{:S(2)}, u32[]{:S(2)}) collective-permute-start(f32[15,1024]{1,0:T(8,128)S(1)} %get-tuple-element.42), channel_id=1, source_target_pairs={{4,0},{8,4},{12,8},{16,12},{20,16},{24,20},{28,24},{32,28},{36,32}... | collective-permute-start | bytes 184328 | tf_op jit(solution)/shard_map/ppermute | solution.py:19
  329.4 86.5 %collective-permute-start.3 = (f32[15,1024]{1,0:T(8,128)S(1)}, f32[15,1024]{1,0:T(8,128)S(1)}, u32[]{:S(2)}, u32[]{:S(2)}) collective-permute-start(f32[15,1024]{1,0:T(8,128)S(1)} %get-tuple-element.43), channel_id=1, source_target_pairs={{0,4},{4,8},{8,12},{12,16},{16,20},{20,24},{24,28},{28,32},{32,36}... | collective-permute-start | bytes 184328 | tf_op jit(solution)/shard_map/ppermute | solution.py:17
Sparse Core Ops, SparseCore 0:
  25.9 39.0 all-gather.8
  67.7 78.5 all-gather.10
  148.2 29.7 all-gather.4
  180.6 78.5 all-gather.6
  271.8 45.5 reduce-scatter.3
  322.0 145.6 reduce-scatter.7
  472.3 142.6 reduce-scatter.5
  621.1 244.0 all-reduce.1
where the time goes:
time: 874 us
  waiting for transfers between devices  698 us (80%)
  blocking collectives  79 us (9%)
  matrix products  32.2 us (4%)
  other arithmetic  29.3 us (3%)
  between operations  14.3 us (2%)
  local copies, waits for them, and re-layouts  12.5 us (1%)
    psum x1, waiting for transfers between devices, per_device(): kernel_sum, gain_sum = lax.psum((kernel_term, gain_term), ('seq', 'utt'))  250 us
    reduce_scatter x1, waiting for transfers between devices, per_device(): lax.psum_scatter(lax.dot_general(columns, up_grad, (((0,), (0,)), ((), ()...  147 us
    all_gather x1, waiting for transfers between devices, per_device(): lax.all_gather(weight_in, 'seq', axis=0, tiled=True)  81.4 us
    all_gather x1, waiting for transfers between devices, per_device(): lax.all_gather(weight_out, 'seq', axis=0, tiled=True)  81.2 us
    psum x1, blocking collectives, per_device(): kernel_sum, gain_sum = lax.psum((kernel_term, gain_term), ('seq', 'utt'))  79 us
    reduce_scatter x1, waiting for transfers between devices, per_device(): lax.psum_scatter(0.5 * lax.dot_general(columns, grad_all, (((0,), (0,)),...  45.3 us
    all_gather x1, waiting for transfers between devices, per_device(): lax.all_gather(scaled, 'utt', axis=0, tiled=True)  35.7 us
    reduce_scatter x1, waiting for transfers between devices, per_device(): lax.psum_scatter(partial_grad, 'utt', scatter_dimension=0, tiled=True)  30.8 us
  transfers between devices with their start and end apart: 12, of which 8 were waited for; matrix products, arithmetic and copies ran while one was open for 6% of the time, Pallas kernels for 0%

commit v1 on v0

v1 whole, which is shorter than its diff:
```python
import jax
import jax.numpy as jnp
from jax import lax
from jax.sharding import Mesh, PartitionSpec as P

norm_eps = 1e-05
BLOCK = 128
SEQ = ("y", "z", "core")
f32 = jnp.float32
bf16 = jnp.bfloat16


def shift(cells, axis, by):
    count = lax.axis_size(axis)
    return lax.ppermute(cells, axis, [(i, i + by) for i in range(count) if 0 <= i + by < count])


def turn(cells, axis, by):
    count = lax.axis_size(axis)
    return lax.ppermute(cells, axis, [(i, (i + by) % count) for i in range(count)])


def with_halo(cells, width):
    head = cells[:width]
    tail = cells[cells.shape[0] - width :]
    return jnp.concatenate([shift(tail, SEQ, 1), cells, shift(head, SEQ, -1)], axis=0)


def exchange(cells, axis):
    return lax.all_to_all(cells, axis, 0, 0, tiled=True)


def spread(cells, axis):
    count = lax.axis_size(axis)
    return exchange(jnp.broadcast_to(cells[None], (count,) + cells.shape), axis)


def ring_gather(cells, axis):
    count = lax.axis_size(axis)
    me = lax.axis_index(axis)
    out = jnp.zeros((count,) + cells.shape, cells.dtype)

    def put(out, piece, owner):
        return lax.dynamic_update_slice_in_dim(out, piece[None], owner % count, 0)

    out = put(out, cells, me)
    ahead = behind = cells
    for step in range(1, count // 2 + 1):
        ahead = turn(ahead, axis, 1)
        out = put(out, ahead, me - step + count)
        if 2 * step < count:
            behind = turn(behind, axis, -1)
            out = put(out, behind, me + step)
    return out


def silu_grad(values):
    sigmoid = jax.nn.sigmoid(values)
    return sigmoid * (1.0 + values * (1.0 - sigmoid))


def per_device(
    features, cotangent, conv_kernel, norm_gain, weight_in, weight_out, keep_count, keep_index
):
    frames = features[0]
    length, width = frames.shape
    tap_count = conv_kernel.shape[0]
    half_width = tap_count // 2
    shard = lax.axis_index(SEQ)
    core = lax.axis_index("core")
    ny, nz = lax.axis_size("y"), lax.axis_size("z")
    rows_in = weight_in.shape[0]
    hidden_dev = weight_in.shape[1]

    pair = jnp.stack([weight_in, weight_out])
    pieces = ring_gather(spread(pair, "y"), "z")
    others = turn(pieces, "core", 1)
    both = jnp.stack([jnp.where(core == 0, pieces, others), jnp.where(core == 0, others, pieces)])
    both = both.transpose(3, 2, 1, 0, 4, 5)
    w_in = both[0].reshape(width, hidden_dev)
    w_out = both[1].reshape(hidden_dev, width)

    counts = keep_count[0]
    blocks = (counts + BLOCK - 1) // BLOCK
    before = jnp.sum(jnp.where(jnp.arange(counts.shape[0]) < shard, blocks, 0))
    late = before - shard > 0
    local_index = keep_index[0]
    valid = jnp.arange(length, dtype=jnp.int32) < counts[shard]
    zero_bf = jnp.zeros((), bf16)

    def place(rows):
        going = jnp.where(late, rows[:BLOCK], rows[BLOCK:])
        came = shift(going, SEQ, 1)
        return jnp.where(late, came, rows[:BLOCK])

    picked_grad = place(jnp.where(valid[:, None], cotangent[0][local_index], zero_bf))
    grad_all = spread(picked_grad, "utt").reshape(-1, width)

    wide_rows = with_halo(frames, half_width)
    wide32 = wide_rows.astype(f32)
    conv_out = jnp.zeros((length, width), f32)
    for offset in range(tap_count):
        conv_out = conv_out + conv_kernel[offset] * wide32[offset : offset + length]
    hidden = (frames.astype(f32) + jax.nn.silu(conv_out)).astype(bf16)
    picked = place(jnp.where(valid[:, None], hidden[local_index], zero_bf))
    rows32 = picked.astype(f32)
    row_mean = jnp.mean(rows32, axis=1, keepdims=True)
    centred = rows32 - row_mean
    row_var = jnp.mean(centred * centred, axis=1, keepdims=True)
    inv_scale = lax.rsqrt(row_var + norm_eps)
    normed = centred * inv_scale
    scaled = (normed * norm_gain).astype(bf16)
    scaled_all = spread(scaled, "utt").reshape(-1, width)

    pre_act = jnp.dot(scaled_all, w_in, preferred_element_type=f32)
    activation = jax.nn.silu(pre_act).astype(bf16)
    act_grad = 0.5 * lax.dot_general(
        grad_all, w_out, (((1,), (1,)), ((), ())), preferred_element_type=f32
    )
    up_grad = (act_grad * silu_grad(pre_act)).astype(bf16)
    partial_grad = lax.dot_general(
        up_grad, w_in, (((1,), (1,)), ((), ())), preferred_element_type=f32
    )
    parts = exchange(partial_grad.astype(bf16).reshape(-1, BLOCK, width), "utt")
    norm_grad = jnp.sum(parts.astype(f32), axis=0)

    over_rows = (((0,), (0,)), ((), ()))
    g_in = lax.dot_general(scaled_all, up_grad, over_rows, preferred_element_type=f32)
    g_out = 0.5 * lax.dot_general(activation, grad_all, over_rows, preferred_element_type=f32)
    grads = jnp.stack(
        [
            g_in.reshape(ny, nz, 2, rows_in, hidden_dev),
            g_out.reshape(ny, nz, 2, rows_in, width),
        ],
        axis=2,
    )
    first, second = grads[:, :, :, 0], grads[:, :, :, 1]
    theirs = jnp.where(core == 0, second, first).astype(bf16)
    mine = jnp.where(core == 0, first, second)
    chip = (mine + turn(theirs, "core", 1).astype(f32)).astype(bf16)
    chip = jnp.sum(exchange(chip, "y").astype(f32), axis=0).astype(bf16)
    chip = jnp.sum(exchange(chip, "z").astype(f32), axis=0)
    grad_weight_in, grad_weight_out = chip[0], chip[1]

    gain_term = jnp.sum(norm_grad * normed, axis=0)
    gain_grad = norm_grad * norm_gain
    back_term = (
        gain_grad
        - jnp.mean(gain_grad, axis=1, keepdims=True)
        - normed * jnp.mean(gain_grad * normed, axis=1, keepdims=True)
    ) * inv_scale
    row_grad = (picked_grad.astype(f32) + back_term).astype(bf16)
    returned = shift(row_grad, SEQ, -1)
    low = jnp.where(late, returned, row_grad)
    high = returned
    local_grad = jnp.concatenate([low, high]).astype(f32)
    frame_grad = (
        jnp.zeros((length, width), f32)
        .at[local_index]
        .add(jnp.where(valid[:, None], local_grad, 0.0))
    )
    conv_grad = frame_grad * silu_grad(conv_out)
    grad_wide = with_halo(conv_grad, half_width)
    kernel_term = [
        jnp.sum(conv_grad * wide32[offset : offset + length], axis=0)
        for offset in range(tap_count)
    ]
    transposed = jnp.zeros((length, width), f32)
    for offset in range(tap_count):
        begin = 2 * half_width - offset
        transposed = transposed + conv_kernel[offset] * grad_wide[begin : begin + length]
    grad_x = (frame_grad + transposed).astype(bf16)

    small = jnp.stack(kernel_term + [gain_term])
    half = small.shape[0] // 2
    own = jnp.where(core == 0, small[:half], small[half:])
    gone = jnp.where(core == 0, small[half:], small[:half])
    total = own + turn(gone, "core", 1)
    for axis in ("utt", "y", "z"):
        total = jnp.sum(spread(total, axis), axis=0)
    back = turn(total, "core", 1)
    full = jnp.concatenate([jnp.where(core == 0, total, back), jnp.where(core == 0, back, total)])
    return (grad_x[None], grad_weight_in, grad_weight_out, full[:tap_count], full[tap_count])


def solution(mesh):
    utts = mesh.shape["utt"]
    fine = Mesh(mesh.devices.reshape(4, 8, 2, utts), ("y", "z", "core", "utt"))
    placed = (
        P("utt", SEQ, None),
        P("utt", SEQ, None),
        P(),
        P(),
        P(SEQ, "utt"),
        P(("utt",) + SEQ, None),
        P("utt", None),
        P("utt", SEQ),
    )
    return jax.shard_map(
        per_device,
        mesh=fine,
        in_specs=placed,
        out_specs=(P("utt", SEQ, None), P(SEQ, "utt"), P(("utt",) + SEQ, None), P(), P()),
        check_vma=False,
    )
```

time: 874 us -> 252 us (0.29)
  waiting for transfers between devices: 698 us -> 73.3 us
  blocking collectives: 79 us -> 19.6 us
  starting transfers between devices: 7.86 us -> 62.3 us
  local copies, waits for them, and re-layouts: 12.5 us -> 31.3 us
  other arithmetic: 29.3 us -> 43 us
  matrix products: 32.2 us -> 18.6 us
  between operations: 14.3 us -> 2.4 us
    psum x1 -> x0, waiting for transfers between devices: 250 us -> none  [per_device(): kernel_sum, gain_sum = lax.psum((kernel_term, gain_term), ('seq', 'utt'))]
    reduce_scatter x3 -> x0, waiting for transfers between devices: 223 us -> none  [the longest x1 147 us: per_device(): lax.psum_scatter(lax.dot_general(columns, up_grad, (((0,), (0,)), ((), ()...]
    all_gather x4 -> x0, waiting for transfers between devices: 223 us -> none  [the longest x1 81.4 us: per_device(): lax.all_gather(weight_in, 'seq', axis=0, tiled=True)]
    psum x1 -> x0, blocking collectives: 79 us -> none  [per_device(): kernel_sum, gain_sum = lax.psum((kernel_term, gain_term), ('seq', 'utt'))]
    all_to_all x0 -> x7, waiting for transfers between devices: none -> 50.9 us  [exchange(): return lax.all_to_all(cells, axis, 0, 0, tiled=True)]
    all_to_all x0 -> x7, starting transfers between devices: none -> 39.2 us  [exchange(): return lax.all_to_all(cells, axis, 0, 0, tiled=True)]
    ppermute x4 -> x18, waiting for transfers between devices: 0.01 us -> 22.4 us  [the longest x11 21.3 us: turn(): lax.ppermute(cells, axis, [(i, (i + by) % count) for i in range(count)])]
    all_to_all x0 -> x2, blocking collectives: none -> 19.6 us  [exchange(): return lax.all_to_all(cells, axis, 0, 0, tiled=True)]
  transfers between devices with their start and end apart: 12 -> 25, of which waited for: 8 -> 12; matrix products, arithmetic and copies ran while one was open for 6% -> 33% of each run, Pallas kernels for 0% -> 0%
where the time goes in v1:
time: 252 us; the launch traced here: 251 us
  waiting for transfers between devices  73.3 us (29%)
  starting transfers between devices  62.3 us (25%)
  other arithmetic  43 us (17%)
  local copies, waits for them, and re-layouts  31.3 us (12%)
  blocking collectives  19.6 us (8%)
  matrix products  18.6 us (7%)
    all_to_all x7, waiting for transfers between devices, exchange(): return lax.all_to_all(cells, axis, 0, 0, tiled=True)  50.9 us
    all_to_all x7, starting transfers between devices, exchange(): return lax.all_to_all(cells, axis, 0, 0, tiled=True)  39.2 us
    ppermute x11, waiting for transfers between devices, turn(): lax.ppermute(cells, axis, [(i, (i + by) % count) for i in range(count)])  21.3 us
    all_to_all x2, blocking collectives, exchange(): return lax.all_to_all(cells, axis, 0, 0, tiled=True)  19.6 us
    ppermute x7, starting transfers between devices, shift(): lax.ppermute(cells, axis, [(i, i + by) for i in range(count) if 0 <= i +...  11.8 us
    ppermute x11, starting transfers between devices, turn(): lax.ppermute(cells, axis, [(i, (i + by) % count) for i in range(count)])  11.3 us
    broadcast_in_dim x1, other arithmetic, per_device(): grad_x[None]  6.59 us
    dynamic_update_slice x8, local copies, waits for them, and re-layouts, put(): return lax.dynamic_update_slice_in_dim(out, piece[None], owner % count, 0)  5.8 us
  transfers between devices with their start and end apart: 25, of which 12 were waited for; matrix products, arithmetic and copies ran while one was open for 33% of the time, Pallas kernels for 0%

profile of v1, /device:TPU:2, one launch (start us, length us, event | category | flops | bytes accessed | tf_op | source)
XLA Modules:
  0.0 250.7 jit_solution(7767677893851163806)
XLA Ops:
  0.6 0.8 slice_bitcast_fusion.3
  1.5 1.7 collective-permute-start.9
  3.2 1.3 collective-permute-start.10
  4.5 0.8 pad_maximum_fusion.4
  6.1 10.6 %all-to-all-start.1 = ((bf16[4,2,16,1024]{3,2,1,0:T(8,128)(2,1)}), bf16[4,2,16,1024]{3,2,1,0:T(8,128)(2,1)S(1)}, u32[]{:S(2)}, u32[]{:S(2)}) async-start(bf16[4,2,16,1024]{3,2,1,0:T(8,128)(2,1)} %broadcast_in_dim.112), calls=%async_computation.1 | async-start | bytes 524288 | tf_op jit(solution)/shard_map/all_to_all | solution.py:30
  16.6 1.1 fusion.121
  17.8 1.3 fusion.120
  19.4 1.4 fusion.116
  20.7 1.2 constant_dynamic-slice_fusion
  24.2 2.0 gather_fusion
  26.6 5.2 %add_convert_fusion = (bf16[256,1024]{1,0:T(8,128)(2,1)S(1)}, f32[256,1024]{1,0:T(8,128)}) fusion(bf16[1,256,1024]{2,1,0:T(8,128)(2,1)S(1)} %copy-done.4, f32[286,1024]{1,0:T(8,128)S(1)} %maximum_convert_fusion, f32[1024]{0:T(1024)S(1)} %bitcast.206, f32[1024]{0:T(1024)S(1)} %bitcast.208, f32[1024]{0:T(1024)S(1)} %bitcast.212, f32[1024]{0:T(1024)S(1)} %bitcast.214, ...), kind=kLoop, calls=%fused_computation.202 | loop fusion | flops 17825792 | bytes 34729984 | tf_op jit(solution)/shard_map/convert_element_type | solution.py:104
  31.8 2.0 gather_fusion.1
  33.7 1.3 broadcast_select_fusion.1
  35.2 3.2 %collective-permute-start.2 = (bf16[4,2,16,1024]{3,2,0,1:T(8,128)(2,1)S(1)}, bf16[4,2,16,1024]{3,2,0,1:T(8,128)(2,1)S(1)}, u32[]{:S(2)}, u32[]{:S(2)}) collective-permute-start(bf16[4,2,16,1024]{3,2,0,1:T(8,128)(2,1)S(1)} %copy.84), channel_id=1, source_target_pairs={{0,56},{8,0},{16,8},{24,16},{32,24},{40,32},{48,40},{56,48},{1,57}... | collective-permute-start | bytes 786440 | tf_op jit(solution)/shard_map/ppermute | solution.py:20
  38.5 1.3 collective-permute-start.11
  39.8 1.6 broadcast_in_dim.64
  42.8 3.2 %collective-permute-start.4 = (bf16[4,2,16,1024]{3,2,0,1:T(8,128)(2,1)S(1)}, bf16[4,2,16,1024]{3,2,0,1:T(8,128)(2,1)S(1)}, u32[]{:S(2)}, u32[]{:S(2)}) collective-permute-start(bf16[4,2,16,1024]{3,2,0,1:T(8,128)(2,1)S(1)} %collective-permute-done.2), channel_id=1, source_target_pairs={{0,56},{8,0},{16,8},{24,16},{32,24},{40,32},{48,40},{56,48},{1,57}... | collective-permute-start | bytes 786440 | tf_op jit(solution)/shard_map/ppermute | solution.py:20
  47.4 5.7 %collective-permute-done.3 = bf16[4,2,16,1024]{3,2,0,1:T(8,128)(2,1)S(1)} collective-permute-done((bf16[4,2,16,1024]{3,2,0,1:T(8,128)(2,1)S(1)}, bf16[4,2,16,1024]{3,2,0,1:T(8,128)(2,1)S(1)}, u32[]{:S(2)}, u32[]{:S(2)}) %collective-permute-start.3) | collective-permute-done | bytes 262176 | tf_op jit(solution)/shard_map/ppermute | solution.py:20
  53.2 3.2 %collective-permute-start.6 = (bf16[4,2,16,1024]{3,2,0,1:T(8,128)(2,1)S(1)}, bf16[4,2,16,1024]{3,2,0,1:T(8,128)(2,1)S(1)}, u32[]{:S(2)}, u32[]{:S(2)}) collective-permute-start(bf16[4,2,16,1024]{3,2,0,1:T(8,128)(2,1)S(1)} %collective-permute-done.4), channel_id=1, source_target_pairs={{0,56},{8,0},{16,8},{24,16},{32,24},{40,32},{48,40},{56,48},{1,57}... | collective-permute-start | bytes 786440 | tf_op jit(solution)/shard_map/ppermute | solution.py:20
  57.9 5.6 %collective-permute-done.5 = bf16[4,2,16,1024]{3,2,0,1:T(8,128)(2,1)S(1)} collective-permute-done((bf16[4,2,16,1024]{3,2,0,1:T(8,128)(2,1)S(1)}, bf16[4,2,16,1024]{3,2,0,1:T(8,128)(2,1)S(1)}, u32[]{:S(2)}, u32[]{:S(2)}) %collective-permute-start.5) | collective-permute-done | bytes 262176 | tf_op jit(solution)/shard_map/ppermute | solution.py:20
  64.9 8.1 %collective-permute-done.7 = bf16[4,2,16,1024]{3,2,0,1:T(8,128)(2,1)S(1)} collective-permute-done((bf16[4,2,16,1024]{3,2,0,1:T(8,128)(2,1)S(1)}, bf16[4,2,16,1024]{3,2,0,1:T(8,128)(2,1)S(1)}, u32[]{:S(2)}, u32[]{:S(2)}) %collective-permute-start.7) | collective-permute-done | bytes 262176 | tf_op jit(solution)/shard_map/ppermute | solution.py:20
  75.2 1.1 broadcast_in_dim.121
  76.4 4.8 %all-to-all-start.2 = ((bf16[4,128,1024]{1,2,0:T(8,128)(2,1)}), bf16[4,128,1024]{1,2,0:T(8,128)(2,1)S(1)}, u32[]{:S(2)}, u32[]{:S(2)}) async-start(bf16[4,128,1024]{1,2,0:T(8,128)(2,1)} %broadcast_in_dim.121), calls=%async_computation.2 | async-start | bytes 2097152 | tf_op jit(solution)/shard_map/all_to_all | solution.py:30
  81.2 1.9 collective-permute-start
  83.1 1.1 collective-permute-done
  84.3 11.2 %all-to-all-done.2 = bf16[4,128,1024]{1,2,0:T(8,128)(2,1)S(1)} async-done(((bf16[4,128,1024]{1,2,0:T(8,128)(2,1)}), bf16[4,128,1024]{1,2,0:T(8,128)(2,1)S(1)}, u32[]{:S(2)}, u32[]{:S(2)}) %all-to-all-start.2) | async-done | bytes 1048608 | tf_op jit(solution)/shard_map/all_to_all | solution.py:30
  95.5 1.1 broadcast_in_dim.63
  96.6 5.7 %all-to-all-start = ((bf16[4,128,1024]{2,1,0:T(8,128)(2,1)}), bf16[4,128,1024]{2,1,0:T(8,128)(2,1)}, u32[]{:S(2)}, u32[]{:S(2)}) async-start(bf16[4,128,1024]{2,1,0:T(8,128)(2,1)} %broadcast_in_dim.63), calls=%async_computation | async-start | bytes 2097152 | tf_op jit(solution)/shard_map/all_to_all | solution.py:30
  102.3 1.3 copy.94
  103.6 2.3 copy.95
  105.9 2.5 select_bitcast_fusion.1
  108.8 1.8 fusion.118
  110.6 1.3 copy-done.5
  111.9 2.6 %fusion.122 = f32[512,1024]{1,0:T(8,128)} fusion(bf16[512,1024]{1,0:T(8,128)(2,1)S(1)} %bitcast.179, bf16[1024,1024]{1,0:T(8,128)(2,1)S(1)} %bitcast.182), kind=kOutput, calls=%fused_computation.274 | convolution fusion | flops 1073741824 | bytes 5242880 | tf_op jit(solution)/shard_map/dot_general | solution.py:115
  114.5 1.3 all-to-all-done
  115.8 4.3 %multiply_convert_fusion.1 = bf16[512,1024]{1,0:T(8,128)(2,1)S(1)} fusion(f32[512,1024]{1,0:T(8,128)} %fusion.122, bf16[512,1024]{1,0:T(8,128)(2,1)} %bitcast.5, bf16[1024,1024]{1,0:T(8,128)(2,1)} %bitcast.184), kind=kOutput, calls=%fused_computation.46 | convolution fusion | flops 1078984704 | bytes 6291456 | tf_op jit(solution)/shard_map/dot_general | solution.py:117
  120.2 2.3 convolution_convert_fusion
  122.5 4.9 %all-to-all-start.3 = ((bf16[4,128,1024]{2,1,0:T(8,128)(2,1)}), bf16[4,128,1024]{2,1,0:T(8,128)(2,1)S(1)}, u32[]{:S(2)}, u32[]{:S(2)}) async-start(bf16[4,128,1024]{2,1,0:T(8,128)(2,1)} %bitcast.185), calls=%async_computation.3 | async-start | bytes 2097152 | tf_op jit(solution)/shard_map/all_to_all | solution.py:30
  127.4 4.9 %convolution_bitcast_fusion = f32[4,8,1,2,16,1024]{5,4,3,1,0,2:T(8,128)} fusion(bf16[4,8,2,16,512]{4,3,2,1,0:T(8,128)(2,1)} %bitcast.180, bf16[512,1024]{1,0:T(8,128)(2,1)} %copy-done.7), kind=kOutput, calls=%fused_computation.42 | convolution fusion | flops 1073741824 | bytes 6291456 | tf_op jit(solution)/shard_map/dot_general | solution.py:128
  132.3 4.6 %convolution_multiply_fusion = f32[1024,1024]{1,0:T(8,128)} fusion(bf16[512,1024]{1,0:T(8,128)(2,1)} %bitcast.5, f32[512,1024]{1,0:T(8,128)S(1)} %copy-done.45), kind=kOutput, calls=%fused_computation.41 | convolution fusion | flops 1077411840 | bytes 7340032 | tf_op jit(solution)/shard_map/dot_general | solution.py:129
  136.8 3.2 %all-to-all-done.3 = bf16[4,128,1024]{2,1,0:T(8,128)(2,1)S(1)} async-done(((bf16[4,128,1024]{2,1,0:T(8,128)(2,1)}), bf16[4,128,1024]{2,1,0:T(8,128)(2,1)S(1)}, u32[]{:S(2)}, u32[]{:S(2)}) %all-to-all-start.3) | async-done | bytes 1048608 | tf_op jit(solution)/shard_map/all_to_all | solution.py:30
  140.8 1.3 collective-permute-start.12
  142.1 4.7 %fusion.4 = bf16[4,8,2,16,1024]{4,3,1,0,2:T(8,128)(2,1)} fusion(pred[]{:T(512)S(6)} %eq.19, f32[4,8,1,2,16,1024]{5,4,3,1,0,2:T(8,128)} %bitcast.176, f32[4,8,1,2,16,1024]{5,4,3,1,0,2:T(8,128)} %convolution_bitcast_fusion), kind=kLoop, calls=%fused_computation.43 | loop fusion | flops 3145728 | bytes 10485761 | tf_op jit(solution)/shard_map/convert_element_type | solution.py:138
  146.8 1.1 collective-permute-start.15
  148.0 3.9 %scatter_custom_fusion = f32[256,1024]{1,0:T(8,128)} fusion(s32[256]{0:T(256)} %bitcast.283, bf16[128,1024]{1,0:T(8,128)(2,1)S(1)} %collective-permute-done.12, bf16[]{:T(256)} %constant.135, bf16[128,1024]{1,0:T(8,128)(2,1)S(1)} %broadcast_select_fusion.2, f32[]{:T(128)} %constant.100.clone.1, pred[256]{0:T(512)(128)(4,1)S(1)} %copy-done.44), kind=kCustom, calls=%fused_computation.223 | custom fusion | flops 1572864 | bytes 1574656 | tf_op jit(solution)/shard_map/scatter-add | solution.py:160
  151.9 3.3 %multiply_reduce_fusion.20 = (f32[1024]{0:T(1024)S(1)}, f32[1024]{0:T(1024)S(1)}, f32[1024]{0:T(1024)S(1)}, f32[1024]{0:T(1024)S(1)}, f32[1024]{0:T(1024)S(1)}, ...) fusion(f32[286,1024]{1,0:T(8,128)S(1)} %maximum_convert_fusion,, ...), kind=kLoop, calls=%fused_computation.188 | loop fusion | flops 8899584 | bytes 16830464 | tf_op jit(solution)/shard_map/reduce_sum | solution.py:165
  155.1 2.5 multiply_reduce_fusion.15
  158.0 1.2 collective-permute-done.16
  159.3 9.7 %all_to_all.45 = f32[4,16,1024]{2,1,0:T(8,128)S(1)} all-to-all(f32[4,16,1024]{2,1,0:T(8,128)S(1)} %broadcast_in_dim.123), channel_id=1, replica_groups=mesh['y'=4,'z'=8,'core'=2,'utt'=4] {'utt'}, dimensions={0} | all-to-all | bytes 524288 | tf_op jit(solution)/shard_map/all_to_all | solution.py:30
  169.0 10.0 %all_to_all.46 = f32[4,16,1024]{2,1,0:T(8,128)S(1)} all-to-all(f32[4,16,1024]{2,1,0:T(8,128)S(1)} %broadcast_in_dim.124), channel_id=1, replica_groups=mesh['y'=4,'z'=8,'core'=2,'utt'=4] {'y'}, dimensions={0} | all-to-all | bytes 524288 | tf_op jit(solution)/shard_map/all_to_all | solution.py:30
  179.0 0.8 broadcast_in_dim.125
  179.8 5.3 %all-to-all-start.8 = ((f32[8,16,1024]{2,1,0:T(8,128)}), f32[8,16,1024]{2,1,0:T(8,128)S(1)}, u32[]{:S(2)}, u32[]{:S(2)}) async-start(f32[8,16,1024]{2,1,0:T(8,128)} %broadcast_in_dim.125), calls=%async_computation.8 | async-start | bytes 1048576 | tf_op jit(solution)/shard_map/all_to_all | solution.py:30
  185.1 4.7 %fusion.3 = bf16[4,8,2,16,1024]{4,3,1,0,2:T(8,128)(2,1)S(1)} fusion(bf16[4,8,2,16,1024]{4,3,1,0,2:T(8,128)(2,1)} %collective-permute-done.15, pred[]{:T(512)S(6)} %eq.19, f32[4,8,1,2,16,1024]{5,4,3,1,0,2:T(8,128)} %bitcast.177, f32[4,8,1,2,16,1024]{5,4,3,1,0,2:T(8,128)} %convolution_bitcast_fusion), kind=kLoop, calls=%fused_computation.39 | loop fusion | flops 6291456 | bytes 12582913 | tf_op jit(solution)/shard_map/convert_element_type | solution.py:140
  189.8 1.5 copy.100
  191.3 9.4 %all-to-all-done.8 = f32[8,16,1024]{2,1,0:T(8,128)S(1)} async-done(((f32[8,16,1024]{2,1,0:T(8,128)}), f32[8,16,1024]{2,1,0:T(8,128)S(1)}, u32[]{:S(2)}, u32[]{:S(2)}) %all-to-all-start.8) | async-done | bytes 524320 | tf_op jit(solution)/shard_map/all_to_all | solution.py:30
  200.6 4.4 %all-to-all-start.4 = ((bf16[4,8,2,16,1024]{4,3,1,2,0:T(8,128)(2,1)}), bf16[4,8,2,16,1024]{4,3,1,2,0:T(8,128)(2,1)}, u32[]{:S(2)}, u32[]{:S(2)}) async-start(bf16[4,8,2,16,1024]{4,3,1,2,0:T(8,128)(2,1)} %copy.100), calls=%async_computation.4 | async-start | bytes 4194304 | tf_op jit(solution)/shard_map/all_to_all | solution.py:30
  205.1 1.3 collective-permute-start.13
  206.4 3.0 %collective-permute-start.14 = (f32[15,1024]{1,0:T(8,128)S(1)}, f32[15,1024]{1,0:T(8,128)S(1)}, u32[]{:S(2)}, u32[]{:S(2)}) collective-permute-start(f32[15,1024]{1,0:T(8,128)S(1)} %get-tuple-element.49), channel_id=1, source_target_pairs={{0,4},{4,8},{8,12},{12,16},{16,20},{20,24},{24,28},{28,32},{32,36}... | collective-permute-start | bytes 184328 | tf_op jit(solution)/shard_map/ppermute | solution.py:15
  209.8 19.5 %all-to-all-done.4 = bf16[4,8,2,16,1024]{4,3,1,2,0:T(8,128)(2,1)} async-done(((bf16[4,8,2,16,1024]{4,3,1,2,0:T(8,128)(2,1)}), bf16[4,8,2,16,1024]{4,3,1,2,0:T(8,128)(2,1)}, u32[]{:S(2)}, u32[]{:S(2)}) %all-to-all-start.4) | async-done | bytes 2097184 | tf_op jit(solution)/shard_map/all_to_all | solution.py:30
  229.3 2.0 reduce_sum.396
  231.3 0.8 copy.102
  232.1 3.5 %all-to-all-start.5 = ((bf16[8,2,16,1024]{3,2,1,0:T(8,128)(2,1)}), bf16[8,2,16,1024]{3,2,1,0:T(8,128)(2,1)S(1)}, u32[]{:S(2)}, u32[]{:S(2)}) async-start(bf16[8,2,16,1024]{3,2,1,0:T(8,128)(2,1)} %copy.102), calls=%async_computation.5 | async-start | bytes 1048576 | tf_op jit(solution)/shard_map/all_to_all | solution.py:30
  235.7 6.6 %fusion.115 = bf16[1,256,1024]{2,1,0:T(8,128)(2,1)} fusion(f32[256,1024]{1,0:T(8,128)S(1)} %copy-done.2, f32[256,1024]{1,0:T(8,128)S(1)} %get-tuple-element.39, f32[15,1024]{1,0:T(8,128)S(1)} %collective-permute-done.14, f32[1024]{0:T(1024)} %bitcast.207, f32[1024]{0:T(1024)} %bitcast.209, f32[1024]{0:T(1024)} %bitcast.213, f32[1024]{0:T(1024)} %bitcast.215, ...), kind=kLoop, calls=%fused_computation.229 | loop fusion | flops 24379392 | bytes 2871296 | tf_op jit(solution)/shard_map/broadcast_in_dim | solution.py:183
  243.6 6.3 %all-to-all-done.5 = bf16[8,2,16,1024]{3,2,1,0:T(8,128)(2,1)S(1)} async-done(((bf16[8,2,16,1024]{3,2,1,0:T(8,128)(2,1)}), bf16[8,2,16,1024]{3,2,1,0:T(8,128)(2,1)S(1)}, u32[]{:S(2)}, u32[]{:S(2)}) %all-to-all-start.5) | async-done | bytes 524320 | tf_op jit(solution)/shard_map/all_to_all | solution.py:30
  (156 shorter events, 14.7 us)
Async XLA Ops:
  0.6 23.5 %copy-start = (bf16[1,256,1024]{2,1,0:T(8,128)(2,1)S(1)}, bf16[1,256,1024]{2,1,0:T(8,128)(2,1)}, u32[]{:S(2)}) copy-start(bf16[1,256,1024]{2,1,0:T(8,128)(2,1)} %param.9) | copy-start | bytes 1572868
  1.5 24.6 %collective-permute-start.9 = (bf16[15,1024]{1,0:T(8,128)(2,1)S(1)}, bf16[15,1024]{1,0:T(8,128)(2,1)S(1)}, u32[]{:S(2)}, u32[]{:S(2)}) collective-permute-start(bf16[15,1024]{1,0:T(8,128)(2,1)S(1)} %get-tuple-element.50), channel_id=1, source_target_pairs={{0,4},{4,8},{8,12},{12,16},{16,20},{20,24},{24,28},{28,32},{32,36}... | collective-permute-start | bytes 92168 | tf_op jit(solution)/shard_map/ppermute | solution.py:15
  3.2 22.9 %collective-permute-start.10 = (bf16[15,1024]{1,0:T(8,128)(2,1)S(1)}, bf16[15,1024]{1,0:T(8,128)(2,1)S(1)}, u32[]{:S(2)}, u32[]{:S(2)}) collective-permute-start(bf16[15,1024]{1,0:T(8,128)(2,1)S(1)} %get-tuple-element.51), channel_id=1, source_target_pairs={{4,0},{8,4},{12,8},{16,12},{20,16},{24,20},{28,24},{32,28},{36,32}... | collective-permute-start | bytes 92168 | tf_op jit(solution)/shard_map/ppermute | solution.py:15
  6.1 29.0 %all-to-all-start.1 = ((bf16[4,2,16,1024]{3,2,1,0:T(8,128)(2,1)}), bf16[4,2,16,1024]{3,2,1,0:T(8,128)(2,1)S(1)}, u32[]{:S(2)}, u32[]{:S(2)}) async-start(bf16[4,2,16,1024]{3,2,1,0:T(8,128)(2,1)} %broadcast_in_dim.112), calls=%async_computation.1 | async-start | bytes 524288 | tf_op jit(solution)/shard_map/all_to_all | solution.py:30
  17.7 8.6 %copy-start.9 = (f32[1,1024]{1,0:T(1,128)}, f32[1,1024]{1,0:T(1,128)S(1)}, u32[]{:S(2)}) copy-start(f32[1,1024]{1,0:T(1,128)S(1)} %get-tuple-element.78) | copy-start | bytes 12292
  17.8 8.6 %copy-start.11 = (f32[1,1024]{1,0:T(1,128)}, f32[1,1024]{1,0:T(1,128)S(1)}, u32[]{:S(2)}) copy-start(f32[1,1024]{1,0:T(1,128)S(1)} %get-tuple-element.79) | copy-start | bytes 12292
  17.8 8.6 %copy-start.12 = (f32[1,1024]{1,0:T(1,128)}, f32[1,1024]{1,0:T(1,128)S(1)}, u32[]{:S(2)}) copy-start(f32[1,1024]{1,0:T(1,128)S(1)} %get-tuple-element.80) | copy-start | bytes 12292
  17.8 8.6 %copy-start.13 = (f32[1,1024]{1,0:T(1,128)}, f32[1,1024]{1,0:T(1,128)S(1)}, u32[]{:S(2)}) copy-start(f32[1,1024]{1,0:T(1,128)S(1)} %get-tuple-element.81) | copy-start | bytes 12292
  17.8 8.6 %copy-start.14 = (f32[1,1024]{1,0:T(1,128)}, f32[1,1024]{1,0:T(1,128)S(1)}, u32[]{:S(2)}) copy-start(f32[1,1024]{1,0:T(1,128)S(1)} %get-tuple-element.82) | copy-start | bytes 12292
  17.8 8.6 %copy-start.15 = (f32[1,1024]{1,0:T(1,128)}, f32[1,1024]{1,0:T(1,128)S(1)}, u32[]{:S(2)}) copy-start(f32[1,1024]{1,0:T(1,128)S(1)} %get-tuple-element.83) | copy-start | bytes 12292
  17.8 8.6 %copy-start.16 = (f32[1,1024]{1,0:T(1,128)}, f32[1,1024]{1,0:T(1,128)S(1)}, u32[]{:S(2)}) copy-start(f32[1,1024]{1,0:T(1,128)S(1)} %get-tuple-element.84) | copy-start | bytes 12292
  17.8 8.6 %copy-start.17 = (f32[1,1024]{1,0:T(1,128)}, f32[1,1024]{1,0:T(1,128)S(1)}, u32[]{:S(2)}) copy-start(f32[1,1024]{1,0:T(1,128)S(1)} %get-tuple-element.85) | copy-start | bytes 12292
  17.8 8.6 %copy-start.18 = (f32[1,1024]{1,0:T(1,128)}, f32[1,1024]{1,0:T(1,128)S(1)}, u32[]{:S(2)}) copy-start(f32[1,1024]{1,0:T(1,128)S(1)} %get-tuple-element.86) | copy-start | bytes 12292
  19.2 7.2 %copy-start.19 = (f32[1,1024]{1,0:T(1,128)}, f32[1,1024]{1,0:T(1,128)S(1)}, u32[]{:S(2)}) copy-start(f32[1,1024]{1,0:T(1,128)S(1)} %get-tuple-element.56) | copy-start | bytes 12292
  19.2 7.2 %copy-start.20 = (f32[1,1024]{1,0:T(1,128)}, f32[1,1024]{1,0:T(1,128)S(1)}, u32[]{:S(2)}) copy-start(f32[1,1024]{1,0:T(1,128)S(1)} %get-tuple-element.57) | copy-start | bytes 12292
  19.2 7.2 %copy-start.21 = (f32[1,1024]{1,0:T(1,128)}, f32[1,1024]{1,0:T(1,128)S(1)}, u32[]{:S(2)}) copy-start(f32[1,1024]{1,0:T(1,128)S(1)} %get-tuple-element.58) | copy-start | bytes 12292
  19.2 7.2 %copy-start.22 = (f32[1,1024]{1,0:T(1,128)}, f32[1,1024]{1,0:T(1,128)S(1)}, u32[]{:S(2)}) copy-start(f32[1,1024]{1,0:T(1,128)S(1)} %get-tuple-element.59) | copy-start | bytes 12292
  19.2 7.2 %copy-start.23 = (f32[1,1024]{1,0:T(1,128)}, f32[1,1024]{1,0:T(1,128)S(1)}, u32[]{:S(2)}) copy-start(f32[1,1024]{1,0:T(1,128)S(1)} %get-tuple-element.60) | copy-start | bytes 12292
  19.2 7.2 %copy-start.24 = (f32[1,1024]{1,0:T(1,128)}, f32[1,1024]{1,0:T(1,128)S(1)}, u32[]{:S(2)}) copy-start(f32[1,1024]{1,0:T(1,128)S(1)} %get-tuple-element.61) | copy-start | bytes 12292
  19.2 7.2 %copy-start.25 = (f32[1,1024]{1,0:T(1,128)}, f32[1,1024]{1,0:T(1,128)S(1)}, u32[]{:S(2)}) copy-start(f32[1,1024]{1,0:T(1,128)S(1)} %get-tuple-element.62) | copy-start | bytes 12292
  19.2 7.2 %copy-start.26 = (f32[1,1024]{1,0:T(1,128)}, f32[1,1024]{1,0:T(1,128)S(1)}, u32[]{:S(2)}) copy-start(f32[1,1024]{1,0:T(1,128)S(1)} %get-tuple-element.63) | copy-start | bytes 12292
  19.2 7.2 %copy-start.27 = (f32[1,1024]{1,0:T(1,128)}, f32[1,1024]{1,0:T(1,128)S(1)}, u32[]{:S(2)}) copy-start(f32[1,1024]{1,0:T(1,128)S(1)} %get-tuple-element.64) | copy-start | bytes 12292
  19.3 7.2 %copy-start.28 = (f32[1,1024]{1,0:T(1,128)}, f32[1,1024]{1,0:T(1,128)S(1)}, u32[]{:S(2)}) copy-start(f32[1,1024]{1,0:T(1,128)S(1)} %get-tuple-element.65) | copy-start | bytes 12292
  19.3 7.2 %copy-start.29 = (f32[1,1024]{1,0:T(1,128)}, f32[1,1024]{1,0:T(1,128)S(1)}, u32[]{:S(2)}) copy-start(f32[1,1024]{1,0:T(1,128)S(1)} %get-tuple-element.66) | copy-start | bytes 12292
  19.3 7.2 %copy-start.30 = (f32[1,1024]{1,0:T(1,128)}, f32[1,1024]{1,0:T(1,128)S(1)}, u32[]{:S(2)}) copy-start(f32[1,1024]{1,0:T(1,128)S(1)} %get-tuple-element.67) | copy-start | bytes 12292
  19.3 7.2 %copy-start.31 = (f32[1,1024]{1,0:T(1,128)}, f32[1,1024]{1,0:T(1,128)S(1)}, u32[]{:S(2)}) copy-start(f32[1,1024]{1,0:T(1,128)S(1)} %get-tuple-element.68) | copy-start | bytes 12292
  19.3 7.2 %copy-start.32 = (f32[1,1024]{1,0:T(1,128)}, f32[1,1024]{1,0:T(1,128)S(1)}, u32[]{:S(2)}) copy-start(f32[1,1024]{1,0:T(1,128)S(1)} %get-tuple-element.69) | copy-start | bytes 12292
  19.3 7.2 %copy-start.33 = (f32[1,1024]{1,0:T(1,128)}, f32[1,1024]{1,0:T(1,128)S(1)}, u32[]{:S(2)}) copy-start(f32[1,1024]{1,0:T(1,128)S(1)} %get-tuple-element.70) | copy-start | bytes 12292
  19.3 7.2 %copy-start.34 = (f32[1,1024]{1,0:T(1,128)}, f32[1,1024]{1,0:T(1,128)S(1)}, u32[]{:S(2)}) copy-start(f32[1,1024]{1,0:T(1,128)S(1)} %get-tuple-element.71) | copy-start | bytes 12292
  19.3 7.2 %copy-start.35 = (f32[1,1024]{1,0:T(1,128)}, f32[1,1024]{1,0:T(1,128)S(1)}, u32[]{:S(2)}) copy-start(f32[1,1024]{1,0:T(1,128)S(1)} %get-tuple-element.72) | copy-start | bytes 12292
  19.3 7.2 %copy-start.36 = (f32[1,1024]{1,0:T(1,128)}, f32[1,1024]{1,0:T(1,128)S(1)}, u32[]{:S(2)}) copy-start(f32[1,1024]{1,0:T(1,128)S(1)} %get-tuple-element.73) | copy-start | bytes 12292
  19.3 7.2 %copy-start.37 = (f32[1,1024]{1,0:T(1,128)}, f32[1,1024]{1,0:T(1,128)S(1)}, u32[]{:S(2)}) copy-start(f32[1,1024]{1,0:T(1,128)S(1)} %get-tuple-element.74) | copy-start | bytes 12292
  23.3 10.4 %copy-start.43 = (pred[256]{0:T(512)(128)(4,1)}, pred[256]{0:T(512)(128)(4,1)S(1)}, u32[]{:S(2)}) copy-start(pred[256]{0:T(512)(128)(4,1)S(1)} %iota_compare_fusion) | copy-start | bytes 772
  35.1 7.7 %collective-permute-start.1 = (bf16[4,2,16,1024]{3,2,0,1:T(8,128)(2,1)S(1)}, bf16[4,2,16,1024]{3,2,0,1:T(8,128)(2,1)S(1)}, u32[]{:S(2)}, u32[]{:S(2)}) collective-permute-start(bf16[4,2,16,1024]{3,2,0,1:T(8,128)(2,1)S(1)} %copy.84), channel_id=1, source_target_pairs={{0,8},{8,16},{16,24},{24,32},{32,40},{40,48},{48,56},{56,0},{1,9},... | collective-permute-start | bytes 786440 | tf_op jit(solution)/shard_map/ppermute | solution.py:20
  35.2 7.6 %collective-permute-start.2 = (bf16[4,2,16,1024]{3,2,0,1:T(8,128)(2,1)S(1)}, bf16[4,2,16,1024]{3,2,0,1:T(8,128)(2,1)S(1)}, u32[]{:S(2)}, u32[]{:S(2)}) collective-permute-start(bf16[4,2,16,1024]{3,2,0,1:T(8,128)(2,1)S(1)} %copy.84), channel_id=1, source_target_pairs={{0,56},{8,0},{16,8},{24,16},{32,24},{40,32},{48,40},{56,48},{1,57}... | collective-permute-start | bytes 786440 | tf_op jit(solution)/shard_map/ppermute | solution.py:20
  38.5 35.2 %collective-permute-start.11 = (bf16[128,1024]{1,0:T(8,128)(2,1)S(1)}, bf16[128,1024]{1,0:T(8,128)(2,1)S(1)}, u32[]{:S(2)}, u32[]{:S(2)}) collective-permute-start(bf16[128,1024]{1,0:T(8,128)(2,1)S(1)} %slice_select_fusion), channel_id=1, source_target_pairs={{0,4},{4,8},{8,12},{12,16},{16,20},{20,24},{24,28},{28,32},{32,36}... | collective-permute-start | bytes 786440 | tf_op jit(solution)/shard_map/ppermute | solution.py:15
  42.8 10.4 %collective-permute-start.3 = (bf16[4,2,16,1024]{3,2,0,1:T(8,128)(2,1)S(1)}, bf16[4,2,16,1024]{3,2,0,1:T(8,128)(2,1)S(1)}, u32[]{:S(2)}, u32[]{:S(2)}) collective-permute-start(bf16[4,2,16,1024]{3,2,0,1:T(8,128)(2,1)S(1)} %collective-permute-done.1), channel_id=1, source_target_pairs={{0,8},{8,16},{16,24},{24,32},{32,40},{40,48},{48,56},{56,0},{1,9},... | collective-permute-start | bytes 786440 | tf_op jit(solution)/shard_map/ppermute | solution.py:20
  42.8 10.4 %collective-permute-start.4 = (bf16[4,2,16,1024]{3,2,0,1:T(8,128)(2,1)S(1)}, bf16[4,2,16,1024]{3,2,0,1:T(8,128)(2,1)S(1)}, u32[]{:S(2)}, u32[]{:S(2)}) collective-permute-start(bf16[4,2,16,1024]{3,2,0,1:T(8,128)(2,1)S(1)} %collective-permute-done.2), channel_id=1, source_target_pairs={{0,56},{8,0},{16,8},{24,16},{32,24},{40,32},{48,40},{56,48},{1,57}... | collective-permute-start | bytes 786440 | tf_op jit(solution)/shard_map/ppermute | solution.py:20
  46.7 28.1 %copy-start.8 = (f32[1024]{0:T(1024)S(1)}, f32[1024]{0:T(1024)}, u32[]{:S(2)}) copy-start(f32[1024]{0:T(1024)} %param.11) | copy-start | bytes 12292
  53.2 10.3 %collective-permute-start.5 = (bf16[4,2,16,1024]{3,2,0,1:T(8,128)(2,1)S(1)}, bf16[4,2,16,1024]{3,2,0,1:T(8,128)(2,1)S(1)}, u32[]{:S(2)}, u32[]{:S(2)}) collective-permute-start(bf16[4,2,16,1024]{3,2,0,1:T(8,128)(2,1)S(1)} %collective-permute-done.3), channel_id=1, source_target_pairs={{0,8},{8,16},{16,24},{24,32},{32,40},{40,48},{48,56},{56,0},{1,9},... | collective-permute-start | bytes 786440 | tf_op jit(solution)/shard_map/ppermute | solution.py:20
  53.2 11.0 %collective-permute-start.6 = (bf16[4,2,16,1024]{3,2,0,1:T(8,128)(2,1)S(1)}, bf16[4,2,16,1024]{3,2,0,1:T(8,128)(2,1)S(1)}, u32[]{:S(2)}, u32[]{:S(2)}) collective-permute-start(bf16[4,2,16,1024]{3,2,0,1:T(8,128)(2,1)S(1)} %collective-permute-done.4), channel_id=1, source_target_pairs={{0,56},{8,0},{16,8},{24,16},{32,24},{40,32},{48,40},{56,48},{1,57}... | collective-permute-start | bytes 786440 | tf_op jit(solution)/shard_map/ppermute | solution.py:20
  63.4 9.5 %collective-permute-start.7 = (bf16[4,2,16,1024]{3,2,0,1:T(8,128)(2,1)S(1)}, bf16[4,2,16,1024]{3,2,0,1:T(8,128)(2,1)S(1)}, u32[]{:S(2)}, u32[]{:S(2)}) collective-permute-start(bf16[4,2,16,1024]{3,2,0,1:T(8,128)(2,1)S(1)} %collective-permute-done.5), channel_id=1, source_target_pairs={{0,8},{8,16},{16,24},{24,32},{32,40},{40,48},{48,56},{56,0},{1,9},... | collective-permute-start | bytes 786440 | tf_op jit(solution)/shard_map/ppermute | solution.py:20
  73.7 32.2 %collective-permute-start.8 = (bf16[8,4,2,16,1024]{4,3,0,1,2:T(8,128)(2,1)}, bf16[8,4,2,16,1024]{4,3,0,1,2:T(8,128)(2,1)}, u32[]{:S(2)}, u32[]{:S(2)}) collective-permute-start(bf16[8,4,2,16,1024]{4,3,0,1,2:T(8,128)(2,1)} %bitcast_dynamic-update-slice_fusion.5), channel_id=1, source_target_pairs={{0,4},{4,0},{1,5},{5,1},{2,6},{6,2},{3,7},{7,3},{8,12},{12,8},{9,1... | collective-permute-start | bytes 6291464 | tf_op jit(solution)/shard_map/ppermute | solution.py:20
  76.4 19.1 %all-to-all-start.2 = ((bf16[4,128,1024]{1,2,0:T(8,128)(2,1)}), bf16[4,128,1024]{1,2,0:T(8,128)(2,1)S(1)}, u32[]{:S(2)}, u32[]{:S(2)}) async-start(bf16[4,128,1024]{1,2,0:T(8,128)(2,1)} %broadcast_in_dim.121), calls=%async_computation.2 | async-start | bytes 2097152 | tf_op jit(solution)/shard_map/all_to_all | solution.py:30
  81.2 3.0 %collective-permute-start = (bf16[128,1024]{1,0:T(8,128)(2,1)S(1)}, bf16[128,1024]{1,0:T(8,128)(2,1)S(1)}, u32[]{:S(2)}, u32[]{:S(2)}) collective-permute-start(bf16[128,1024]{1,0:T(8,128)(2,1)S(1)} %slice_select_fusion.1), channel_id=1, source_target_pairs={{0,4},{4,8},{8,12},{12,16},{16,20},{20,24},{24,28},{28,32},{32,36}... | collective-permute-start | bytes 786440 | tf_op jit(solution)/shard_map/ppermute | solution.py:15
  96.6 19.2 %all-to-all-start = ((bf16[4,128,1024]{2,1,0:T(8,128)(2,1)}), bf16[4,128,1024]{2,1,0:T(8,128)(2,1)}, u32[]{:S(2)}, u32[]{:S(2)}) async-start(bf16[4,128,1024]{2,1,0:T(8,128)(2,1)} %broadcast_in_dim.63), calls=%async_computation | async-start | bytes 2097152 | tf_op jit(solution)/shard_map/all_to_all | solution.py:30
  115.8 4.3 %copy-start.6 = (bf16[1,4,8,2,16,1024]{5,4,3,2,1,0:T(8,128)(2,1)S(1)}, bf16[1,4,8,2,16,1024]{5,4,3,2,1,0:T(8,128)(2,1)}, u32[]{:S(2)}) copy-start(bf16[1,4,8,2,16,1024]{5,4,3,2,1,0:T(8,128)(2,1)} %copy-done.5) | copy-start | bytes 6291460
  122.5 17.5 %all-to-all-start.3 = ((bf16[4,128,1024]{2,1,0:T(8,128)(2,1)}), bf16[4,128,1024]{2,1,0:T(8,128)(2,1)S(1)}, u32[]{:S(2)}, u32[]{:S(2)}) async-start(bf16[4,128,1024]{2,1,0:T(8,128)(2,1)} %bitcast.185), calls=%async_computation.3 | async-start | bytes 2097152 | tf_op jit(solution)/shard_map/all_to_all | solution.py:30
  127.4 4.9 %copy-start.45 = (f32[512,1024]{1,0:T(8,128)S(1)}, f32[512,1024]{1,0:T(8,128)}, u32[]{:S(2)}) copy-start(f32[512,1024]{1,0:T(8,128)} %fusion.122) | copy-start | bytes 6291460
  132.3 7.9 %copy-start.39 = (f32[128]{0:T(128)S(1)}, f32[128]{0:T(128)}, u32[]{:S(2)}) copy-start(f32[128]{0:T(128)} %copy-done.38) | copy-start | bytes 1540
  132.3 7.9 %copy-start.41 = (f32[128]{0:T(128)S(1)}, f32[128]{0:T(128)}, u32[]{:S(2)}) copy-start(f32[128]{0:T(128)} %copy-done.40) | copy-start | bytes 1540
  140.8 7.1 %collective-permute-start.12 = (bf16[128,1024]{1,0:T(8,128)(2,1)S(1)}, bf16[128,1024]{1,0:T(8,128)(2,1)S(1)}, u32[]{:S(2)}, u32[]{:S(2)}) collective-permute-start(bf16[128,1024]{1,0:T(8,128)(2,1)S(1)} %fusion.108), channel_id=1, source_target_pairs={{4,0},{8,4},{12,8},{16,12},{20,16},{24,20},{28,24},{32,28},{36,32}... | collective-permute-start | bytes 786440 | tf_op jit(solution)/shard_map/ppermute | solution.py:15
  142.1 5.9 %copy-start.44 = (pred[256]{0:T(512)(128)(4,1)S(1)}, pred[256]{0:T(512)(128)(4,1)}, u32[]{:S(2)}) copy-start(pred[256]{0:T(512)(128)(4,1)} %copy-done.43) | copy-start | bytes 772
  146.8 38.3 %collective-permute-start.15 = (bf16[4,8,2,16,1024]{4,3,1,0,2:T(8,128)(2,1)}, bf16[4,8,2,16,1024]{4,3,1,0,2:T(8,128)(2,1)}, u32[]{:S(2)}, u32[]{:S(2)}) collective-permute-start(bf16[4,8,2,16,1024]{4,3,1,0,2:T(8,128)(2,1)} %fusion.4), channel_id=1, source_target_pairs={{0,4},{4,0},{1,5},{5,1},{2,6},{6,2},{3,7},{7,3},{8,12},{12,8},{9,1... | collective-permute-start | bytes 6291464 | tf_op jit(solution)/shard_map/ppermute | solution.py:20
  157.9 1.3 collective-permute-start.16
  179.8 20.8 %all-to-all-start.8 = ((f32[8,16,1024]{2,1,0:T(8,128)}), f32[8,16,1024]{2,1,0:T(8,128)S(1)}, u32[]{:S(2)}, u32[]{:S(2)}) async-start(f32[8,16,1024]{2,1,0:T(8,128)} %broadcast_in_dim.125), calls=%async_computation.8 | async-start | bytes 1048576 | tf_op jit(solution)/shard_map/all_to_all | solution.py:30
  200.6 28.6 %all-to-all-start.4 = ((bf16[4,8,2,16,1024]{4,3,1,2,0:T(8,128)(2,1)}), bf16[4,8,2,16,1024]{4,3,1,2,0:T(8,128)(2,1)}, u32[]{:S(2)}, u32[]{:S(2)}) async-start(bf16[4,8,2,16,1024]{4,3,1,2,0:T(8,128)(2,1)} %copy.100), calls=%async_computation.4 | async-start | bytes 4194304 | tf_op jit(solution)/shard_map/all_to_all | solution.py:30
  205.1 30.6 %collective-permute-start.13 = (f32[15,1024]{1,0:T(8,128)S(1)}, f32[15,1024]{1,0:T(8,128)S(1)}, u32[]{:S(2)}, u32[]{:S(2)}) collective-permute-start(f32[15,1024]{1,0:T(8,128)S(1)} %get-tuple-element.48), channel_id=1, source_target_pairs={{4,0},{8,4},{12,8},{16,12},{20,16},{24,20},{28,24},{32,28},{36,32}... | collective-permute-start | bytes 184328 | tf_op jit(solution)/shard_map/ppermute | solution.py:15
  206.4 29.3 %collective-permute-start.14 = (f32[15,1024]{1,0:T(8,128)S(1)}, f32[15,1024]{1,0:T(8,128)S(1)}, u32[]{:S(2)}, u32[]{:S(2)}) collective-permute-start(f32[15,1024]{1,0:T(8,128)S(1)} %get-tuple-element.49), channel_id=1, source_target_pairs={{0,4},{4,8},{8,12},{12,16},{16,20},{20,24},{24,28},{28,32},{32,36}... | collective-permute-start | bytes 184328 | tf_op jit(solution)/shard_map/ppermute | solution.py:15
  209.5 26.2 %copy-start.2 = (f32[256,1024]{1,0:T(8,128)S(1)}, f32[256,1024]{1,0:T(8,128)}, u32[]{:S(2)}) copy-start(f32[256,1024]{1,0:T(8,128)} %scatter_custom_fusion) | copy-start | bytes 3145732
  209.5 26.2 %copy-start.10 = (f32[1,1024]{1,0:T(1,128)S(1)}, f32[1,1024]{1,0:T(1,128)}, u32[]{:S(2)}) copy-start(f32[1,1024]{1,0:T(1,128)} %copy-done.9) | copy-start | bytes 12292
  209.5 32.8 %collective-permute-start.17 = (f32[16,1024]{1,0:T(8,128)S(1)}, f32[16,1024]{1,0:T(8,128)S(1)}, u32[]{:S(2)}, u32[]{:S(2)}) collective-permute-start(f32[16,1024]{1,0:T(8,128)S(1)} %reduce_sum.432), channel_id=1, source_target_pairs={{0,4},{4,0},{1,5},{5,1},{2,6},{6,2},{3,7},{7,3},{8,12},{12,8},{9,1... | collective-permute-start | bytes 196616 | tf_op jit(solution)/shard_map/ppermute | solution.py:20
  232.1 17.8 %all-to-all-start.5 = ((bf16[8,2,16,1024]{3,2,1,0:T(8,128)(2,1)}), bf16[8,2,16,1024]{3,2,1,0:T(8,128)(2,1)S(1)}, u32[]{:S(2)}, u32[]{:S(2)}) async-start(bf16[8,2,16,1024]{3,2,1,0:T(8,128)(2,1)} %copy.102), calls=%async_computation.5 | async-start | bytes 1048576 | tf_op jit(solution)/shard_map/all_to_all | solution.py:30
  235.6 15.0 %copy-start.1 = (bf16[1,256,1024]{2,1,0:T(8,128)(2,1)S(1)}, bf16[1,256,1024]{2,1,0:T(8,128)(2,1)}, u32[]{:S(2)}) copy-start(bf16[1,256,1024]{2,1,0:T(8,128)(2,1)} %param.9) | copy-start | bytes 1572868
  (7 other events, 13.1 us)

commit v2 on v1

--- a/solution.py
+++ b/solution.py
@@ -1,6 +1,7 @@
 import jax
 import jax.numpy as jnp
 from jax import lax
+from jax.experimental.layout import Layout, with_layout_constraint
 from jax.sharding import Mesh, PartitionSpec as P
 
 norm_eps = 1e-05
@@ -35,23 +36,38 @@
     return exchange(jnp.broadcast_to(cells[None], (count,) + cells.shape), axis)
 
 
-def ring_gather(cells, axis):
-    count = lax.axis_size(axis)
-    me = lax.axis_index(axis)
-    out = jnp.zeros((count,) + cells.shape, cells.dtype)
-
-    def put(out, piece, owner):
-        return lax.dynamic_update_slice_in_dim(out, piece[None], owner % count, 0)
-
-    out = put(out, cells, me)
-    ahead = behind = cells
-    for step in range(1, count // 2 + 1):
-        ahead = turn(ahead, axis, 1)
-        out = put(out, ahead, me - step + count)
-        if 2 * step < count:
-            behind = turn(behind, axis, -1)
-            out = put(out, behind, me + step)
-    return out
+def pick(cells, which, axis):
+    return lax.dynamic_index_in_dim(cells, which, axis, keepdims=False)
+
+
+def gather_weights(pair, core):
+    half = spread(pair, "z")
+    half = spread(half, "y")
+    other = turn(half, "core", 1)
+    first = jnp.where(core == 0, half, other)
+    second = jnp.where(core == 0, other, half)
+    both = jnp.stack([first, second], axis=3)
+    width = pair.shape[-1]
+    return [both[:, :, i].reshape(-1, width) for i in range(2)]
+
+
+def scatter_grads(grads, core, rows):
+    ny, nz = lax.axis_size("y"), lax.axis_size("z")
+    cells = [g.reshape(ny, nz, 2, rows, g.shape[1]) for g in grads]
+    theirs = jnp.concatenate([pick(c, 1 - core, 2).astype(bf16) for c in cells], axis=1)
+    came = turn(theirs, "core", 1)
+    mine = jnp.concatenate([pick(c, core, 2) for c in cells], axis=1)
+    chip = (mine + came.astype(f32)).astype(bf16)
+    spot = lax.axis_index("y")
+    leave = [pick(chip, (spot + by) % ny, 0) for by in range(ny)]
+    came = [turn(leave[by], "y", by) for by in range(1, ny)]
+    chip = leave[0].astype(f32)
+    for part in came:
+        chip = chip + part.astype(f32)
+    chip = chip.astype(bf16)
+    chip = chip.reshape((2, nz) + chip.shape[1:]).transpose(1, 0, 2, 3)
+    chip = exchange(chip, "z")
+    return jnp.sum(chip.astype(f32), axis=0)
 
 
 def silu_grad(values):
@@ -68,17 +84,9 @@
     half_width = tap_count // 2
     shard = lax.axis_index(SEQ)
     core = lax.axis_index("core")
-    ny, nz = lax.axis_size("y"), lax.axis_size("z")
     rows_in = weight_in.shape[0]
-    hidden_dev = weight_in.shape[1]
-
-    pair = jnp.stack([weight_in, weight_out])
-    pieces = ring_gather(spread(pair, "y"), "z")
-    others = turn(pieces, "core", 1)
-    both = jnp.stack([jnp.where(core == 0, pieces, others), jnp.where(core == 0, others, pieces)])
-    both = both.transpose(3, 2, 1, 0, 4, 5)
-    w_in = both[0].reshape(width, hidden_dev)
-    w_out = both[1].reshape(hidden_dev, width)
+
+    w_in, w_out = gather_weights(jnp.stack([weight_in, weight_out]), core)
 
     counts = keep_count[0]
     blocks = (counts + BLOCK - 1) // BLOCK
@@ -89,12 +97,9 @@
     zero_bf = jnp.zeros((), bf16)
 
     def place(rows):
-        going = jnp.where(late, rows[:BLOCK], rows[BLOCK:])
+        going = jnp.where(late, rows[:, :BLOCK], rows[:, BLOCK:])
         came = shift(going, SEQ, 1)
-        return jnp.where(late, came, rows[:BLOCK])
-
-    picked_grad = place(jnp.where(valid[:, None], cotangent[0][local_index], zero_bf))
-    grad_all = spread(picked_grad, "utt").reshape(-1, width)
+        return jnp.where(late, came, rows[:, :BLOCK])
 
     wide_rows = with_halo(frames, half_width)
     wide32 = wide_rows.astype(f32)
@@ -102,7 +107,8 @@
     for offset in range(tap_count):
         conv_out = conv_out + conv_kernel[offset] * wide32[offset : offset + length]
     hidden = (frames.astype(f32) + jax.nn.silu(conv_out)).astype(bf16)
-    picked = place(jnp.where(valid[:, None], hidden[local_index], zero_bf))
+    kept = jnp.stack([hidden[local_index], cotangent[0][local_index]])
+    picked, picked_grad = place(jnp.where(valid[:, None], kept, zero_bf))
     rows32 = picked.astype(f32)
     row_mean = jnp.mean(rows32, axis=1, keepdims=True)
     centred = rows32 - row_mean
@@ -110,7 +116,12 @@
     inv_scale = lax.rsqrt(row_var + norm_eps)
     normed = centred * inv_scale
     scaled = (normed * norm_gain).astype(bf16)
-    scaled_all = spread(scaled, "utt").reshape(-1, width)
+    payload = jnp.stack([scaled, picked_grad])
+    utts = lax.axis_size("utt")
+    arrived = [payload] + [turn(payload, "utt", by) for by in range(1, utts)]
+    scaled_all, grad_all = (jnp.concatenate([a[i] for a in arrived]) for i in range(2))
+    plain = Layout(major_to_minor=(0, 1))
+    grad_all = with_layout_constraint(grad_all, plain)
 
     pre_act = jnp.dot(scaled_all, w_in, preferred_element_type=f32)
     activation = jax.nn.silu(pre_act).astype(bf16)
@@ -121,26 +132,16 @@
     partial_grad = lax.dot_general(
         up_grad, w_in, (((1,), (1,)), ((), ())), preferred_element_type=f32
     )
-    parts = exchange(partial_grad.astype(bf16).reshape(-1, BLOCK, width), "utt")
-    norm_grad = jnp.sum(parts.astype(f32), axis=0)
+    parts = partial_grad.reshape(utts, BLOCK, width)
+    norm_grad = parts[0]
+    owed = [turn(parts[by].astype(bf16), "utt", -by) for by in range(1, utts)]
+    for part in owed:
+        norm_grad = norm_grad + part.astype(f32)
 
     over_rows = (((0,), (0,)), ((), ()))
+    g_out = 0.5 * lax.dot_general(activation, grad_all, over_rows, preferred_element_type=f32)
     g_in = lax.dot_general(scaled_all, up_grad, over_rows, preferred_element_type=f32)
-    g_out = 0.5 * lax.dot_general(activation, grad_all, over_rows, preferred_element_type=f32)
-    grads = jnp.stack(
-        [
-            g_in.reshape(ny, nz, 2, rows_in, hidden_dev),
-            g_out.reshape(ny, nz, 2, rows_in, width),
-        ],
-        axis=2,
-    )
-    first, second = grads[:, :, :, 0], grads[:, :, :, 1]
-    theirs = jnp.where(core == 0, second, first).astype(bf16)
-    mine = jnp.where(core == 0, first, second)
-    chip = (mine + turn(theirs, "core", 1).astype(f32)).astype(bf16)
-    chip = jnp.sum(exchange(chip, "y").astype(f32), axis=0).astype(bf16)
-    chip = jnp.sum(exchange(chip, "z").astype(f32), axis=0)
-    grad_weight_in, grad_weight_out = chip[0], chip[1]
+    grad_weight_in, grad_weight_out = scatter_grads([g_in, g_out], core, rows_in)
 
     gain_term = jnp.sum(norm_grad * normed, axis=0)
     gain_grad = norm_grad * norm_gain
@@ -172,14 +173,13 @@
     grad_x = (frame_grad + transposed).astype(bf16)
 
     small = jnp.stack(kernel_term + [gain_term])
-    half = small.shape[0] // 2
-    own = jnp.where(core == 0, small[:half], small[half:])
-    gone = jnp.where(core == 0, small[half:], small[:half])
-    total = own + turn(gone, "core", 1)
-    for axis in ("utt", "y", "z"):
-        total = jnp.sum(spread(total, axis), axis=0)
-    back = turn(total, "core", 1)
-    full = jnp.concatenate([jnp.where(core == 0, total, back), jnp.where(core == 0, back, total)])
+    near = ("core", "utt")
+    part = exchange(small.reshape(lax.axis_size(near), 8, -1), near)
+    part = jnp.sum(part, axis=0)
+    part = spread(part, ("y", "z"))
+    part = jnp.sum(part, axis=0)
+    full = spread(part, near)
+    full = full.reshape(small.shape)
     return (grad_x[None], grad_weight_in, grad_weight_out, full[:tap_count], full[tap_count])
 
 

time: 252 us -> 226 us (0.90)
  blocking collectives: 19.6 us -> 0 us
  matrix products: 18.6 us -> 6.92 us
  waiting for transfers between devices: 73.3 us -> 80.8 us
  local copies, waits for them, and re-layouts: 31.3 us -> 25.4 us
  starting transfers between devices: 62.3 us -> 65.7 us
    ppermute x11, waiting for transfers between devices: 21.3 us -> 41.5 us  [turn(): lax.ppermute(cells, axis, [(i, (i + by) % count) for i in range(count)])]
    all_to_all x2 -> x0, blocking collectives: 19.6 us -> none  [exchange(): return lax.all_to_all(cells, axis, 0, 0, tiled=True)]
    all_to_all x7 -> x6, waiting for transfers between devices: 50.9 us -> 37.8 us  [exchange(): return lax.all_to_all(cells, axis, 0, 0, tiled=True)]
    ppermute x11, starting transfers between devices: 11.3 us -> 18 us  [turn(): lax.ppermute(cells, axis, [(i, (i + by) % count) for i in range(count)])]
    squeeze x1 -> x5, local copies, waits for them, and re-layouts: 0.66 us -> 7.24 us  [the longest x2 5.08 us: pick(): return lax.dynamic_index_in_dim(cells, which, axis, keepdims=False)]
    dynamic_update_slice x8 -> x0, local copies, waits for them, and re-layouts: 5.8 us -> none  [put(): return lax.dynamic_update_slice_in_dim(out, piece[None], owner % count, 0)]
    convert_element_type x2, other arithmetic: 9.39 us -> 5.74 us  [the longest x1 3.84 us: scatter_grads(): chip = (mine + came.astype(f32)).astype(bf16)]
    dot_general x1, matrix products: 4.87 us -> 1.29 us  [per_device(): lax.dot_general(scaled_all, up_grad, over_rows, preferred_element_type=f32)]
  transfers between devices with their start and end apart: 25 -> 23, of which waited for: 12 -> 13; matrix products, arithmetic and copies ran while one was open for 33% -> 27% of each run, Pallas kernels for 0% -> 0%
where the time goes in v2:
time: 226 us; the launch traced here: 224 us
  waiting for transfers between devices  80.8 us (36%)
  starting transfers between devices  65.7 us (29%)
  other arithmetic  42.9 us (19%)
  local copies, waits for them, and re-layouts  25.4 us (11%)
  matrix products  6.92 us (3%)
  between operations  2.29 us (1%)
    ppermute x11, waiting for transfers between devices, turn(): lax.ppermute(cells, axis, [(i, (i + by) % count) for i in range(count)])  41.5 us
    all_to_all x6, waiting for transfers between devices, exchange(): return lax.all_to_all(cells, axis, 0, 0, tiled=True)  37.8 us
    all_to_all x6, starting transfers between devices, exchange(): return lax.all_to_all(cells, axis, 0, 0, tiled=True)  37.7 us
    ppermute x11, starting transfers between devices, turn(): lax.ppermute(cells, axis, [(i, (i + by) % count) for i in range(count)])  18 us
    ppermute x6, starting transfers between devices, shift(): lax.ppermute(cells, axis, [(i, i + by) for i in range(count) if 0 <= i +...  9.97 us
    broadcast_in_dim x1, other arithmetic, per_device(): grad_x[None]  6.59 us
    reduce_sum x2, other arithmetic, per_device(): jnp.sum(conv_grad * wide32[offset:offset + length], axis=0)  5.62 us
    convert_element_type x1, other arithmetic, per_device(): hidden = (frames.astype(f32) + jax.nn.silu(conv_out)).astype(bf16)  5.17 us
  transfers between devices with their start and end apart: 23, of which 13 were waited for; matrix products, arithmetic and copies ran while one was open for 27% of the time, Pallas kernels for 0%

profile of v2, /device:TPU:2, one launch (start us, length us, event | category | flops | bytes accessed | tf_op | source)
XLA Modules:
  0.0 224.0 jit_solution(14103416494456339614)
XLA Ops:
  1.5 1.7 collective-permute-start
  3.3 1.3 collective-permute-start.1
  6.2 12.2 %all-to-all-start = ((bf16[8,2,16,1024]{3,2,1,0:T(8,128)(2,1)}), bf16[8,2,16,1024]{3,2,1,0:T(8,128)(2,1)S(1)}, u32[]{:S(2)}, u32[]{:S(2)}) async-start(bf16[8,2,16,1024]{3,2,1,0:T(8,128)(2,1)} %broadcast_in_dim.40), calls=%async_computation | async-start | bytes 1048576 | tf_op jit(solution)/shard_map/all_to_all | solution.py:31
  18.4 1.1 fusion.135
  19.6 1.4 fusion.134
  23.9 2.0 gather_fusion.1
  26.3 5.2 %add_convert_fusion = (bf16[256,1024]{1,0:T(8,128)(2,1)S(1)}, f32[256,1024]{1,0:T(8,128)}) fusion(bf16[1,256,1024]{2,1,0:T(8,128)(2,1)S(1)} %copy-done.2, f32[286,1024]{1,0:T(8,128)S(1)} %maximum_convert_fusion, f32[1024]{0:T(1024)S(1)} %bitcast.219, f32[1024]{0:T(1024)S(1)} %bitcast.221, f32[1024]{0:T(1024)S(1)} %bitcast.225, f32[1024]{0:T(1024)S(1)} %bitcast.227, ...), kind=kLoop, calls=%fused_computation.208 | loop fusion | flops 17825792 | bytes 34729984 | tf_op jit(solution)/shard_map/convert_element_type | solution.py:109
  31.5 2.0 gather_fusion
  34.3 1.6 broadcast_in_dim.41
  35.9 4.5 %all-to-all-start.1 = ((bf16[4,8,2,16,1024]{4,3,1,2,0:T(8,128)(2,1)}), bf16[4,8,2,16,1024]{4,3,1,2,0:T(8,128)(2,1)S(1)}, u32[]{:S(2)}, u32[]{:S(2)}) async-start(bf16[4,8,2,16,1024]{4,3,1,2,0:T(8,128)(2,1)} %broadcast_in_dim.41), calls=%async_computation.1 | async-start | bytes 4194304 | tf_op jit(solution)/shard_map/all_to_all | solution.py:31
  40.4 1.4 maximum_select_fusion
  41.8 1.3 collective-permute-start.2
  43.2 1.5 collective-permute-done.2
  45.5 1.1 convert_reduce_fusion.1
  46.6 23.0 %all-to-all-done.1 = bf16[4,8,2,16,1024]{4,3,1,2,0:T(8,128)(2,1)S(1)} async-done(((bf16[4,8,2,16,1024]{4,3,1,2,0:T(8,128)(2,1)}), bf16[4,8,2,16,1024]{4,3,1,2,0:T(8,128)(2,1)S(1)}, u32[]{:S(2)}, u32[]{:S(2)}) %all-to-all-start.1) | async-done | bytes 2097184 | tf_op jit(solution)/shard_map/all_to_all | solution.py:31
  69.6 1.5 copy.32
  71.2 1.2 fusion.115
  72.4 1.0 slice_bitcast_fusion.10
  73.4 1.2 fusion.100
  75.9 2.4 %collective-permute-start.4 = (bf16[2,128,1024]{2,1,0:T(8,128)(2,1)}, bf16[2,128,1024]{2,1,0:T(8,128)(2,1)}, u32[]{:S(2)}, u32[]{:S(2)}) collective-permute-start(bf16[2,128,1024]{2,1,0:T(8,128)(2,1)} %pad_maximum_fusion.6), channel_id=1, source_target_pairs={{0,2},{1,3},{2,0},{3,1},{4,6},{5,7},{6,4},{7,5},{8,10},{9,11},{10,... | collective-permute-start | bytes 1572872 | tf_op jit(solution)/shard_map/ppermute | solution.py:21
  78.3 1.8 collective-permute-start.3
  80.1 1.2 fusion.108
  81.3 8.7 %collective-permute-done.5 = bf16[2,128,1024]{2,1,0:T(8,128)(2,1)} collective-permute-done((bf16[2,128,1024]{2,1,0:T(8,128)(2,1)}, bf16[2,128,1024]{2,1,0:T(8,128)(2,1)}, u32[]{:S(2)}, u32[]{:S(2)}) %collective-permute-start.5) | collective-permute-done | bytes 524320 | tf_op jit(solution)/shard_map/ppermute | solution.py:21
  90.0 1.1 slice_bitcast_fusion.3
  91.1 11.1 %collective-permute-done.4 = bf16[2,128,1024]{2,1,0:T(8,128)(2,1)} collective-permute-done((bf16[2,128,1024]{2,1,0:T(8,128)(2,1)}, bf16[2,128,1024]{2,1,0:T(8,128)(2,1)}, u32[]{:S(2)}, u32[]{:S(2)}) %collective-permute-start.4) | collective-permute-done | bytes 524320 | tf_op jit(solution)/shard_map/ppermute | solution.py:21
  102.2 1.1 slice_bitcast_fusion.4
  103.3 1.9 select_bitcast_fusion.1
  105.6 1.3 fusion.124
  106.9 1.3 convolution_multiply_fusion
  108.3 1.7 multiply_convert_fusion.1
  110.0 1.3 fusion.136
  111.3 2.5 %collective-permute-start.7 = (bf16[128,1024]{1,0:T(8,128)(2,1)S(1)}, bf16[128,1024]{1,0:T(8,128)(2,1)S(1)}, u32[]{:S(2)}, u32[]{:S(2)}) collective-permute-start(bf16[128,1024]{1,0:T(8,128)(2,1)S(1)} %get-tuple-element.52), channel_id=1, source_target_pairs={{0,3},{1,0},{2,1},{3,2},{4,7},{5,4},{6,5},{7,6},{8,11},{9,8},{10,9... | collective-permute-start | bytes 786440 | tf_op jit(solution)/shard_map/ppermute | solution.py:21
  113.8 4.3 %collective-permute-start.8 = (bf16[128,1024]{1,0:T(8,128)(2,1)S(1)}, bf16[128,1024]{1,0:T(8,128)(2,1)S(1)}, u32[]{:S(2)}, u32[]{:S(2)}) collective-permute-start(bf16[128,1024]{1,0:T(8,128)(2,1)S(1)} %get-tuple-element.54), channel_id=1, source_target_pairs={{0,2},{1,3},{2,0},{3,1},{4,6},{5,7},{6,4},{7,5},{8,10},{9,11},{10,... | collective-permute-start | bytes 786440 | tf_op jit(solution)/shard_map/ppermute | solution.py:21
  118.1 1.3 fusion.123
  119.5 1.1 collective-permute-done.7
  120.5 2.7 %collective-permute-done.9 = bf16[128,1024]{1,0:T(8,128)(2,1)S(1)} collective-permute-done((bf16[128,1024]{1,0:T(8,128)(2,1)S(1)}, bf16[128,1024]{1,0:T(8,128)(2,1)S(1)}, u32[]{:S(2)}, u32[]{:S(2)}) %collective-permute-start.9) | collective-permute-done | bytes 262176 | tf_op jit(solution)/shard_map/ppermute | solution.py:21
  123.2 3.4 %collective-permute-done.8 = bf16[128,1024]{1,0:T(8,128)(2,1)S(1)} collective-permute-done((bf16[128,1024]{1,0:T(8,128)(2,1)S(1)}, bf16[128,1024]{1,0:T(8,128)(2,1)S(1)}, u32[]{:S(2)}, u32[]{:S(2)}) %collective-permute-start.8) | collective-permute-done | bytes 262176 | tf_op jit(solution)/shard_map/ppermute | solution.py:21
  126.7 1.3 fusion.114
  128.0 1.3 fusion.113
  129.3 1.3 collective-permute-start.10
  131.0 1.5 pad_maximum_fusion.1
  132.5 1.1 collective-permute-start.13
  133.7 3.2 %scatter_custom_fusion = f32[256,1024]{1,0:T(8,128)S(1)} fusion(s32[256]{0:T(256)} %bitcast.296, bf16[128,1024]{1,0:T(8,128)(2,1)S(1)} %collective-permute-done.10, bf16[]{:T(256)} %constant.122, bf16[128,1024]{1,0:T(8,128)(2,1)S(1)} %broadcast_select_fusion.1, f32[]{:T(128)} %constant.94.clone.1, pred[256]{0:T(512)(128)(4,1)S(1)} %copy-done.42), kind=kCustom, calls=%fused_computation.238 | custom fusion | flops 1572864 | bytes 1574656 | tf_op jit(solution)/shard_map/scatter-add | solution.py:161
  136.8 3.9 %multiply_reduce_fusion = (f32[1024]{0:T(1024)S(1)}, f32[1024]{0:T(1024)S(1)}, f32[1024]{0:T(1024)S(1)}, f32[1024]{0:T(1024)S(1)}, f32[1024]{0:T(1024)S(1)}, /*i...) fusion(f32[286,1024]{1,0:T(8,128)S(1)} %maximum_convert_fusion,, ...), kind=kLoop, calls=%fused_computation.173 | loop fusion | flops 11515904 | bytes 22093824 | tf_op jit(solution)/shard_map/reduce_sum | solution.py:166
  140.7 1.8 multiply_reduce_fusion.1
  143.4 7.5 %all-to-all-start.3 = ((f32[8,8,512]{2,1,0:T(8,128)}), f32[8,8,512]{2,1,0:T(8,128)S(1)}, u32[]{:S(2)}, u32[]{:S(2)}) async-start(f32[8,8,512]{2,1,0:T(8,128)} %reshape.125), calls=%async_computation.3 | async-start | bytes 262144 | tf_op jit(solution)/shard_map/all_to_all | solution.py:31
  150.9 4.5 %all-to-all-done.3 = f32[8,8,512]{2,1,0:T(8,128)S(1)} async-done(((f32[8,8,512]{2,1,0:T(8,128)}), f32[8,8,512]{2,1,0:T(8,128)S(1)}, u32[]{:S(2)}, u32[]{:S(2)}) %all-to-all-start.3) | async-done | bytes 131104 | tf_op jit(solution)/shard_map/all_to_all | solution.py:31
  155.4 0.9 broadcast_in_dim.43
  156.2 3.9 %all-to-all-start.4 = ((f32[32,8,512]{2,1,0:T(8,128)}), f32[32,8,512]{2,1,0:T(8,128)S(1)}, u32[]{:S(2)}, u32[]{:S(2)}) async-start(f32[32,8,512]{2,1,0:T(8,128)} %broadcast_in_dim.43), calls=%async_computation.4 | async-start | bytes 1048576 | tf_op jit(solution)/shard_map/all_to_all | solution.py:31
  160.1 2.5 %dynamic-slice_bitcast_fusion = (f32[4,8,16,1024]{3,2,1,0:T(8,128)S(1)}, f32[4,8,16,1024]{3,2,1,0:T(8,128)S(1)}) fusion(f32[4,8,2,16,1024]{4,3,2,1,0:T(8,128)} %bitcast.189, s32[]{:T(128)S(6)} %select_n.119, f32[4,8,2,16,1024]{4,3,2,1,0:T(8,128)} %bitcast.191), kind=kLoop, calls=%fused_computation.41 | loop fusion | bytes 8388612 | tf_op jit(solution)/shard_map/jit(dynamic_index_in_dim)/squeeze | solution.py:40
  162.7 3.8 %fusion = bf16[4,16,16,1024]{3,2,1,0:T(8,128)(2,1)} fusion(f32[4,8,16,1024]{3,2,1,0:T(8,128)S(1)} %get-tuple-element.102, f32[4,8,16,1024]{3,2,1,0:T(8,128)S(1)} %get-tuple-element.103, bf16[4,16,16,1024]{3,2,1,0:T(8,128)(2,1)} %collective-permute-done.13), kind=kLoop, calls=%fused_computation.34 | loop fusion | flops 4194304 | bytes 8388608 | tf_op jit(solution)/shard_map/convert_element_type | solution.py:60
  166.5 2.5 %dynamic-slice_bitcast_fusion.4 = (bf16[16,16,1024]{2,1,0:T(8,128)(2,1)}, bf16[16,16,1024]{2,1,0:T(8,128)(2,1)}, bf16[16,16,1024]{2,1,0:T(8,128)(2,1)S(1)}) fusion(bf16[4,16,16,1024]{3,2,1,0:T(8,128)(2,1)} %fusion, s32[]{:T(128)S(6)} %select_n.124, s32[]{:T(128)S(6)} %select_n.128, s32[]{:T(128)S(6)} %select_n.126), kind=kLoop, calls=%fused_computation.242 | loop fusion | bytes 3145740 | tf_op jit(solution)/shard_map/jit(dynamic_index_in_dim)/squeeze | solution.py:40
  169.1 1.8 collective-permute-start.14
  170.8 1.5 collective-permute-start.16
  172.3 2.1 collective-permute-start.15
  174.4 1.3 collective-permute-start.11
  175.7 3.0 %collective-permute-start.12 = (f32[15,1024]{1,0:T(8,128)S(1)}, f32[15,1024]{1,0:T(8,128)S(1)}, u32[]{:S(2)}, u32[]{:S(2)}) collective-permute-start(f32[15,1024]{1,0:T(8,128)S(1)} %get-tuple-element.51), channel_id=1, source_target_pairs={{0,4},{4,8},{8,12},{12,16},{16,20},{20,24},{24,28},{28,32},{32,36}... | collective-permute-start | bytes 184328 | tf_op jit(solution)/shard_map/ppermute | solution.py:16
  179.5 4.8 %all-to-all-start.5 = ((f32[8,8,512]{2,1,0:T(8,128)}), f32[8,8,512]{2,1,0:T(8,128)S(1)}, u32[]{:S(2)}, u32[]{:S(2)}) async-start(f32[8,8,512]{2,1,0:T(8,128)} %broadcast_in_dim.44), calls=%async_computation.5 | async-start | bytes 262144 | tf_op jit(solution)/shard_map/all_to_all | solution.py:31
  184.2 2.2 collective-permute-done.14
  186.5 12.3 %collective-permute-done.15 = bf16[16,16,1024]{2,1,0:T(8,128)(2,1)} collective-permute-done((bf16[16,16,1024]{2,1,0:T(8,128)(2,1)S(1)}, bf16[16,16,1024]{2,1,0:T(8,128)(2,1)}, u32[]{:S(2)}, u32[]{:S(2)}) %collective-permute-start.15) | collective-permute-done | bytes 524320 | tf_op jit(solution)/shard_map/ppermute | solution.py:21
  198.7 1.9 fusion.96
  201.5 4.9 %all-to-all-start.2 = ((bf16[8,2,16,1024]{3,2,1,0:T(8,128)(2,1)}), bf16[8,2,16,1024]{3,2,1,0:T(8,128)(2,1)S(1)}, u32[]{:S(2)}, u32[]{:S(2)}) async-start(bf16[8,2,16,1024]{3,2,1,0:T(8,128)(2,1)} %copy.37), calls=%async_computation.2 | async-start | bytes 1048576 | tf_op jit(solution)/shard_map/all_to_all | solution.py:31
  206.4 6.6 %fusion.122 = bf16[1,256,1024]{2,1,0:T(8,128)(2,1)} fusion(f32[256,1024]{1,0:T(8,128)S(1)} %scatter_custom_fusion, f32[256,1024]{1,0:T(8,128)S(1)} %get-tuple-element.39, f32[15,1024]{1,0:T(8,128)S(1)} %collective-permute-done.12, f32[1024]{0:T(1024)} %bitcast.220, f32[1024]{0:T(1024)} %bitcast.222, f32[1024]{0:T(1024)} %bitcast.226, f32[1024]{0:T(1024)} %bitcast.228, ...), kind=kLoop, calls=%fused_computation.246 | loop fusion | flops 24379392 | bytes 2871296 | tf_op jit(solution)/shard_map/broadcast_in_dim | solution.py:183
  213.7 9.5 %all-to-all-done.2 = bf16[8,2,16,1024]{3,2,1,0:T(8,128)(2,1)S(1)} async-done(((bf16[8,2,16,1024]{3,2,1,0:T(8,128)(2,1)}), bf16[8,2,16,1024]{3,2,1,0:T(8,128)(2,1)S(1)}, u32[]{:S(2)}, u32[]{:S(2)}) %all-to-all-start.2) | async-done | bytes 524320 | tf_op jit(solution)/shard_map/all_to_all | solution.py:31
  (137 shorter events, 12.8 us)
Async XLA Ops:
  0.6 23.2 %copy-start = (bf16[1,256,1024]{2,1,0:T(8,128)(2,1)S(1)}, bf16[1,256,1024]{2,1,0:T(8,128)(2,1)}, u32[]{:S(2)}) copy-start(bf16[1,256,1024]{2,1,0:T(8,128)(2,1)} %param.9) | copy-start | bytes 1572868
  0.6 20.5 %copy-start.44 = (s32[1,64]{1,0:T(1,128)S(1)}, s32[1,64]{1,0:T(1,128)}, u32[]{:S(2)}) copy-start(s32[1,64]{1,0:T(1,128)} %param.14) | copy-start | bytes 772
  0.7 21.8 %copy-start.43 = (s32[1,256]{1,0:T(1,128)S(1)}, s32[1,256]{1,0:T(1,128)}, u32[]{:S(2)}) copy-start(s32[1,256]{1,0:T(1,128)} %param.15) | copy-start | bytes 3076
  1.5 24.4 %collective-permute-start = (bf16[15,1024]{1,0:T(8,128)(2,1)S(1)}, bf16[15,1024]{1,0:T(8,128)(2,1)S(1)}, u32[]{:S(2)}, u32[]{:S(2)}) collective-permute-start(bf16[15,1024]{1,0:T(8,128)(2,1)S(1)} %get-tuple-element.63), channel_id=1, source_target_pairs={{0,4},{4,8},{8,12},{12,16},{16,20},{20,24},{24,28},{28,32},{32,36}... | collective-permute-start | bytes 92168 | tf_op jit(solution)/shard_map/ppermute | solution.py:16
  3.3 22.6 %collective-permute-start.1 = (bf16[15,1024]{1,0:T(8,128)(2,1)S(1)}, bf16[15,1024]{1,0:T(8,128)(2,1)S(1)}, u32[]{:S(2)}, u32[]{:S(2)}) collective-permute-start(bf16[15,1024]{1,0:T(8,128)(2,1)S(1)} %get-tuple-element.64), channel_id=1, source_target_pairs={{4,0},{8,4},{12,8},{16,12},{20,16},{24,20},{28,24},{32,28},{36,32}... | collective-permute-start | bytes 92168 | tf_op jit(solution)/shard_map/ppermute | solution.py:16
  6.2 28.1 %all-to-all-start = ((bf16[8,2,16,1024]{3,2,1,0:T(8,128)(2,1)}), bf16[8,2,16,1024]{3,2,1,0:T(8,128)(2,1)S(1)}, u32[]{:S(2)}, u32[]{:S(2)}) async-start(bf16[8,2,16,1024]{3,2,1,0:T(8,128)(2,1)} %broadcast_in_dim.40), calls=%async_computation | async-start | bytes 1048576 | tf_op jit(solution)/shard_map/all_to_all | solution.py:31
  19.5 6.5 %copy-start.7 = (f32[1,1024]{1,0:T(1,128)}, f32[1,1024]{1,0:T(1,128)S(1)}, u32[]{:S(2)}) copy-start(f32[1,1024]{1,0:T(1,128)S(1)} %get-tuple-element.89) | copy-start | bytes 12292
  19.5 6.5 %copy-start.9 = (f32[1,1024]{1,0:T(1,128)}, f32[1,1024]{1,0:T(1,128)S(1)}, u32[]{:S(2)}) copy-start(f32[1,1024]{1,0:T(1,128)S(1)} %get-tuple-element.90) | copy-start | bytes 12292
  19.5 6.5 %copy-start.10 = (f32[1,1024]{1,0:T(1,128)}, f32[1,1024]{1,0:T(1,128)S(1)}, u32[]{:S(2)}) copy-start(f32[1,1024]{1,0:T(1,128)S(1)} %get-tuple-element.91) | copy-start | bytes 12292
  19.5 6.5 %copy-start.11 = (f32[1,1024]{1,0:T(1,128)}, f32[1,1024]{1,0:T(1,128)S(1)}, u32[]{:S(2)}) copy-start(f32[1,1024]{1,0:T(1,128)S(1)} %get-tuple-element.92) | copy-start | bytes 12292
  19.6 6.5 %copy-start.12 = (f32[1,1024]{1,0:T(1,128)}, f32[1,1024]{1,0:T(1,128)S(1)}, u32[]{:S(2)}) copy-start(f32[1,1024]{1,0:T(1,128)S(1)} %get-tuple-element.93) | copy-start | bytes 12292
  19.6 6.5 %copy-start.13 = (f32[1,1024]{1,0:T(1,128)}, f32[1,1024]{1,0:T(1,128)S(1)}, u32[]{:S(2)}) copy-start(f32[1,1024]{1,0:T(1,128)S(1)} %get-tuple-element.94) | copy-start | bytes 12292
  19.6 6.5 %copy-start.14 = (f32[1,1024]{1,0:T(1,128)}, f32[1,1024]{1,0:T(1,128)S(1)}, u32[]{:S(2)}) copy-start(f32[1,1024]{1,0:T(1,128)S(1)} %get-tuple-element.95) | copy-start | bytes 12292
  19.6 6.5 %copy-start.15 = (f32[1,1024]{1,0:T(1,128)}, f32[1,1024]{1,0:T(1,128)S(1)}, u32[]{:S(2)}) copy-start(f32[1,1024]{1,0:T(1,128)S(1)} %get-tuple-element.96) | copy-start | bytes 12292
  19.6 6.5 %copy-start.16 = (f32[1,1024]{1,0:T(1,128)}, f32[1,1024]{1,0:T(1,128)S(1)}, u32[]{:S(2)}) copy-start(f32[1,1024]{1,0:T(1,128)S(1)} %get-tuple-element.97) | copy-start | bytes 12292
  21.0 5.2 %copy-start.17 = (f32[1,1024]{1,0:T(1,128)}, f32[1,1024]{1,0:T(1,128)S(1)}, u32[]{:S(2)}) copy-start(f32[1,1024]{1,0:T(1,128)S(1)} %get-tuple-element.67) | copy-start | bytes 12292
  21.0 5.2 %copy-start.18 = (f32[1,1024]{1,0:T(1,128)}, f32[1,1024]{1,0:T(1,128)S(1)}, u32[]{:S(2)}) copy-start(f32[1,1024]{1,0:T(1,128)S(1)} %get-tuple-element.68) | copy-start | bytes 12292
  21.0 5.2 %copy-start.19 = (f32[1,1024]{1,0:T(1,128)}, f32[1,1024]{1,0:T(1,128)S(1)}, u32[]{:S(2)}) copy-start(f32[1,1024]{1,0:T(1,128)S(1)} %get-tuple-element.69) | copy-start | bytes 12292
  21.0 5.2 %copy-start.20 = (f32[1,1024]{1,0:T(1,128)}, f32[1,1024]{1,0:T(1,128)S(1)}, u32[]{:S(2)}) copy-start(f32[1,1024]{1,0:T(1,128)S(1)} %get-tuple-element.70) | copy-start | bytes 12292
  21.0 5.2 %copy-start.21 = (f32[1,1024]{1,0:T(1,128)}, f32[1,1024]{1,0:T(1,128)S(1)}, u32[]{:S(2)}) copy-start(f32[1,1024]{1,0:T(1,128)S(1)} %get-tuple-element.71) | copy-start | bytes 12292
  21.0 5.2 %copy-start.22 = (f32[1,1024]{1,0:T(1,128)}, f32[1,1024]{1,0:T(1,128)S(1)}, u32[]{:S(2)}) copy-start(f32[1,1024]{1,0:T(1,128)S(1)} %get-tuple-element.72) | copy-start | bytes 12292
  21.0 5.2 %copy-start.23 = (f32[1,1024]{1,0:T(1,128)}, f32[1,1024]{1,0:T(1,128)S(1)}, u32[]{:S(2)}) copy-start(f32[1,1024]{1,0:T(1,128)S(1)} %get-tuple-element.73) | copy-start | bytes 12292
  21.1 5.2 %copy-start.24 = (f32[1,1024]{1,0:T(1,128)}, f32[1,1024]{1,0:T(1,128)S(1)}, u32[]{:S(2)}) copy-start(f32[1,1024]{1,0:T(1,128)S(1)} %get-tuple-element.74) | copy-start | bytes 12292
  21.1 5.2 %copy-start.25 = (f32[1,1024]{1,0:T(1,128)}, f32[1,1024]{1,0:T(1,128)S(1)}, u32[]{:S(2)}) copy-start(f32[1,1024]{1,0:T(1,128)S(1)} %get-tuple-element.75) | copy-start | bytes 12292
  21.1 5.2 %copy-start.26 = (f32[1,1024]{1,0:T(1,128)}, f32[1,1024]{1,0:T(1,128)S(1)}, u32[]{:S(2)}) copy-start(f32[1,1024]{1,0:T(1,128)S(1)} %get-tuple-element.76) | copy-start | bytes 12292
  21.1 5.2 %copy-start.27 = (f32[1,1024]{1,0:T(1,128)}, f32[1,1024]{1,0:T(1,128)S(1)}, u32[]{:S(2)}) copy-start(f32[1,1024]{1,0:T(1,128)S(1)} %get-tuple-element.77) | copy-start | bytes 12292
  21.1 5.2 %copy-start.28 = (f32[1,1024]{1,0:T(1,128)}, f32[1,1024]{1,0:T(1,128)S(1)}, u32[]{:S(2)}) copy-start(f32[1,1024]{1,0:T(1,128)S(1)} %get-tuple-element.78) | copy-start | bytes 12292
  21.1 5.2 %copy-start.29 = (f32[1,1024]{1,0:T(1,128)}, f32[1,1024]{1,0:T(1,128)S(1)}, u32[]{:S(2)}) copy-start(f32[1,1024]{1,0:T(1,128)S(1)} %get-tuple-element.79) | copy-start | bytes 12292
  21.1 5.2 %copy-start.30 = (f32[1,1024]{1,0:T(1,128)}, f32[1,1024]{1,0:T(1,128)S(1)}, u32[]{:S(2)}) copy-start(f32[1,1024]{1,0:T(1,128)S(1)} %get-tuple-element.80) | copy-start | bytes 12292
  21.1 5.2 %copy-start.31 = (f32[1,1024]{1,0:T(1,128)}, f32[1,1024]{1,0:T(1,128)S(1)}, u32[]{:S(2)}) copy-start(f32[1,1024]{1,0:T(1,128)S(1)} %get-tuple-element.81) | copy-start | bytes 12292
  21.1 5.2 %copy-start.32 = (f32[1,1024]{1,0:T(1,128)}, f32[1,1024]{1,0:T(1,128)S(1)}, u32[]{:S(2)}) copy-start(f32[1,1024]{1,0:T(1,128)S(1)} %get-tuple-element.82) | copy-start | bytes 12292
  21.1 5.2 %copy-start.33 = (f32[1,1024]{1,0:T(1,128)}, f32[1,1024]{1,0:T(1,128)S(1)}, u32[]{:S(2)}) copy-start(f32[1,1024]{1,0:T(1,128)S(1)} %get-tuple-element.83) | copy-start | bytes 12292
  21.2 5.2 %copy-start.34 = (f32[1,1024]{1,0:T(1,128)}, f32[1,1024]{1,0:T(1,128)S(1)}, u32[]{:S(2)}) copy-start(f32[1,1024]{1,0:T(1,128)S(1)} %get-tuple-element.84) | copy-start | bytes 12292
  21.2 5.2 %copy-start.35 = (f32[1,1024]{1,0:T(1,128)}, f32[1,1024]{1,0:T(1,128)S(1)}, u32[]{:S(2)}) copy-start(f32[1,1024]{1,0:T(1,128)S(1)} %get-tuple-element.85) | copy-start | bytes 12292
  23.2 17.2 %copy-start.41 = (pred[256]{0:T(512)(128)(4,1)}, pred[256]{0:T(512)(128)(4,1)S(1)}, u32[]{:S(2)}) copy-start(pred[256]{0:T(512)(128)(4,1)S(1)} %iota_compare_fusion) | copy-start | bytes 772
  35.9 33.7 %all-to-all-start.1 = ((bf16[4,8,2,16,1024]{4,3,1,2,0:T(8,128)(2,1)}), bf16[4,8,2,16,1024]{4,3,1,2,0:T(8,128)(2,1)S(1)}, u32[]{:S(2)}, u32[]{:S(2)}) async-start(bf16[4,8,2,16,1024]{4,3,1,2,0:T(8,128)(2,1)} %broadcast_in_dim.41), calls=%async_computation.1 | async-start | bytes 4194304 | tf_op jit(solution)/shard_map/all_to_all | solution.py:31
  41.8 2.8 %collective-permute-start.2 = (bf16[2,128,1024]{2,1,0:T(8,128)(2,1)S(1)}, bf16[2,128,1024]{2,1,0:T(8,128)(2,1)S(1)}, u32[]{:S(2)}, u32[]{:S(2)}) collective-permute-start(bf16[2,128,1024]{2,1,0:T(8,128)(2,1)S(1)} %slice_select_fusion), channel_id=1, source_target_pairs={{0,4},{4,8},{8,12},{12,16},{16,20},{20,24},{24,28},{28,32},{32,36}... | collective-permute-start | bytes 1572872 | tf_op jit(solution)/shard_map/ppermute | solution.py:16
  46.6 24.6 %copy-start.36 = (f32[128]{0:T(128)}, f32[128]{0:T(128)S(1)}, u32[]{:S(2)}) copy-start(f32[128]{0:T(128)S(1)} %broadcast_multiply_fusion.2) | copy-start | bytes 1540
  46.6 26.7 %copy-start.6 = (f32[1024]{0:T(1024)S(1)}, f32[1024]{0:T(1024)}, u32[]{:S(2)}) copy-start(f32[1024]{0:T(1024)} %param.11) | copy-start | bytes 12292
  71.2 32.2 %collective-permute-start.6 = (bf16[4,8,2,16,1024]{4,3,1,0,2:T(8,128)(2,1)}, bf16[4,8,2,16,1024]{4,3,1,0,2:T(8,128)(2,1)}, u32[]{:S(2)}, u32[]{:S(2)}) collective-permute-start(bf16[4,8,2,16,1024]{4,3,1,0,2:T(8,128)(2,1)} %copy.32), channel_id=1, source_target_pairs={{0,4},{4,0},{1,5},{5,1},{2,6},{6,2},{3,7},{7,3},{8,12},{12,8},{9,1... | collective-permute-start | bytes 6291464 | tf_op jit(solution)/shard_map/ppermute | solution.py:21
  75.4 14.7 %collective-permute-start.5 = (bf16[2,128,1024]{2,1,0:T(8,128)(2,1)}, bf16[2,128,1024]{2,1,0:T(8,128)(2,1)}, u32[]{:S(2)}, u32[]{:S(2)}) collective-permute-start(bf16[2,128,1024]{2,1,0:T(8,128)(2,1)} %pad_maximum_fusion.6), channel_id=1, source_target_pairs={{0,3},{1,0},{2,1},{3,2},{4,7},{5,4},{6,5},{7,6},{8,11},{9,8},{10,9... | collective-permute-start | bytes 1572872 | tf_op jit(solution)/shard_map/ppermute | solution.py:21
  75.9 26.3 %collective-permute-start.4 = (bf16[2,128,1024]{2,1,0:T(8,128)(2,1)}, bf16[2,128,1024]{2,1,0:T(8,128)(2,1)}, u32[]{:S(2)}, u32[]{:S(2)}) collective-permute-start(bf16[2,128,1024]{2,1,0:T(8,128)(2,1)} %pad_maximum_fusion.6), channel_id=1, source_target_pairs={{0,2},{1,3},{2,0},{3,1},{4,6},{5,7},{6,4},{7,5},{8,10},{9,11},{10,... | collective-permute-start | bytes 1572872 | tf_op jit(solution)/shard_map/ppermute | solution.py:21
  78.3 24.9 %collective-permute-start.3 = (bf16[2,128,1024]{2,1,0:T(8,128)(2,1)}, bf16[2,128,1024]{2,1,0:T(8,128)(2,1)S(1)}, u32[]{:S(2)}, u32[]{:S(2)}) collective-permute-start(bf16[2,128,1024]{2,1,0:T(8,128)(2,1)} %pad_maximum_fusion.6), channel_id=1, source_target_pairs={{0,1},{1,2},{2,3},{3,0},{4,5},{5,6},{6,7},{7,4},{8,9},{9,10},{10,1... | collective-permute-start | bytes 1572872 | tf_op jit(solution)/shard_map/ppermute | solution.py:21
  108.2 22.4 %copy-start.3 = (f32[1024,1024]{1,0:T(8,128)}, f32[1024,1024]{1,0:T(8,128)S(1)}, u32[]{:S(2)}) copy-start(f32[1024,1024]{1,0:T(8,128)S(1)} %convolution_multiply_fusion) | copy-start | bytes 12582916
  111.3 9.2 %collective-permute-start.7 = (bf16[128,1024]{1,0:T(8,128)(2,1)S(1)}, bf16[128,1024]{1,0:T(8,128)(2,1)S(1)}, u32[]{:S(2)}, u32[]{:S(2)}) collective-permute-start(bf16[128,1024]{1,0:T(8,128)(2,1)S(1)} %get-tuple-element.52), channel_id=1, source_target_pairs={{0,3},{1,0},{2,1},{3,2},{4,7},{5,4},{6,5},{7,6},{8,11},{9,8},{10,9... | collective-permute-start | bytes 786440 | tf_op jit(solution)/shard_map/ppermute | solution.py:21
  113.8 9.4 %collective-permute-start.9 = (bf16[128,1024]{1,0:T(8,128)(2,1)S(1)}, bf16[128,1024]{1,0:T(8,128)(2,1)S(1)}, u32[]{:S(2)}, u32[]{:S(2)}) collective-permute-start(bf16[128,1024]{1,0:T(8,128)(2,1)S(1)} %get-tuple-element.53), channel_id=1, source_target_pairs={{0,1},{1,2},{2,3},{3,0},{4,5},{5,6},{6,7},{7,4},{8,9},{9,10},{10,1... | collective-permute-start | bytes 786440 | tf_op jit(solution)/shard_map/ppermute | solution.py:21
  113.8 12.8 %copy-start.37 = (f32[128]{0:T(128)S(1)}, f32[128]{0:T(128)}, u32[]{:S(2)}) copy-start(f32[128]{0:T(128)} %copy-done.36) | copy-start | bytes 1540
  113.8 12.8 %copy-start.39 = (f32[128]{0:T(128)S(1)}, f32[128]{0:T(128)}, u32[]{:S(2)}) copy-start(f32[128]{0:T(128)} %copy-done.38) | copy-start | bytes 1540
  113.8 12.8 %collective-permute-start.8 = (bf16[128,1024]{1,0:T(8,128)(2,1)S(1)}, bf16[128,1024]{1,0:T(8,128)(2,1)S(1)}, u32[]{:S(2)}, u32[]{:S(2)}) collective-permute-start(bf16[128,1024]{1,0:T(8,128)(2,1)S(1)} %get-tuple-element.54), channel_id=1, source_target_pairs={{0,2},{1,3},{2,0},{3,1},{4,6},{5,7},{6,4},{7,5},{8,10},{9,11},{10,... | collective-permute-start | bytes 786440 | tf_op jit(solution)/shard_map/ppermute | solution.py:21
  119.4 11.5 %copy-start.4 = (f32[1024,1024]{1,0:T(8,128)}, f32[1024,1024]{1,0:T(8,128)S(1)}, u32[]{:S(2)}) copy-start(f32[1024,1024]{1,0:T(8,128)S(1)} %fusion.123) | copy-start | bytes 12582916
  129.3 4.3 %collective-permute-start.10 = (bf16[128,1024]{1,0:T(8,128)(2,1)S(1)}, bf16[128,1024]{1,0:T(8,128)(2,1)S(1)}, u32[]{:S(2)}, u32[]{:S(2)}) collective-permute-start(bf16[128,1024]{1,0:T(8,128)(2,1)S(1)} %fusion.113), channel_id=1, source_target_pairs={{4,0},{8,4},{12,8},{16,12},{20,16},{24,20},{28,24},{32,28},{36,32}... | collective-permute-start | bytes 786440 | tf_op jit(solution)/shard_map/ppermute | solution.py:16
  132.5 30.2 %collective-permute-start.13 = (bf16[4,16,16,1024]{3,2,1,0:T(8,128)(2,1)}, bf16[4,16,16,1024]{3,2,1,0:T(8,128)(2,1)}, u32[]{:S(2)}, u32[]{:S(2)}) collective-permute-start(bf16[4,16,16,1024]{3,2,1,0:T(8,128)(2,1)} %pad_maximum_fusion.1), channel_id=1, source_target_pairs={{0,4},{4,0},{1,5},{5,1},{2,6},{6,2},{3,7},{7,3},{8,12},{12,8},{9,1... | collective-permute-start | bytes 6291464 | tf_op jit(solution)/shard_map/ppermute | solution.py:21
  143.4 12.0 %all-to-all-start.3 = ((f32[8,8,512]{2,1,0:T(8,128)}), f32[8,8,512]{2,1,0:T(8,128)S(1)}, u32[]{:S(2)}, u32[]{:S(2)}) async-start(f32[8,8,512]{2,1,0:T(8,128)} %reshape.125), calls=%async_computation.3 | async-start | bytes 262144 | tf_op jit(solution)/shard_map/all_to_all | solution.py:31
  156.2 22.5 %all-to-all-start.4 = ((f32[32,8,512]{2,1,0:T(8,128)}), f32[32,8,512]{2,1,0:T(8,128)S(1)}, u32[]{:S(2)}, u32[]{:S(2)}) async-start(f32[32,8,512]{2,1,0:T(8,128)} %broadcast_in_dim.43), calls=%async_computation.4 | async-start | bytes 1048576 | tf_op jit(solution)/shard_map/all_to_all | solution.py:31
  169.1 17.4 %collective-permute-start.14 = (bf16[16,16,1024]{2,1,0:T(8,128)(2,1)}, bf16[16,16,1024]{2,1,0:T(8,128)(2,1)}, u32[]{:S(2)}, u32[]{:S(2)}) collective-permute-start(bf16[16,16,1024]{2,1,0:T(8,128)(2,1)} %get-tuple-element.47), channel_id=1, source_target_pairs={{0,64},{64,128},{128,192},{192,0},{1,65},{65,129},{129,193},{193,1... | collective-permute-start | bytes 1572872 | tf_op jit(solution)/shard_map/ppermute | solution.py:21
  170.8 15.6 %collective-permute-start.16 = (bf16[16,16,1024]{2,1,0:T(8,128)(2,1)}, bf16[16,16,1024]{2,1,0:T(8,128)(2,1)}, u32[]{:S(2)}, u32[]{:S(2)}) collective-permute-start(bf16[16,16,1024]{2,1,0:T(8,128)(2,1)} %get-tuple-element.48), channel_id=1, source_target_pairs={{0,192},{64,0},{128,64},{192,128},{1,193},{65,1},{129,65},{193,129... | collective-permute-start | bytes 1572872 | tf_op jit(solution)/shard_map/ppermute | solution.py:21
  172.3 26.4 %collective-permute-start.15 = (bf16[16,16,1024]{2,1,0:T(8,128)(2,1)S(1)}, bf16[16,16,1024]{2,1,0:T(8,128)(2,1)}, u32[]{:S(2)}, u32[]{:S(2)}) collective-permute-start(bf16[16,16,1024]{2,1,0:T(8,128)(2,1)S(1)} %get-tuple-element.49), channel_id=1, source_target_pairs={{0,128},{64,192},{128,0},{192,64},{1,129},{65,193},{129,1},{193,65... | collective-permute-start | bytes 1572872 | tf_op jit(solution)/shard_map/ppermute | solution.py:21
  174.4 32.0 %collective-permute-start.11 = (f32[15,1024]{1,0:T(8,128)S(1)}, f32[15,1024]{1,0:T(8,128)S(1)}, u32[]{:S(2)}, u32[]{:S(2)}) collective-permute-start(f32[15,1024]{1,0:T(8,128)S(1)} %get-tuple-element.50), channel_id=1, source_target_pairs={{4,0},{8,4},{12,8},{16,12},{20,16},{24,20},{28,24},{32,28},{36,32}... | collective-permute-start | bytes 184328 | tf_op jit(solution)/shard_map/ppermute | solution.py:16
  175.7 30.7 %collective-permute-start.12 = (f32[15,1024]{1,0:T(8,128)S(1)}, f32[15,1024]{1,0:T(8,128)S(1)}, u32[]{:S(2)}, u32[]{:S(2)}) collective-permute-start(f32[15,1024]{1,0:T(8,128)S(1)} %get-tuple-element.51), channel_id=1, source_target_pairs={{0,4},{4,8},{8,12},{12,16},{16,20},{20,24},{24,28},{28,32},{32,36}... | collective-permute-start | bytes 184328 | tf_op jit(solution)/shard_map/ppermute | solution.py:16
  179.5 22.0 %all-to-all-start.5 = ((f32[8,8,512]{2,1,0:T(8,128)}), f32[8,8,512]{2,1,0:T(8,128)S(1)}, u32[]{:S(2)}, u32[]{:S(2)}) async-start(f32[8,8,512]{2,1,0:T(8,128)} %broadcast_in_dim.44), calls=%async_computation.5 | async-start | bytes 262144 | tf_op jit(solution)/shard_map/all_to_all | solution.py:31
  184.2 22.2 %copy-start.8 = (f32[1,1024]{1,0:T(1,128)S(1)}, f32[1,1024]{1,0:T(1,128)}, u32[]{:S(2)}) copy-start(f32[1,1024]{1,0:T(1,128)} %copy-done.7) | copy-start | bytes 12292
  201.5 21.8 %all-to-all-start.2 = ((bf16[8,2,16,1024]{3,2,1,0:T(8,128)(2,1)}), bf16[8,2,16,1024]{3,2,1,0:T(8,128)(2,1)S(1)}, u32[]{:S(2)}, u32[]{:S(2)}) async-start(bf16[8,2,16,1024]{3,2,1,0:T(8,128)(2,1)} %copy.37), calls=%async_computation.2 | async-start | bytes 1048576 | tf_op jit(solution)/shard_map/all_to_all | solution.py:31
  206.4 17.6 %copy-start.1 = (bf16[1,256,1024]{2,1,0:T(8,128)(2,1)S(1)}, bf16[1,256,1024]{2,1,0:T(8,128)(2,1)}, u32[]{:S(2)}) copy-start(bf16[1,256,1024]{2,1,0:T(8,128)(2,1)} %param.9) | copy-start | bytes 1572868
  213.1 10.9 %copy-start.5 = (f32[32,1024]{1,0:T(8,128)}, f32[32,1024]{1,0:T(8,128)S(1)}, u32[]{:S(2)}) copy-start(f32[32,1024]{1,0:T(8,128)S(1)} %reshape.126) | copy-start | bytes 393220
  (4 other events, 11.1 us)

commit v3 on v2

--- a/solution.py
+++ b/solution.py
@@ -54,20 +54,17 @@
 def scatter_grads(grads, core, rows):
     ny, nz = lax.axis_size("y"), lax.axis_size("z")
     cells = [g.reshape(ny, nz, 2, rows, g.shape[1]) for g in grads]
-    theirs = jnp.concatenate([pick(c, 1 - core, 2).astype(bf16) for c in cells], axis=1)
+    theirs = jnp.concatenate([pick(c, 1 - core, 2) for c in cells], axis=1)
+    mine = jnp.concatenate([pick(c, core, 2) for c in cells], axis=1)
     came = turn(theirs, "core", 1)
-    mine = jnp.concatenate([pick(c, core, 2) for c in cells], axis=1)
-    chip = (mine + came.astype(f32)).astype(bf16)
+    chip = (mine.astype(f32) + came.astype(f32)).astype(bf16)
     spot = lax.axis_index("y")
     leave = [pick(chip, (spot + by) % ny, 0) for by in range(ny)]
     came = [turn(leave[by], "y", by) for by in range(1, ny)]
     chip = leave[0].astype(f32)
     for part in came:
         chip = chip + part.astype(f32)
-    chip = chip.astype(bf16)
-    chip = chip.reshape((2, nz) + chip.shape[1:]).transpose(1, 0, 2, 3)
-    chip = exchange(chip, "z")
-    return jnp.sum(chip.astype(f32), axis=0)
+    return chip.astype(bf16).reshape((2, nz) + chip.shape[1:]).transpose(1, 0, 2, 3)
 
 
 def silu_grad(values):
@@ -141,7 +138,8 @@
     over_rows = (((0,), (0,)), ((), ()))
     g_out = 0.5 * lax.dot_general(activation, grad_all, over_rows, preferred_element_type=f32)
     g_in = lax.dot_general(scaled_all, up_grad, over_rows, preferred_element_type=f32)
-    grad_weight_in, grad_weight_out = scatter_grads([g_in, g_out], core, rows_in)
+    g_out, g_in = g_out.astype(bf16), g_in.astype(bf16)
+    chip = scatter_grads([g_in, g_out], core, rows_in)
 
     gain_term = jnp.sum(norm_grad * normed, axis=0)
     gain_grad = norm_grad * norm_gain
@@ -170,17 +168,27 @@
     for offset in range(tap_count):
         begin = 2 * half_width - offset
         transposed = transposed + conv_kernel[offset] * grad_wide[begin : begin + length]
-    grad_x = (frame_grad + transposed).astype(bf16)
+    grad_x = (frame_grad + transposed).astype(bf16)[None]
 
     small = jnp.stack(kernel_term + [gain_term])
-    near = ("core", "utt")
-    part = exchange(small.reshape(lax.axis_size(near), 8, -1), near)
+    nz = lax.axis_size("z")
+    rounded = lax.reduce_precision(small, 8, 7)
+    value = rounded.astype(bf16)
+    rest = (small - rounded).astype(bf16)
+    lanes = small.reshape(nz, -1, width).shape[1]
+    load = jnp.concatenate(
+        [chip.reshape(nz, -1, width), value.reshape(nz, -1, width), rest.reshape(nz, -1, width)],
+        axis=1,
+    )
+    load = exchange(load, "z")
+    load = jnp.sum(load.astype(f32), axis=0)
+    grad_weight_in, grad_weight_out = load[:rows_in], load[rows_in : 2 * rows_in]
+    part = load[2 * rows_in : 2 * rows_in + lanes] + load[2 * rows_in + lanes :]
+    part = spread(part.reshape(8, -1), ("y", "core", "utt"))
     part = jnp.sum(part, axis=0)
-    part = spread(part, ("y", "z"))
-    part = jnp.sum(part, axis=0)
-    full = spread(part, near)
+    full = spread(part, "z")
     full = full.reshape(small.shape)
-    return (grad_x[None], grad_weight_in, grad_weight_out, full[:tap_count], full[tap_count])
+    return (grad_x, grad_weight_in, grad_weight_out, full[:tap_count], full[tap_count])
 
 
 def solution(mesh):

time: 226 us -> 237 us (1.049)
  blocking collectives: 0 us -> 23.3 us
  starting transfers between devices: 65.7 us -> 49.6 us
  waiting for transfers between devices: 80.8 us -> 94 us
  other arithmetic: 42.9 us -> 36 us
  local copies, waits for them, and re-layouts: 25.4 us -> 21.9 us
    all_to_all x0 -> x1, blocking collectives: none -> 23.3 us  [exchange(): return lax.all_to_all(cells, axis, 0, 0, tiled=True)]
    all_to_all x6 -> x4, starting transfers between devices: 37.7 us -> 24.2 us  [exchange(): return lax.all_to_all(cells, axis, 0, 0, tiled=True)]
    ppermute x11, waiting for transfers between devices: 41.5 us -> 49.6 us  [turn(): lax.ppermute(cells, axis, [(i, (i + by) % count) for i in range(count)])]
    ppermute x11, starting transfers between devices: 18 us -> 14.5 us  [turn(): lax.ppermute(cells, axis, [(i, (i + by) % count) for i in range(count)])]
    all_to_all x6 -> x4, waiting for transfers between devices: 37.8 us -> 41 us  [exchange(): return lax.all_to_all(cells, axis, 0, 0, tiled=True)]
    all_to_all x2, local copies, waits for them, and re-layouts: 1.57 us -> 4.31 us  [exchange(): return lax.all_to_all(cells, axis, 0, 0, tiled=True)]
    convert_element_type x2 -> x3, other arithmetic: 5.74 us -> 4.51 us  [the longest x1 2.57 us: scatter_grads(): chip = (mine.astype(f32) + came.astype(f32)).astype(bf16)]
  transfers between devices with their start and end apart: 23 -> 21, of which waited for: 13 -> 15; matrix products, arithmetic and copies ran while one was open for 27% -> 17% of each run, Pallas kernels for 0% -> 0%
where the time goes in v3:
time: 237 us; the launch traced here: 234 us
  waiting for transfers between devices  94 us (40%)
  starting transfers between devices  49.6 us (21%)
  other arithmetic  36 us (15%)
  blocking collectives  23.3 us (10%)
  local copies, waits for them, and re-layouts  21.9 us (9%)
  matrix products  6.89 us (3%)
  between operations  2.5 us (1%)
    ppermute x11, waiting for transfers between devices, turn(): lax.ppermute(cells, axis, [(i, (i + by) % count) for i in range(count)])  49.6 us
    all_to_all x4, waiting for transfers between devices, exchange(): return lax.all_to_all(cells, axis, 0, 0, tiled=True)  41 us
    all_to_all x4, starting transfers between devices, exchange(): return lax.all_to_all(cells, axis, 0, 0, tiled=True)  24.2 us
    all_to_all x1, blocking collectives, exchange(): return lax.all_to_all(cells, axis, 0, 0, tiled=True)  23.3 us
    ppermute x11, starting transfers between devices, turn(): lax.ppermute(cells, axis, [(i, (i + by) % count) for i in range(count)])  14.5 us
    ppermute x6, starting transfers between devices, shift(): lax.ppermute(cells, axis, [(i, i + by) for i in range(count) if 0 <= i +...  10.9 us
    broadcast_in_dim x1, other arithmetic, per_device(): grad_x = (frame_grad + transposed).astype(bf16)[None]  7.2 us
    reduce_sum x2, other arithmetic, per_device(): jnp.sum(conv_grad * wide32[offset:offset + length], axis=0)  5.89 us
  transfers between devices with their start and end apart: 21, of which 15 were waited for; matrix products, arithmetic and copies ran while one was open for 17% of the time, Pallas kernels for 0%

profile of v3, /device:TPU:2, one launch (start us, length us, event | category | flops | bytes accessed | tf_op | source)
XLA Modules:
  0.0 234.2 jit_solution(10983112751448217802)
XLA Ops:
  0.7 0.8 slice_bitcast_fusion.7
  1.5 1.3 collective-permute-start.1
  2.8 3.0 %collective-permute-start = (bf16[15,1024]{1,0:T(8,128)(2,1)S(1)}, bf16[15,1024]{1,0:T(8,128)(2,1)S(1)}, u32[]{:S(2)}, u32[]{:S(2)}) collective-permute-start(bf16[15,1024]{1,0:T(8,128)(2,1)S(1)} %get-tuple-element.67), channel_id=1, source_target_pairs={{0,4},{4,8},{8,12},{12,16},{16,20},{20,24},{24,28},{28,32},{32,36}... | collective-permute-start | bytes 92168 | tf_op jit(solution)/shard_map/ppermute | solution.py:16
  5.9 0.8 pad_maximum_fusion.12
  6.6 0.9 broadcast_in_dim.42
  7.5 8.5 %all-to-all-start = ((bf16[8,2,16,1024]{3,2,1,0:T(8,128)(2,1)}), bf16[8,2,16,1024]{3,2,1,0:T(8,128)(2,1)}, u32[]{:S(2)}, u32[]{:S(2)}) async-start(bf16[8,2,16,1024]{3,2,1,0:T(8,128)(2,1)} %broadcast_in_dim.42), calls=%async_computation | async-start | bytes 1048576 | tf_op jit(solution)/shard_map/all_to_all | solution.py:31
  16.0 1.1 fusion.133
  17.1 1.3 fusion.132
  21.3 1.2 gather_fusion.1
  23.0 5.1 %add_convert_fusion.1 = (bf16[256,1024]{1,0:T(8,128)(2,1)S(1)}, f32[256,1024]{1,0:T(8,128)}) fusion(bf16[1,256,1024]{2,1,0:T(8,128)(2,1)S(1)} %copy-done.5, f32[286,1024]{1,0:T(8,128)S(1)} %maximum_convert_fusion, f32[1024]{0:T(1024)S(1)} %bitcast.207, f32[1024]{0:T(1024)S(1)} %bitcast.209, f32[1024]{0:T(1024)S(1)} %bitcast.213, f32[1024]{0:T(1024)S(1)} %bitcast.215, ...), kind=kLoop, calls=%fused_computation.206 | loop fusion | flops 17825792 | bytes 34729984 | tf_op jit(solution)/shard_map/convert_element_type | solution.py:106
  28.1 1.2 gather_fusion
  29.3 5.7 %all-to-all-done = bf16[8,2,16,1024]{3,2,1,0:T(8,128)(2,1)} async-done(((bf16[8,2,16,1024]{3,2,1,0:T(8,128)(2,1)}), bf16[8,2,16,1024]{3,2,1,0:T(8,128)(2,1)}, u32[]{:S(2)}, u32[]{:S(2)}) %all-to-all-start) | async-done | bytes 524320 | tf_op jit(solution)/shard_map/all_to_all | solution.py:31
  34.9 1.1 copy.22
  36.0 1.6 broadcast_in_dim.43
  37.6 4.7 %all-to-all-start.1 = ((bf16[4,8,2,16,1024]{4,3,1,2,0:T(8,128)(2,1)}), bf16[4,8,2,16,1024]{4,3,1,2,0:T(8,128)(2,1)}, u32[]{:S(2)}, u32[]{:S(2)}) async-start(bf16[4,8,2,16,1024]{4,3,1,2,0:T(8,128)(2,1)} %broadcast_in_dim.43), calls=%async_computation.1 | async-start | bytes 4194304 | tf_op jit(solution)/shard_map/all_to_all | solution.py:31
  42.6 1.8 collective-permute-start.2
  44.3 1.5 collective-permute-done.2
  46.0 28.8 %all-to-all-done.1 = bf16[4,8,2,16,1024]{4,3,1,2,0:T(8,128)(2,1)} async-done(((bf16[4,8,2,16,1024]{4,3,1,2,0:T(8,128)(2,1)}), bf16[4,8,2,16,1024]{4,3,1,2,0:T(8,128)(2,1)}, u32[]{:S(2)}, u32[]{:S(2)}) %all-to-all-start.1) | async-done | bytes 2097184 | tf_op jit(solution)/shard_map/all_to_all | solution.py:31
  74.8 3.2 %copy.24 = bf16[4,8,2,16,1024]{4,3,1,0,2:T(8,128)(2,1)} copy(bf16[4,8,2,16,1024]{4,3,1,2,0:T(8,128)(2,1)} %all-to-all-done.1) | data formatting | bytes 4194304 | tf_op jit(solution)/shard_map/all_to_all | solution.py:31
  79.5 2.4 %collective-permute-start.4 = (bf16[2,128,1024]{2,1,0:T(8,128)(2,1)S(1)}, bf16[2,128,1024]{2,1,0:T(8,128)(2,1)S(1)}, u32[]{:S(2)}, u32[]{:S(2)}) collective-permute-start(bf16[2,128,1024]{2,1,0:T(8,128)(2,1)S(1)} %pad_maximum_fusion.7), channel_id=1, source_target_pairs={{0,2},{1,3},{2,0},{3,1},{4,6},{5,7},{6,4},{7,5},{8,10},{9,11},{10,... | collective-permute-start | bytes 1572872 | tf_op jit(solution)/shard_map/ppermute | solution.py:21
  81.9 1.8 collective-permute-start.3
  83.7 0.9 fusion.105
  84.6 8.8 %collective-permute-done.5 = bf16[2,128,1024]{2,1,0:T(8,128)(2,1)} collective-permute-done((bf16[2,128,1024]{2,1,0:T(8,128)(2,1)S(1)}, bf16[2,128,1024]{2,1,0:T(8,128)(2,1)}, u32[]{:S(2)}, u32[]{:S(2)}) %collective-permute-start.5) | collective-permute-done | bytes 524320 | tf_op jit(solution)/shard_map/ppermute | solution.py:21
  93.4 1.1 slice_bitcast_fusion.3
  94.5 11.0 %collective-permute-done.4 = bf16[2,128,1024]{2,1,0:T(8,128)(2,1)S(1)} collective-permute-done((bf16[2,128,1024]{2,1,0:T(8,128)(2,1)S(1)}, bf16[2,128,1024]{2,1,0:T(8,128)(2,1)S(1)}, u32[]{:S(2)}, u32[]{:S(2)}) %collective-permute-start.4) | collective-permute-done | bytes 524320 | tf_op jit(solution)/shard_map/ppermute | solution.py:21
  105.5 0.9 collective-permute-done.3
  106.4 2.5 %select_bitcast_fusion.1 = (bf16[4,8,2,1,16,1024]{5,4,3,1,0,2:T(8,128)(2,1)S(1)}, bf16[4,8,2,1,16,1024]{5,4,3,1,0,2:T(8,128)(2,1)S(1)}) fusion(bf16[4,8,2,16,1024]{4,3,1,0,2:T(8,128)(2,1)} %collective-permute-done.6, pred[]{:T(512)S(6)} %eq.9, bf16[4,8,2,16,1024]{4,3,1,2,0:T(8,128)(2,1)} %all-to-all-done.1), kind=kLoop, calls=%fused_computation.42 | loop fusion | flops 2097152 | bytes 8388609 | tf_op jit(solution)/shard_map/stack | solution.py:49
  109.3 1.3 fusion.120
  110.6 1.3 multiply_convert_fusion
  111.9 1.7 multiply_convert_fusion.2
  113.6 1.3 fusion.134
  114.9 1.3 convolution_convert_fusion
  116.3 1.5 collective-permute-start.9
  117.8 3.3 %collective-permute-start.8 = (bf16[128,1024]{1,0:T(8,128)(2,1)S(1)}, bf16[128,1024]{1,0:T(8,128)(2,1)S(1)}, u32[]{:S(2)}, u32[]{:S(2)}) collective-permute-start(bf16[128,1024]{1,0:T(8,128)(2,1)S(1)} %get-tuple-element.58), channel_id=1, source_target_pairs={{0,2},{1,3},{2,0},{3,1},{4,6},{5,7},{6,4},{7,5},{8,10},{9,11},{10,... | collective-permute-start | bytes 786440 | tf_op jit(solution)/shard_map/ppermute | solution.py:21
  121.8 2.2 dynamic-slice_bitcast_fusion.2
  123.9 1.5 pad_maximum_fusion.1
  125.4 0.8 collective-permute-done.9
  126.2 2.3 collective-permute-done.8
  128.5 4.4 %collective-permute-done.7 = bf16[128,1024]{1,0:T(8,128)(2,1)S(1)} collective-permute-done((bf16[128,1024]{1,0:T(8,128)(2,1)S(1)}, bf16[128,1024]{1,0:T(8,128)(2,1)S(1)}, u32[]{:S(2)}, u32[]{:S(2)}) %collective-permute-start.7) | collective-permute-done | bytes 262176 | tf_op jit(solution)/shard_map/ppermute | solution.py:21
  133.6 1.5 collective-permute-start.10
  135.2 1.9 collective-permute-done.10
  137.1 3.9 %scatter_custom_fusion = f32[256,1024]{1,0:T(8,128)} fusion(s32[256]{0:T(256)} %bitcast.284, bf16[128,1024]{1,0:T(8,128)(2,1)S(1)} %collective-permute-done.10, bf16[]{:T(256)} %constant.122, bf16[128,1024]{1,0:T(8,128)(2,1)S(1)} %broadcast_select_fusion.1, f32[]{:T(128)} %constant.94.clone.1, pred[256]{0:T(512)(128)(4,1)S(1)} %copy-done.51), kind=kCustom, calls=%fused_computation.237 | custom fusion | flops 1572864 | bytes 1574656 | tf_op jit(solution)/shard_map/scatter-add | solution.py:159
  141.0 4.1 %multiply_reduce_fusion = (f32[1024]{0:T(1024)S(1)}, f32[1024]{0:T(1024)S(1)}, f32[1024]{0:T(1024)S(1)}, f32[1024]{0:T(1024)S(1)}, f32[1024]{0:T(1024)S(1)}, /*i...) fusion(f32[286,1024]{1,0:T(8,128)S(1)} %maximum_convert_fusion,, ...), kind=kLoop, calls=%fused_computation.168 | loop fusion | flops 11515904 | bytes 22093824 | tf_op jit(solution)/shard_map/reduce_sum | solution.py:164
  145.2 2.6 %add_convert_fusion = bf16[4,16,16,1024]{3,2,1,0:T(8,128)(2,1)S(1)} fusion(bf16[4,16,16,1024]{3,2,1,0:T(8,128)(2,1)} %collective-permute-done.13, bf16[4,8,16,1024]{3,2,1,0:T(8,128)(2,1)S(1)} %copy-done.3, bf16[4,8,16,1024]{3,2,1,0:T(8,128)(2,1)S(1)} %copy-done.4), kind=kLoop, calls=%fused_computation.33 | loop fusion | flops 5242880 | bytes 6291456 | tf_op jit(solution)/shard_map/convert_element_type | solution.py:60
  147.8 1.3 dynamic-slice_bitcast_fusion.6
  149.1 2.8 %collective-permute-start.15 = (bf16[16,16,1024]{2,1,0:T(8,128)(2,1)}, bf16[16,16,1024]{2,1,0:T(8,128)(2,1)}, u32[]{:S(2)}, u32[]{:S(2)}) collective-permute-start(bf16[16,16,1024]{2,1,0:T(8,128)(2,1)} %get-tuple-element.49), channel_id=1, source_target_pairs={{0,128},{64,192},{128,0},{192,64},{1,129},{65,193},{129,1},{193,65... | collective-permute-start | bytes 1572872 | tf_op jit(solution)/shard_map/ppermute | solution.py:21
  151.9 1.4 collective-permute-start.14
  153.3 1.7 multiply_reduce_fusion.1
  155.4 5.5 %collective-permute-done.16 = bf16[16,16,1024]{2,1,0:T(8,128)(2,1)} collective-permute-done((bf16[16,16,1024]{2,1,0:T(8,128)(2,1)}, bf16[16,16,1024]{2,1,0:T(8,128)(2,1)}, u32[]{:S(2)}, u32[]{:S(2)}) %collective-permute-start.16) | collective-permute-done | bytes 524320 | tf_op jit(solution)/shard_map/ppermute | solution.py:21
  160.9 2.7 %collective-permute-done.15 = bf16[16,16,1024]{2,1,0:T(8,128)(2,1)} collective-permute-done((bf16[16,16,1024]{2,1,0:T(8,128)(2,1)}, bf16[16,16,1024]{2,1,0:T(8,128)(2,1)}, u32[]{:S(2)}, u32[]{:S(2)}) %collective-permute-start.15) | collective-permute-done | bytes 524320 | tf_op jit(solution)/shard_map/ppermute | solution.py:21
  163.6 13.2 %collective-permute-done.14 = bf16[16,16,1024]{2,1,0:T(8,128)(2,1)} collective-permute-done((bf16[16,16,1024]{2,1,0:T(8,128)(2,1)S(1)}, bf16[16,16,1024]{2,1,0:T(8,128)(2,1)}, u32[]{:S(2)}, u32[]{:S(2)}) %collective-permute-start.14) | collective-permute-done | bytes 524320 | tf_op jit(solution)/shard_map/ppermute | solution.py:21
  176.9 1.9 fusion.93
  178.9 23.3 %all_to_all.25 = bf16[8,40,1024]{2,1,0:T(8,128)(2,1)S(1)} all-to-all(bf16[8,40,1024]{2,1,0:T(8,128)(2,1)S(1)} %pad_maximum_fusion.6), channel_id=1, replica_groups=mesh['y'=4,'z'=8,'core'=2,'utt'=4] {'z'}, dimensions={0} | all-to-all | bytes 1310720 | tf_op jit(solution)/shard_map/all_to_all | solution.py:31
  202.4 0.9 broadcast_in_dim.74
  203.2 7.4 %all-to-all-start.3 = ((f32[32,8,512]{2,1,0:T(8,128)}), f32[32,8,512]{2,1,0:T(8,128)S(1)}, u32[]{:S(2)}, u32[]{:S(2)}) async-start(f32[32,8,512]{2,1,0:T(8,128)} %broadcast_in_dim.74), calls=%async_computation.3 | async-start | bytes 1048576 | tf_op jit(solution)/shard_map/all_to_all | solution.py:31
  210.6 0.7 fusion.129
  211.2 2.0 collective-permute-start.12
  213.3 1.3 collective-permute-start.11
  214.6 5.1 %all-to-all-done.3 = f32[32,8,512]{2,1,0:T(8,128)S(1)} async-done(((f32[32,8,512]{2,1,0:T(8,128)}), f32[32,8,512]{2,1,0:T(8,128)S(1)}, u32[]{:S(2)}, u32[]{:S(2)}) %all-to-all-start.3) | async-done | bytes 524320 | tf_op jit(solution)/shard_map/all_to_all | solution.py:31
  219.8 0.7 broadcast_in_dim.75
  220.4 3.6 %all-to-all-start.4 = ((f32[8,8,512]{2,1,0:T(8,128)}), f32[8,8,512]{2,1,0:T(8,128)S(1)}, u32[]{:S(2)}, u32[]{:S(2)}) async-start(f32[8,8,512]{2,1,0:T(8,128)} %broadcast_in_dim.75), calls=%async_computation.4 | async-start | bytes 262144 | tf_op jit(solution)/shard_map/all_to_all | solution.py:31
  224.2 7.2 %fusion.119 = bf16[1,256,1024]{2,1,0:T(8,128)(2,1)} fusion(f32[256,1024]{1,0:T(8,128)S(1)} %copy-done.1, f32[256,1024]{1,0:T(8,128)S(1)} %get-tuple-element.39, f32[15,1024]{1,0:T(8,128)S(1)} %collective-permute-done.12, f32[1024]{0:T(1024)S(1)} %bitcast.208, f32[1024]{0:T(1024)S(1)} %bitcast.210, f32[1024]{0:T(1024)} %bitcast.214, f32[1024]{0:T(1024)} %bitcast.216, ...), kind=kLoop, calls=%fused_computation.245 | loop fusion | flops 24379392 | bytes 2871296 | tf_op jit(solution)/shard_map/broadcast_in_dim | solution.py:171
  231.4 0.7 fusion.131
  232.0 1.4 all-to-all-done.4
  (154 shorter events, 7.2 us)
Async XLA Ops:
  0.6 20.6 %copy-start = (bf16[1,256,1024]{2,1,0:T(8,128)(2,1)S(1)}, bf16[1,256,1024]{2,1,0:T(8,128)(2,1)}, u32[]{:S(2)}) copy-start(bf16[1,256,1024]{2,1,0:T(8,128)(2,1)} %param.9) | copy-start | bytes 1572868
  0.6 18.0 %copy-start.52 = (s32[1,256]{1,0:T(1,128)S(1)}, s32[1,256]{1,0:T(1,128)}, u32[]{:S(2)}) copy-start(s32[1,256]{1,0:T(1,128)} %param.15) | copy-start | bytes 3076
  0.7 18.1 %copy-start.53 = (s32[1,64]{1,0:T(1,128)S(1)}, s32[1,64]{1,0:T(1,128)}, u32[]{:S(2)}) copy-start(s32[1,64]{1,0:T(1,128)} %param.14) | copy-start | bytes 772
  1.5 21.0 %collective-permute-start.1 = (bf16[15,1024]{1,0:T(8,128)(2,1)S(1)}, bf16[15,1024]{1,0:T(8,128)(2,1)S(1)}, u32[]{:S(2)}, u32[]{:S(2)}) collective-permute-start(bf16[15,1024]{1,0:T(8,128)(2,1)S(1)} %get-tuple-element.68), channel_id=1, source_target_pairs={{4,0},{8,4},{12,8},{16,12},{20,16},{24,20},{28,24},{32,28},{36,32}... | collective-permute-start | bytes 92168 | tf_op jit(solution)/shard_map/ppermute | solution.py:16
  2.8 19.7 %collective-permute-start = (bf16[15,1024]{1,0:T(8,128)(2,1)S(1)}, bf16[15,1024]{1,0:T(8,128)(2,1)S(1)}, u32[]{:S(2)}, u32[]{:S(2)}) collective-permute-start(bf16[15,1024]{1,0:T(8,128)(2,1)S(1)} %get-tuple-element.67), channel_id=1, source_target_pairs={{0,4},{4,8},{8,12},{12,16},{16,20},{20,24},{24,28},{28,32},{32,36}... | collective-permute-start | bytes 92168 | tf_op jit(solution)/shard_map/ppermute | solution.py:16
  7.5 27.4 %all-to-all-start = ((bf16[8,2,16,1024]{3,2,1,0:T(8,128)(2,1)}), bf16[8,2,16,1024]{3,2,1,0:T(8,128)(2,1)}, u32[]{:S(2)}, u32[]{:S(2)}) async-start(bf16[8,2,16,1024]{3,2,1,0:T(8,128)(2,1)} %broadcast_in_dim.42), calls=%async_computation | async-start | bytes 1048576 | tf_op jit(solution)/shard_map/all_to_all | solution.py:31
  17.0 5.6 %copy-start.8 = (f32[1,1024]{1,0:T(1,128)}, f32[1,1024]{1,0:T(1,128)S(1)}, u32[]{:S(2)}) copy-start(f32[1,1024]{1,0:T(1,128)S(1)} %get-tuple-element.95) | copy-start | bytes 12292
  17.1 5.6 %copy-start.10 = (f32[1,1024]{1,0:T(1,128)}, f32[1,1024]{1,0:T(1,128)S(1)}, u32[]{:S(2)}) copy-start(f32[1,1024]{1,0:T(1,128)S(1)} %get-tuple-element.96) | copy-start | bytes 12292
  17.1 5.6 %copy-start.12 = (f32[1,1024]{1,0:T(1,128)}, f32[1,1024]{1,0:T(1,128)S(1)}, u32[]{:S(2)}) copy-start(f32[1,1024]{1,0:T(1,128)S(1)} %get-tuple-element.97) | copy-start | bytes 12292
  17.1 5.6 %copy-start.14 = (f32[1,1024]{1,0:T(1,128)}, f32[1,1024]{1,0:T(1,128)S(1)}, u32[]{:S(2)}) copy-start(f32[1,1024]{1,0:T(1,128)S(1)} %get-tuple-element.98) | copy-start | bytes 12292
  17.1 5.6 %copy-start.16 = (f32[1,1024]{1,0:T(1,128)}, f32[1,1024]{1,0:T(1,128)S(1)}, u32[]{:S(2)}) copy-start(f32[1,1024]{1,0:T(1,128)S(1)} %get-tuple-element.99) | copy-start | bytes 12292
  17.1 5.6 %copy-start.18 = (f32[1,1024]{1,0:T(1,128)}, f32[1,1024]{1,0:T(1,128)S(1)}, u32[]{:S(2)}) copy-start(f32[1,1024]{1,0:T(1,128)S(1)} %get-tuple-element.100) | copy-start | bytes 12292
  17.1 5.6 %copy-start.20 = (f32[1,1024]{1,0:T(1,128)}, f32[1,1024]{1,0:T(1,128)S(1)}, u32[]{:S(2)}) copy-start(f32[1,1024]{1,0:T(1,128)S(1)} %get-tuple-element.101) | copy-start | bytes 12292
  17.1 5.6 %copy-start.22 = (f32[1,1024]{1,0:T(1,128)}, f32[1,1024]{1,0:T(1,128)S(1)}, u32[]{:S(2)}) copy-start(f32[1,1024]{1,0:T(1,128)S(1)} %get-tuple-element.102) | copy-start | bytes 12292
  17.1 5.6 %copy-start.24 = (f32[1,1024]{1,0:T(1,128)}, f32[1,1024]{1,0:T(1,128)S(1)}, u32[]{:S(2)}) copy-start(f32[1,1024]{1,0:T(1,128)S(1)} %get-tuple-element.103) | copy-start | bytes 12292
  18.5 4.3 %copy-start.26 = (f32[1,1024]{1,0:T(1,128)}, f32[1,1024]{1,0:T(1,128)S(1)}, u32[]{:S(2)}) copy-start(f32[1,1024]{1,0:T(1,128)S(1)} %get-tuple-element.73) | copy-start | bytes 12292
  18.5 4.3 %copy-start.27 = (f32[1,1024]{1,0:T(1,128)}, f32[1,1024]{1,0:T(1,128)S(1)}, u32[]{:S(2)}) copy-start(f32[1,1024]{1,0:T(1,128)S(1)} %get-tuple-element.74) | copy-start | bytes 12292
  18.5 4.3 %copy-start.28 = (f32[1,1024]{1,0:T(1,128)}, f32[1,1024]{1,0:T(1,128)S(1)}, u32[]{:S(2)}) copy-start(f32[1,1024]{1,0:T(1,128)S(1)} %get-tuple-element.75) | copy-start | bytes 12292
  18.5 4.3 %copy-start.29 = (f32[1,1024]{1,0:T(1,128)}, f32[1,1024]{1,0:T(1,128)S(1)}, u32[]{:S(2)}) copy-start(f32[1,1024]{1,0:T(1,128)S(1)} %get-tuple-element.76) | copy-start | bytes 12292
  18.5 4.3 %copy-start.30 = (f32[1,1024]{1,0:T(1,128)}, f32[1,1024]{1,0:T(1,128)S(1)}, u32[]{:S(2)}) copy-start(f32[1,1024]{1,0:T(1,128)S(1)} %get-tuple-element.77) | copy-start | bytes 12292
  18.5 4.3 %copy-start.31 = (f32[1,1024]{1,0:T(1,128)}, f32[1,1024]{1,0:T(1,128)S(1)}, u32[]{:S(2)}) copy-start(f32[1,1024]{1,0:T(1,128)S(1)} %get-tuple-element.78) | copy-start | bytes 12292
  18.5 4.3 %copy-start.32 = (f32[1,1024]{1,0:T(1,128)}, f32[1,1024]{1,0:T(1,128)S(1)}, u32[]{:S(2)}) copy-start(f32[1,1024]{1,0:T(1,128)S(1)} %get-tuple-element.79) | copy-start | bytes 12292
  18.5 4.3 %copy-start.33 = (f32[1,1024]{1,0:T(1,128)}, f32[1,1024]{1,0:T(1,128)S(1)}, u32[]{:S(2)}) copy-start(f32[1,1024]{1,0:T(1,128)S(1)} %get-tuple-element.80) | copy-start | bytes 12292
  18.6 4.3 %copy-start.34 = (f32[1,1024]{1,0:T(1,128)}, f32[1,1024]{1,0:T(1,128)S(1)}, u32[]{:S(2)}) copy-start(f32[1,1024]{1,0:T(1,128)S(1)} %get-tuple-element.81) | copy-start | bytes 12292
  18.6 4.3 %copy-start.35 = (f32[1,1024]{1,0:T(1,128)}, f32[1,1024]{1,0:T(1,128)S(1)}, u32[]{:S(2)}) copy-start(f32[1,1024]{1,0:T(1,128)S(1)} %get-tuple-element.82) | copy-start | bytes 12292
  18.6 4.3 %copy-start.36 = (f32[1,1024]{1,0:T(1,128)}, f32[1,1024]{1,0:T(1,128)S(1)}, u32[]{:S(2)}) copy-start(f32[1,1024]{1,0:T(1,128)S(1)} %get-tuple-element.83) | copy-start | bytes 12292
  18.6 4.3 %copy-start.37 = (f32[1,1024]{1,0:T(1,128)}, f32[1,1024]{1,0:T(1,128)S(1)}, u32[]{:S(2)}) copy-start(f32[1,1024]{1,0:T(1,128)S(1)} %get-tuple-element.84) | copy-start | bytes 12292
  18.6 4.3 %copy-start.38 = (f32[1,1024]{1,0:T(1,128)}, f32[1,1024]{1,0:T(1,128)S(1)}, u32[]{:S(2)}) copy-start(f32[1,1024]{1,0:T(1,128)S(1)} %get-tuple-element.85) | copy-start | bytes 12292
  18.6 4.3 %copy-start.39 = (f32[1,1024]{1,0:T(1,128)}, f32[1,1024]{1,0:T(1,128)S(1)}, u32[]{:S(2)}) copy-start(f32[1,1024]{1,0:T(1,128)S(1)} %get-tuple-element.86) | copy-start | bytes 12292
  18.6 4.3 %copy-start.40 = (f32[1,1024]{1,0:T(1,128)}, f32[1,1024]{1,0:T(1,128)S(1)}, u32[]{:S(2)}) copy-start(f32[1,1024]{1,0:T(1,128)S(1)} %get-tuple-element.87) | copy-start | bytes 12292
  20.6 21.7 %copy-start.50 = (pred[256]{0:T(512)(128)(4,1)}, pred[256]{0:T(512)(128)(4,1)S(1)}, u32[]{:S(2)}) copy-start(pred[256]{0:T(512)(128)(4,1)S(1)} %iota_compare_fusion) | copy-start | bytes 772
  37.6 37.3 %all-to-all-start.1 = ((bf16[4,8,2,16,1024]{4,3,1,2,0:T(8,128)(2,1)}), bf16[4,8,2,16,1024]{4,3,1,2,0:T(8,128)(2,1)}, u32[]{:S(2)}, u32[]{:S(2)}) async-start(bf16[4,8,2,16,1024]{4,3,1,2,0:T(8,128)(2,1)} %broadcast_in_dim.43), calls=%async_computation.1 | async-start | bytes 4194304 | tf_op jit(solution)/shard_map/all_to_all | solution.py:31
  42.6 3.3 %collective-permute-start.2 = (bf16[2,128,1024]{2,1,0:T(8,128)(2,1)S(1)}, bf16[2,128,1024]{2,1,0:T(8,128)(2,1)S(1)}, u32[]{:S(2)}, u32[]{:S(2)}) collective-permute-start(bf16[2,128,1024]{2,1,0:T(8,128)(2,1)S(1)} %slice_select_fusion), channel_id=1, source_target_pairs={{0,4},{4,8},{8,12},{12,16},{16,20},{20,24},{24,28},{28,32},{32,36}... | collective-permute-start | bytes 1572872 | tf_op jit(solution)/shard_map/ppermute | solution.py:16
  46.0 32.3 %copy-start.45 = (f32[128]{0:T(128)}, f32[128]{0:T(128)S(1)}, u32[]{:S(2)}) copy-start(f32[128]{0:T(128)S(1)} %broadcast_multiply_fusion.2) | copy-start | bytes 1540
  46.0 32.3 %copy-start.7 = (f32[1024]{0:T(1024)S(1)}, f32[1024]{0:T(1024)}, u32[]{:S(2)}) copy-start(f32[1024]{0:T(1024)} %param.11) | copy-start | bytes 12292
  78.1 28.3 %collective-permute-start.6 = (bf16[4,8,2,16,1024]{4,3,1,0,2:T(8,128)(2,1)}, bf16[4,8,2,16,1024]{4,3,1,0,2:T(8,128)(2,1)}, u32[]{:S(2)}, u32[]{:S(2)}) collective-permute-start(bf16[4,8,2,16,1024]{4,3,1,0,2:T(8,128)(2,1)} %copy.24), channel_id=1, source_target_pairs={{0,4},{4,0},{1,5},{5,1},{2,6},{6,2},{3,7},{7,3},{8,12},{12,8},{9,1... | collective-permute-start | bytes 6291464 | tf_op jit(solution)/shard_map/ppermute | solution.py:21
  78.9 14.5 %collective-permute-start.5 = (bf16[2,128,1024]{2,1,0:T(8,128)(2,1)S(1)}, bf16[2,128,1024]{2,1,0:T(8,128)(2,1)}, u32[]{:S(2)}, u32[]{:S(2)}) collective-permute-start(bf16[2,128,1024]{2,1,0:T(8,128)(2,1)S(1)} %pad_maximum_fusion.7), channel_id=1, source_target_pairs={{0,3},{1,0},{2,1},{3,2},{4,7},{5,4},{6,5},{7,6},{8,11},{9,8},{10,9... | collective-permute-start | bytes 1572872 | tf_op jit(solution)/shard_map/ppermute | solution.py:21
  79.5 26.0 %collective-permute-start.4 = (bf16[2,128,1024]{2,1,0:T(8,128)(2,1)S(1)}, bf16[2,128,1024]{2,1,0:T(8,128)(2,1)S(1)}, u32[]{:S(2)}, u32[]{:S(2)}) collective-permute-start(bf16[2,128,1024]{2,1,0:T(8,128)(2,1)S(1)} %pad_maximum_fusion.7), channel_id=1, source_target_pairs={{0,2},{1,3},{2,0},{3,1},{4,6},{5,7},{6,4},{7,5},{8,10},{9,11},{10,... | collective-permute-start | bytes 1572872 | tf_op jit(solution)/shard_map/ppermute | solution.py:21
  81.9 24.4 %collective-permute-start.3 = (bf16[2,128,1024]{2,1,0:T(8,128)(2,1)S(1)}, bf16[2,128,1024]{2,1,0:T(8,128)(2,1)S(1)}, u32[]{:S(2)}, u32[]{:S(2)}) collective-permute-start(bf16[2,128,1024]{2,1,0:T(8,128)(2,1)S(1)} %pad_maximum_fusion.7), channel_id=1, source_target_pairs={{0,1},{1,2},{2,3},{3,0},{4,5},{5,6},{6,7},{7,4},{8,9},{9,10},{10,1... | collective-permute-start | bytes 1572872 | tf_op jit(solution)/shard_map/ppermute | solution.py:21
  116.3 9.9 %collective-permute-start.9 = (bf16[128,1024]{1,0:T(8,128)(2,1)S(1)}, bf16[128,1024]{1,0:T(8,128)(2,1)S(1)}, u32[]{:S(2)}, u32[]{:S(2)}) collective-permute-start(bf16[128,1024]{1,0:T(8,128)(2,1)S(1)} %get-tuple-element.57), channel_id=1, source_target_pairs={{0,1},{1,2},{2,3},{3,0},{4,5},{5,6},{6,7},{7,4},{8,9},{9,10},{10,1... | collective-permute-start | bytes 786440 | tf_op jit(solution)/shard_map/ppermute | solution.py:21
  117.8 10.7 %collective-permute-start.8 = (bf16[128,1024]{1,0:T(8,128)(2,1)S(1)}, bf16[128,1024]{1,0:T(8,128)(2,1)S(1)}, u32[]{:S(2)}, u32[]{:S(2)}) collective-permute-start(bf16[128,1024]{1,0:T(8,128)(2,1)S(1)} %get-tuple-element.58), channel_id=1, source_target_pairs={{0,2},{1,3},{2,0},{3,1},{4,6},{5,7},{6,4},{7,5},{8,10},{9,11},{10,... | collective-permute-start | bytes 786440 | tf_op jit(solution)/shard_map/ppermute | solution.py:21
  121.1 11.8 %collective-permute-start.7 = (bf16[128,1024]{1,0:T(8,128)(2,1)S(1)}, bf16[128,1024]{1,0:T(8,128)(2,1)S(1)}, u32[]{:S(2)}, u32[]{:S(2)}) collective-permute-start(bf16[128,1024]{1,0:T(8,128)(2,1)S(1)} %get-tuple-element.56), channel_id=1, source_target_pairs={{0,3},{1,0},{2,1},{3,2},{4,7},{5,4},{6,5},{7,6},{8,11},{9,8},{10,9... | collective-permute-start | bytes 786440 | tf_op jit(solution)/shard_map/ppermute | solution.py:21
  123.9 9.0 %copy-start.46 = (f32[128]{0:T(128)S(1)}, f32[128]{0:T(128)}, u32[]{:S(2)}) copy-start(f32[128]{0:T(128)} %copy-done.45) | copy-start | bytes 1540
  123.9 9.0 %copy-start.48 = (f32[128]{0:T(128)S(1)}, f32[128]{0:T(128)}, u32[]{:S(2)}) copy-start(f32[128]{0:T(128)} %copy-done.47) | copy-start | bytes 1540
  125.4 19.7 %collective-permute-start.13 = (bf16[4,16,16,1024]{3,2,1,0:T(8,128)(2,1)}, bf16[4,16,16,1024]{3,2,1,0:T(8,128)(2,1)}, u32[]{:S(2)}, u32[]{:S(2)}) collective-permute-start(bf16[4,16,16,1024]{3,2,1,0:T(8,128)(2,1)} %pad_maximum_fusion.1), channel_id=1, source_target_pairs={{0,4},{4,0},{1,5},{5,1},{2,6},{6,2},{3,7},{7,3},{8,12},{12,8},{9,1... | collective-permute-start | bytes 6291464 | tf_op jit(solution)/shard_map/ppermute | solution.py:21
  133.6 3.4 %collective-permute-start.10 = (bf16[128,1024]{1,0:T(8,128)(2,1)S(1)}, bf16[128,1024]{1,0:T(8,128)(2,1)S(1)}, u32[]{:S(2)}, u32[]{:S(2)}) collective-permute-start(bf16[128,1024]{1,0:T(8,128)(2,1)S(1)} %fusion.110), channel_id=1, source_target_pairs={{4,0},{8,4},{12,8},{16,12},{20,16},{24,20},{28,24},{32,28},{36,32}... | collective-permute-start | bytes 786440 | tf_op jit(solution)/shard_map/ppermute | solution.py:16
  147.8 7.3 %copy-start.2 = (bf16[4,16,16,1024]{3,2,1,0:T(8,128)(2,1)}, bf16[4,16,16,1024]{3,2,1,0:T(8,128)(2,1)S(1)}, u32[]{:S(2)}) copy-start(bf16[4,16,16,1024]{3,2,1,0:T(8,128)(2,1)S(1)} %add_convert_fusion) | copy-start | bytes 6291460
  149.1 11.8 %collective-permute-start.16 = (bf16[16,16,1024]{2,1,0:T(8,128)(2,1)}, bf16[16,16,1024]{2,1,0:T(8,128)(2,1)}, u32[]{:S(2)}, u32[]{:S(2)}) collective-permute-start(bf16[16,16,1024]{2,1,0:T(8,128)(2,1)} %get-tuple-element.48), channel_id=1, source_target_pairs={{0,192},{64,0},{128,64},{192,128},{1,193},{65,1},{129,65},{193,129... | collective-permute-start | bytes 1572872 | tf_op jit(solution)/shard_map/ppermute | solution.py:21
  149.1 14.5 %collective-permute-start.15 = (bf16[16,16,1024]{2,1,0:T(8,128)(2,1)}, bf16[16,16,1024]{2,1,0:T(8,128)(2,1)}, u32[]{:S(2)}, u32[]{:S(2)}) collective-permute-start(bf16[16,16,1024]{2,1,0:T(8,128)(2,1)} %get-tuple-element.49), channel_id=1, source_target_pairs={{0,128},{64,192},{128,0},{192,64},{1,129},{65,193},{129,1},{193,65... | collective-permute-start | bytes 1572872 | tf_op jit(solution)/shard_map/ppermute | solution.py:21
  151.9 24.9 %collective-permute-start.14 = (bf16[16,16,1024]{2,1,0:T(8,128)(2,1)S(1)}, bf16[16,16,1024]{2,1,0:T(8,128)(2,1)}, u32[]{:S(2)}, u32[]{:S(2)}) collective-permute-start(bf16[16,16,1024]{2,1,0:T(8,128)(2,1)S(1)} %get-tuple-element.47), channel_id=1, source_target_pairs={{0,64},{64,128},{128,192},{192,0},{1,65},{65,129},{129,193},{193,1... | collective-permute-start | bytes 1572872 | tf_op jit(solution)/shard_map/ppermute | solution.py:21
  202.2 21.9 %copy-start.1 = (f32[256,1024]{1,0:T(8,128)S(1)}, f32[256,1024]{1,0:T(8,128)}, u32[]{:S(2)}) copy-start(f32[256,1024]{1,0:T(8,128)} %scatter_custom_fusion) | copy-start | bytes 3145732
  202.2 21.9 %copy-start.9 = (f32[1,1024]{1,0:T(1,128)S(1)}, f32[1,1024]{1,0:T(1,128)}, u32[]{:S(2)}) copy-start(f32[1,1024]{1,0:T(1,128)} %copy-done.8) | copy-start | bytes 12292
  202.2 21.9 %copy-start.11 = (f32[1,1024]{1,0:T(1,128)S(1)}, f32[1,1024]{1,0:T(1,128)}, u32[]{:S(2)}) copy-start(f32[1,1024]{1,0:T(1,128)} %copy-done.10) | copy-start | bytes 12292
  202.2 21.9 %copy-start.13 = (f32[1,1024]{1,0:T(1,128)S(1)}, f32[1,1024]{1,0:T(1,128)}, u32[]{:S(2)}) copy-start(f32[1,1024]{1,0:T(1,128)} %copy-done.12) | copy-start | bytes 12292
  202.2 21.9 %copy-start.15 = (f32[1,1024]{1,0:T(1,128)S(1)}, f32[1,1024]{1,0:T(1,128)}, u32[]{:S(2)}) copy-start(f32[1,1024]{1,0:T(1,128)} %copy-done.14) | copy-start | bytes 12292
  202.2 21.9 %copy-start.17 = (f32[1,1024]{1,0:T(1,128)S(1)}, f32[1,1024]{1,0:T(1,128)}, u32[]{:S(2)}) copy-start(f32[1,1024]{1,0:T(1,128)} %copy-done.16) | copy-start | bytes 12292
  202.2 21.9 %copy-start.19 = (f32[1,1024]{1,0:T(1,128)S(1)}, f32[1,1024]{1,0:T(1,128)}, u32[]{:S(2)}) copy-start(f32[1,1024]{1,0:T(1,128)} %copy-done.18) | copy-start | bytes 12292
  202.2 21.9 %copy-start.21 = (f32[1,1024]{1,0:T(1,128)S(1)}, f32[1,1024]{1,0:T(1,128)}, u32[]{:S(2)}) copy-start(f32[1,1024]{1,0:T(1,128)} %copy-done.20) | copy-start | bytes 12292
  202.2 21.9 %copy-start.23 = (f32[1,1024]{1,0:T(1,128)S(1)}, f32[1,1024]{1,0:T(1,128)}, u32[]{:S(2)}) copy-start(f32[1,1024]{1,0:T(1,128)} %copy-done.22) | copy-start | bytes 12292
  202.2 21.9 %copy-start.25 = (f32[1,1024]{1,0:T(1,128)S(1)}, f32[1,1024]{1,0:T(1,128)}, u32[]{:S(2)}) copy-start(f32[1,1024]{1,0:T(1,128)} %copy-done.24) | copy-start | bytes 12292
  203.2 16.5 %all-to-all-start.3 = ((f32[32,8,512]{2,1,0:T(8,128)}), f32[32,8,512]{2,1,0:T(8,128)S(1)}, u32[]{:S(2)}, u32[]{:S(2)}) async-start(f32[32,8,512]{2,1,0:T(8,128)} %broadcast_in_dim.74), calls=%async_computation.3 | async-start | bytes 1048576 | tf_op jit(solution)/shard_map/all_to_all | solution.py:31
  211.2 12.8 %collective-permute-start.12 = (f32[15,1024]{1,0:T(8,128)}, f32[15,1024]{1,0:T(8,128)S(1)}, u32[]{:S(2)}, u32[]{:S(2)}) collective-permute-start(f32[15,1024]{1,0:T(8,128)} %get-tuple-element.55), channel_id=1, source_target_pairs={{0,4},{4,8},{8,12},{12,16},{16,20},{20,24},{24,28},{28,32},{32,36}... | collective-permute-start | bytes 184328 | tf_op jit(solution)/shard_map/ppermute | solution.py:16
  213.3 10.8 %collective-permute-start.11 = (f32[15,1024]{1,0:T(8,128)}, f32[15,1024]{1,0:T(8,128)}, u32[]{:S(2)}, u32[]{:S(2)}) collective-permute-start(f32[15,1024]{1,0:T(8,128)} %get-tuple-element.54), channel_id=1, source_target_pairs={{4,0},{8,4},{12,8},{16,12},{20,16},{24,20},{28,24},{32,28},{36,32}... | collective-permute-start | bytes 184328 | tf_op jit(solution)/shard_map/ppermute | solution.py:16
  220.4 13.0 %all-to-all-start.4 = ((f32[8,8,512]{2,1,0:T(8,128)}), f32[8,8,512]{2,1,0:T(8,128)S(1)}, u32[]{:S(2)}, u32[]{:S(2)}) async-start(f32[8,8,512]{2,1,0:T(8,128)} %broadcast_in_dim.75), calls=%async_computation.4 | async-start | bytes 262144 | tf_op jit(solution)/shard_map/all_to_all | solution.py:31
  (11 other events, 35.8 us)

commit v4 on v2

--- a/solution.py
+++ b/solution.py
@@ -43,31 +43,31 @@
 def gather_weights(pair, core):
     half = spread(pair, "z")
     half = spread(half, "y")
+    half = with_layout_constraint(half, Layout(major_to_minor=(0, 1, 2, 3, 4)))
     other = turn(half, "core", 1)
-    first = jnp.where(core == 0, half, other)
-    second = jnp.where(core == 0, other, half)
-    both = jnp.stack([first, second], axis=3)
     width = pair.shape[-1]
-    return [both[:, :, i].reshape(-1, width) for i in range(2)]
+    whole = []
+    for i in range(2):
+        ours, came = half[:, :, i], other[:, :, i]
+        both = [jnp.where(core == 0, ours, came), jnp.where(core == 0, came, ours)]
+        whole.append(jnp.stack(both, axis=2).reshape(-1, width))
+    return whole
 
 
 def scatter_grads(grads, core, rows):
     ny, nz = lax.axis_size("y"), lax.axis_size("z")
     cells = [g.reshape(ny, nz, 2, rows, g.shape[1]) for g in grads]
-    theirs = jnp.concatenate([pick(c, 1 - core, 2).astype(bf16) for c in cells], axis=1)
+    theirs = jnp.concatenate([pick(c, 1 - core, 2) for c in cells], axis=1)
+    mine = jnp.concatenate([pick(c, core, 2) for c in cells], axis=1)
     came = turn(theirs, "core", 1)
-    mine = jnp.concatenate([pick(c, core, 2) for c in cells], axis=1)
-    chip = (mine + came.astype(f32)).astype(bf16)
+    chip = (mine.astype(f32) + came.astype(f32)).astype(bf16)
     spot = lax.axis_index("y")
     leave = [pick(chip, (spot + by) % ny, 0) for by in range(ny)]
     came = [turn(leave[by], "y", by) for by in range(1, ny)]
     chip = leave[0].astype(f32)
     for part in came:
         chip = chip + part.astype(f32)
-    chip = chip.astype(bf16)
-    chip = chip.reshape((2, nz) + chip.shape[1:]).transpose(1, 0, 2, 3)
-    chip = exchange(chip, "z")
-    return jnp.sum(chip.astype(f32), axis=0)
+    return chip.astype(bf16).reshape((2, nz) + chip.shape[1:]).transpose(1, 0, 2, 3)
 
 
 def silu_grad(values):
@@ -141,7 +141,8 @@
     over_rows = (((0,), (0,)), ((), ()))
     g_out = 0.5 * lax.dot_general(activation, grad_all, over_rows, preferred_element_type=f32)
     g_in = lax.dot_general(scaled_all, up_grad, over_rows, preferred_element_type=f32)
-    grad_weight_in, grad_weight_out = scatter_grads([g_in, g_out], core, rows_in)
+    g_out, g_in = g_out.astype(bf16), g_in.astype(bf16)
+    chip = scatter_grads([g_in, g_out], core, rows_in)
 
     gain_term = jnp.sum(norm_grad * normed, axis=0)
     gain_grad = norm_grad * norm_gain
@@ -170,7 +171,7 @@
     for offset in range(tap_count):
         begin = 2 * half_width - offset
         transposed = transposed + conv_kernel[offset] * grad_wide[begin : begin + length]
-    grad_x = (frame_grad + transposed).astype(bf16)
+    grad_x = (frame_grad + transposed).astype(bf16)[None]
 
     small = jnp.stack(kernel_term + [gain_term])
     near = ("core", "utt")
@@ -180,7 +181,9 @@
     part = jnp.sum(part, axis=0)
     full = spread(part, near)
     full = full.reshape(small.shape)
-    return (grad_x[None], grad_weight_in, grad_weight_out, full[:tap_count], full[tap_count])
+    load = exchange(chip, "z")
+    grad_weight_in, grad_weight_out = jnp.sum(load.astype(f32), axis=0)
+    return (grad_x, grad_weight_in, grad_weight_out, full[:tap_count], full[tap_count])
 
 
 def solution(mesh):

time: 226 us -> 228 us (level)
  waiting for transfers between devices: 80.8 us -> 94.9 us
  starting transfers between devices: 65.7 us -> 53.2 us
  blocking collectives: 0 us -> 11.8 us
  other arithmetic: 42.9 us -> 35.5 us
  local copies, waits for them, and re-layouts: 25.4 us -> 20.2 us
    all_to_all x0 -> x1, blocking collectives: none -> 11.8 us  [exchange(): return lax.all_to_all(cells, axis, 0, 0, tiled=True)]
    all_to_all x6 -> x5, waiting for transfers between devices: 37.8 us -> 49.3 us  [exchange(): return lax.all_to_all(cells, axis, 0, 0, tiled=True)]
    all_to_all x6 -> x5, starting transfers between devices: 37.7 us -> 27.1 us  [exchange(): return lax.all_to_all(cells, axis, 0, 0, tiled=True)]
    ppermute x11, waiting for transfers between devices: 41.5 us -> 44.1 us  [turn(): lax.ppermute(cells, axis, [(i, (i + by) % count) for i in range(count)])]
    select_n x0 -> x1, other arithmetic: none -> 2.47 us  [gather_weights(): both = [jnp.where(core == 0, ours, came), jnp.where(core == 0, came, ours)]]
    squeeze x2 -> x3, local copies, waits for them, and re-layouts: 5.08 us -> 3.6 us  [pick(): return lax.dynamic_index_in_dim(cells, which, axis, keepdims=False)]
  transfers between devices with their start and end apart: 23 -> 22, of which waited for: 13 -> 13; matrix products, arithmetic and copies ran while one was open for 27% -> 21% of each run, Pallas kernels for 0% -> 0%
where the time goes in v4:
time: 228 us; the launch traced here: 225 us
  waiting for transfers between devices  94.9 us (42%)
  starting transfers between devices  53.2 us (23%)
  other arithmetic  35.5 us (16%)
  local copies, waits for them, and re-layouts  20.2 us (9%)
  blocking collectives  11.8 us (5%)
  matrix products  6.94 us (3%)
  between operations  2.31 us (1%)
    all_to_all x5, waiting for transfers between devices, exchange(): return lax.all_to_all(cells, axis, 0, 0, tiled=True)  49.3 us
    ppermute x11, waiting for transfers between devices, turn(): lax.ppermute(cells, axis, [(i, (i + by) % count) for i in range(count)])  44.1 us
    all_to_all x5, starting transfers between devices, exchange(): return lax.all_to_all(cells, axis, 0, 0, tiled=True)  27.1 us
    ppermute x11, starting transfers between devices, turn(): lax.ppermute(cells, axis, [(i, (i + by) % count) for i in range(count)])  16.1 us
    all_to_all x1, blocking collectives, exchange(): return lax.all_to_all(cells, axis, 0, 0, tiled=True)  11.8 us
    ppermute x6, starting transfers between devices, shift(): lax.ppermute(cells, axis, [(i, i + by) for i in range(count) if 0 <= i +...  9.97 us
    broadcast_in_dim x1, other arithmetic, per_device(): grad_x = (frame_grad + transposed).astype(bf16)[None]  6.59 us
    reduce_sum x2, other arithmetic, per_device(): jnp.sum(conv_grad * wide32[offset:offset + length], axis=0)  5.76 us
  transfers between devices with their start and end apart: 22, of which 13 were waited for; matrix products, arithmetic and copies ran while one was open for 21% of the time, Pallas kernels for 0%

profile of v4, /device:TPU:2, one launch (start us, length us, event | category | flops | bytes accessed | tf_op | source)
XLA Modules:
  0.0 224.7 jit_solution(5190738235634351410)
XLA Ops:
  0.7 0.8 slice_bitcast_fusion.9
  1.5 1.3 collective-permute-start.1
  2.8 3.0 %collective-permute-start = (bf16[15,1024]{1,0:T(8,128)(2,1)S(1)}, bf16[15,1024]{1,0:T(8,128)(2,1)S(1)}, u32[]{:S(2)}, u32[]{:S(2)}) collective-permute-start(bf16[15,1024]{1,0:T(8,128)(2,1)S(1)} %get-tuple-element.67), channel_id=1, source_target_pairs={{0,4},{4,8},{8,12},{12,16},{16,20},{20,24},{24,28},{28,32},{32,36}... | collective-permute-start | bytes 92168 | tf_op jit(solution)/shard_map/ppermute | solution.py:16
  5.9 0.8 pad_maximum_fusion.12
  6.6 0.9 broadcast_in_dim.40
  7.5 8.5 %all-to-all-start = ((bf16[8,2,16,1024]{3,2,1,0:T(8,128)(2,1)}), bf16[8,2,16,1024]{3,2,1,0:T(8,128)(2,1)}, u32[]{:S(2)}, u32[]{:S(2)}) async-start(bf16[8,2,16,1024]{3,2,1,0:T(8,128)(2,1)} %broadcast_in_dim.40), calls=%async_computation | async-start | bytes 1048576 | tf_op jit(solution)/shard_map/all_to_all | solution.py:31
  16.0 1.1 fusion.130
  17.1 1.3 fusion.129
  18.7 0.7 fusion.120
  21.2 1.2 gather_fusion.1
  22.9 5.2 %add_convert_fusion.1 = (bf16[256,1024]{1,0:T(8,128)(2,1)S(1)}, f32[256,1024]{1,0:T(8,128)}) fusion(bf16[1,256,1024]{2,1,0:T(8,128)(2,1)S(1)} %copy-done.4, f32[286,1024]{1,0:T(8,128)S(1)} %maximum_convert_fusion, f32[1024]{0:T(1024)S(1)} %bitcast.203, f32[1024]{0:T(1024)S(1)} %bitcast.205, f32[1024]{0:T(1024)S(1)} %bitcast.209, f32[1024]{0:T(1024)S(1)} %bitcast.211, ...), kind=kLoop, calls=%fused_computation.202 | loop fusion | flops 17825792 | bytes 34729984 | tf_op jit(solution)/shard_map/convert_element_type | solution.py:109
  28.0 1.2 gather_fusion
  29.2 5.7 %all-to-all-done = bf16[8,2,16,1024]{3,2,1,0:T(8,128)(2,1)} async-done(((bf16[8,2,16,1024]{3,2,1,0:T(8,128)(2,1)}), bf16[8,2,16,1024]{3,2,1,0:T(8,128)(2,1)}, u32[]{:S(2)}, u32[]{:S(2)}) %all-to-all-start) | async-done | bytes 524320 | tf_op jit(solution)/shard_map/all_to_all | solution.py:31
  34.9 2.6 %broadcast_in_dim.41 = bf16[4,8,2,16,1024]{4,3,2,1,0:T(8,128)(2,1)} broadcast(bf16[8,2,16,1024]{3,2,1,0:T(8,128)(2,1)} %all-to-all-done), dimensions={1,2,3,4} | broadcast | bytes 2621440 | tf_op jit(solution)/shard_map/broadcast_in_dim | solution.py:36
  37.5 4.8 %all-to-all-start.1 = ((bf16[4,8,2,16,1024]{4,3,2,1,0:T(8,128)(2,1)}), bf16[4,8,2,16,1024]{4,3,2,1,0:T(8,128)(2,1)}, u32[]{:S(2)}, u32[]{:S(2)}) async-start(bf16[4,8,2,16,1024]{4,3,2,1,0:T(8,128)(2,1)} %broadcast_in_dim.41), calls=%async_computation.1 | async-start | bytes 4194304 | tf_op jit(solution)/shard_map/all_to_all | solution.py:31
  42.5 1.8 collective-permute-start.2
  44.3 1.5 collective-permute-done.2
  46.0 28.8 %all-to-all-done.1 = bf16[4,8,2,16,1024]{4,3,2,1,0:T(8,128)(2,1)} async-done(((bf16[4,8,2,16,1024]{4,3,2,1,0:T(8,128)(2,1)}), bf16[4,8,2,16,1024]{4,3,2,1,0:T(8,128)(2,1)}, u32[]{:S(2)}, u32[]{:S(2)}) %all-to-all-start.1) | async-done | bytes 2097184 | tf_op jit(solution)/shard_map/all_to_all | solution.py:31
  76.2 2.4 %collective-permute-start.4 = (bf16[2,128,1024]{2,1,0:T(8,128)(2,1)S(1)}, bf16[2,128,1024]{2,1,0:T(8,128)(2,1)S(1)}, u32[]{:S(2)}, u32[]{:S(2)}) collective-permute-start(bf16[2,128,1024]{2,1,0:T(8,128)(2,1)S(1)} %pad_maximum_fusion.7), channel_id=1, source_target_pairs={{0,2},{1,3},{2,0},{3,1},{4,6},{5,7},{6,4},{7,5},{8,10},{9,11},{10,... | collective-permute-start | bytes 1572872 | tf_op jit(solution)/shard_map/ppermute | solution.py:21
  78.6 1.8 collective-permute-start.3
  80.4 0.9 fusion.104
  81.4 8.8 %collective-permute-done.5 = bf16[2,128,1024]{2,1,0:T(8,128)(2,1)} collective-permute-done((bf16[2,128,1024]{2,1,0:T(8,128)(2,1)S(1)}, bf16[2,128,1024]{2,1,0:T(8,128)(2,1)}, u32[]{:S(2)}, u32[]{:S(2)}) %collective-permute-start.5) | collective-permute-done | bytes 524320 | tf_op jit(solution)/shard_map/ppermute | solution.py:21
  90.1 1.1 slice_bitcast_fusion.3
  91.2 11.0 %collective-permute-done.4 = bf16[2,128,1024]{2,1,0:T(8,128)(2,1)S(1)} collective-permute-done((bf16[2,128,1024]{2,1,0:T(8,128)(2,1)S(1)}, bf16[2,128,1024]{2,1,0:T(8,128)(2,1)S(1)}, u32[]{:S(2)}, u32[]{:S(2)}) %collective-permute-start.4) | collective-permute-done | bytes 524320 | tf_op jit(solution)/shard_map/ppermute | solution.py:21
  102.2 0.9 collective-permute-done.3
  103.1 2.5 %broadcast_select_fusion.3 = (bf16[4,8,1,16,1024]{4,3,2,1,0:T(8,128)(2,1)S(1)}, bf16[4,8,1,16,1024]{4,3,2,1,0:T(8,128)(2,1)S(1)}, bf16[4,8,1,16,1024]{4,3,2,1,0:T(8,128)(2,1)S(1)}, bf16[4,8,1,16,1024]{4,3,2,1,0:T(8,128)(2,1)S(1)}) fusion(pred[]{:T(512)S(6)} %eq.11, bf16[4,8,2,16,1024]{4,3,2,1,0:T(8,128)(2,1)} %collective-permute-done.6, ...), kind=kLoop, calls=%fused_computation.208 | loop fusion | flops 2097152 | bytes 8388609 | tf_op jit(solution)/shard_map/jit(_where)/select_n | solution.py:52
  106.0 1.3 fusion.119
  107.2 1.3 multiply_convert_fusion
  108.6 1.7 multiply_convert_fusion.2
  110.3 1.3 fusion.131
  111.7 1.5 collective-permute-start.9
  113.2 3.3 %collective-permute-start.8 = (bf16[128,1024]{1,0:T(8,128)(2,1)S(1)}, bf16[128,1024]{1,0:T(8,128)(2,1)S(1)}, u32[]{:S(2)}, u32[]{:S(2)}) collective-permute-start(bf16[128,1024]{1,0:T(8,128)(2,1)S(1)} %get-tuple-element.58), channel_id=1, source_target_pairs={{0,2},{1,3},{2,0},{3,1},{4,6},{5,7},{6,4},{7,5},{8,10},{9,11},{10,... | collective-permute-start | bytes 786440 | tf_op jit(solution)/shard_map/ppermute | solution.py:21
  117.2 1.2 dynamic-slice_bitcast_fusion.2
  118.4 1.3 convolution_convert_fusion
  119.7 1.9 collective-permute-done.9
  121.6 2.3 %collective-permute-done.8 = bf16[128,1024]{1,0:T(8,128)(2,1)S(1)} collective-permute-done((bf16[128,1024]{1,0:T(8,128)(2,1)S(1)}, bf16[128,1024]{1,0:T(8,128)(2,1)S(1)}, u32[]{:S(2)}, u32[]{:S(2)}) %collective-permute-start.8) | collective-permute-done | bytes 262176 | tf_op jit(solution)/shard_map/ppermute | solution.py:21
  123.9 4.4 %collective-permute-done.7 = bf16[128,1024]{1,0:T(8,128)(2,1)S(1)} collective-permute-done((bf16[128,1024]{1,0:T(8,128)(2,1)S(1)}, bf16[128,1024]{1,0:T(8,128)(2,1)S(1)}, u32[]{:S(2)}, u32[]{:S(2)}) %collective-permute-start.7) | collective-permute-done | bytes 262176 | tf_op jit(solution)/shard_map/ppermute | solution.py:21
  129.1 1.3 collective-permute-start.10
  130.4 1.2 dynamic-slice_bitcast_fusion.3
  131.5 1.5 pad_maximum_fusion.2
  133.0 1.1 collective-permute-start.13
  134.2 3.9 %scatter_custom_fusion = f32[256,1024]{1,0:T(8,128)} fusion(s32[256]{0:T(256)} %bitcast.280, bf16[128,1024]{1,0:T(8,128)(2,1)S(1)} %collective-permute-done.10, bf16[]{:T(256)} %constant.122, bf16[128,1024]{1,0:T(8,128)(2,1)S(1)} %broadcast_select_fusion.5, f32[]{:T(128)} %constant.94.clone.1, pred[256]{0:T(512)(128)(4,1)S(1)} %copy-done.42), kind=kCustom, calls=%fused_computation.236 | custom fusion | flops 1572864 | bytes 1574656 | tf_op jit(solution)/shard_map/scatter-add | solution.py:162
  138.1 4.0 %multiply_reduce_fusion = (f32[1024]{0:T(1024)S(1)}, f32[1024]{0:T(1024)S(1)}, f32[1024]{0:T(1024)S(1)}, f32[1024]{0:T(1024)S(1)}, f32[1024]{0:T(1024)S(1)}, /*i...) fusion(f32[286,1024]{1,0:T(8,128)S(1)} %maximum_convert_fusion,, ...), kind=kLoop, calls=%fused_computation.163 | loop fusion | flops 11515904 | bytes 22093824 | tf_op jit(solution)/shard_map/reduce_sum | solution.py:167
  142.1 1.8 multiply_reduce_fusion.1
  144.1 11.8 %all_to_all.30 = f32[8,8,512]{2,1,0:T(8,128)S(1)} all-to-all(f32[8,8,512]{2,1,0:T(8,128)S(1)} %reshape.131), channel_id=1, replica_groups=mesh['y'=4,'z'=8,'core'=2,'utt'=4] {'core','utt'}, dimensions={0} | all-to-all | bytes 262144 | tf_op jit(solution)/shard_map/all_to_all | solution.py:31
  155.9 0.9 broadcast_in_dim.43
  156.8 3.9 %all-to-all-start.4 = ((f32[32,8,512]{2,1,0:T(8,128)}), f32[32,8,512]{2,1,0:T(8,128)S(1)}, u32[]{:S(2)}, u32[]{:S(2)}) async-start(f32[32,8,512]{2,1,0:T(8,128)} %broadcast_in_dim.43), calls=%async_computation.4 | async-start | bytes 1048576 | tf_op jit(solution)/shard_map/all_to_all | solution.py:31
  160.7 3.0 %add_convert_fusion = bf16[4,16,16,1024]{3,2,1,0:T(8,128)(2,1)S(1)} fusion(bf16[4,16,16,1024]{3,2,1,0:T(8,128)(2,1)} %collective-permute-done.13, bf16[4,8,16,1024]{3,2,1,0:T(8,128)(2,1)S(1)} %copy-done.3, bf16[4,8,16,1024]{3,2,1,0:T(8,128)(2,1)} %get-tuple-element.50), kind=kLoop, calls=%fused_computation.31 | loop fusion | flops 5242880 | bytes 6291456 | tf_op jit(solution)/shard_map/convert_element_type | solution.py:63
  163.7 1.3 copy-done.2
  165.1 1.2 dynamic-slice_bitcast_fusion.6
  166.3 3.0 %collective-permute-start.16 = (bf16[16,16,1024]{2,1,0:T(8,128)(2,1)}, bf16[16,16,1024]{2,1,0:T(8,128)(2,1)}, u32[]{:S(2)}, u32[]{:S(2)}) collective-permute-start(bf16[16,16,1024]{2,1,0:T(8,128)(2,1)} %get-tuple-element.48), channel_id=1, source_target_pairs={{0,192},{64,0},{128,64},{192,128},{1,193},{65,1},{129,65},{193,129... | collective-permute-start | bytes 1572872 | tf_op jit(solution)/shard_map/ppermute | solution.py:21
  169.3 0.7 collective-permute-start.15
  170.1 0.9 collective-permute-start.14
  171.0 1.3 collective-permute-start.12
  172.3 1.3 collective-permute-start.11
  173.6 4.4 %all-to-all-done.4 = f32[32,8,512]{2,1,0:T(8,128)S(1)} async-done(((f32[32,8,512]{2,1,0:T(8,128)}), f32[32,8,512]{2,1,0:T(8,128)S(1)}, u32[]{:S(2)}, u32[]{:S(2)}) %all-to-all-start.4) | async-done | bytes 524320 | tf_op jit(solution)/shard_map/all_to_all | solution.py:31
  178.7 4.4 %all-to-all-start.5 = ((f32[8,8,512]{2,1,0:T(8,128)}), f32[8,8,512]{2,1,0:T(8,128)S(1)}, u32[]{:S(2)}, u32[]{:S(2)}) async-start(f32[8,8,512]{2,1,0:T(8,128)} %broadcast_in_dim.44), calls=%async_computation.5 | async-start | bytes 262144 | tf_op jit(solution)/shard_map/all_to_all | solution.py:31
  183.1 11.5 %collective-permute-done.16 = bf16[16,16,1024]{2,1,0:T(8,128)(2,1)} collective-permute-done((bf16[16,16,1024]{2,1,0:T(8,128)(2,1)}, bf16[16,16,1024]{2,1,0:T(8,128)(2,1)}, u32[]{:S(2)}, u32[]{:S(2)}) %collective-permute-start.16) | collective-permute-done | bytes 524320 | tf_op jit(solution)/shard_map/ppermute | solution.py:21
  194.6 3.4 %collective-permute-done.14 = bf16[16,16,1024]{2,1,0:T(8,128)(2,1)} collective-permute-done((bf16[16,16,1024]{2,1,0:T(8,128)(2,1)}, bf16[16,16,1024]{2,1,0:T(8,128)(2,1)}, u32[]{:S(2)}, u32[]{:S(2)}) %collective-permute-start.14) | collective-permute-done | bytes 524320 | tf_op jit(solution)/shard_map/ppermute | solution.py:21
  198.0 1.9 fusion.92
  199.9 0.8 copy.14
  200.7 5.6 %all-to-all-start.2 = ((bf16[8,2,16,1024]{3,2,1,0:T(8,128)(2,1)}), bf16[8,2,16,1024]{3,2,1,0:T(8,128)(2,1)S(1)}, u32[]{:S(2)}, u32[]{:S(2)}) async-start(bf16[8,2,16,1024]{3,2,1,0:T(8,128)(2,1)} %copy.14), calls=%async_computation.2 | async-start | bytes 1048576 | tf_op jit(solution)/shard_map/all_to_all | solution.py:31
  206.3 6.6 %fusion.118 = bf16[1,256,1024]{2,1,0:T(8,128)(2,1)} fusion(f32[256,1024]{1,0:T(8,128)S(1)} %copy-done.1, f32[256,1024]{1,0:T(8,128)S(1)} %get-tuple-element.39, f32[15,1024]{1,0:T(8,128)S(1)} %collective-permute-done.12, f32[1024]{0:T(1024)} %bitcast.204, f32[1024]{0:T(1024)} %bitcast.206, f32[1024]{0:T(1024)} %bitcast.210, f32[1024]{0:T(1024)} %bitcast.212, ...), kind=kLoop, calls=%fused_computation.244 | loop fusion | flops 24379392 | bytes 2871296 | tf_op jit(solution)/shard_map/broadcast_in_dim | solution.py:174
  213.6 10.4 %all-to-all-done.2 = bf16[8,2,16,1024]{3,2,1,0:T(8,128)(2,1)S(1)} async-done(((bf16[8,2,16,1024]{3,2,1,0:T(8,128)(2,1)}), bf16[8,2,16,1024]{3,2,1,0:T(8,128)(2,1)S(1)}, u32[]{:S(2)}, u32[]{:S(2)}) %all-to-all-start.2) | async-done | bytes 524320 | tf_op jit(solution)/shard_map/all_to_all | solution.py:31
  (135 shorter events, 7.5 us)
Async XLA Ops:
  0.6 20.6 %copy-start = (bf16[1,256,1024]{2,1,0:T(8,128)(2,1)S(1)}, bf16[1,256,1024]{2,1,0:T(8,128)(2,1)}, u32[]{:S(2)}) copy-start(bf16[1,256,1024]{2,1,0:T(8,128)(2,1)} %param.9) | copy-start | bytes 1572868
  0.6 18.0 %copy-start.43 = (s32[1,256]{1,0:T(1,128)S(1)}, s32[1,256]{1,0:T(1,128)}, u32[]{:S(2)}) copy-start(s32[1,256]{1,0:T(1,128)} %param.15) | copy-start | bytes 3076
  0.7 18.1 %copy-start.44 = (s32[1,64]{1,0:T(1,128)S(1)}, s32[1,64]{1,0:T(1,128)}, u32[]{:S(2)}) copy-start(s32[1,64]{1,0:T(1,128)} %param.14) | copy-start | bytes 772
  1.5 20.9 %collective-permute-start.1 = (bf16[15,1024]{1,0:T(8,128)(2,1)S(1)}, bf16[15,1024]{1,0:T(8,128)(2,1)S(1)}, u32[]{:S(2)}, u32[]{:S(2)}) collective-permute-start(bf16[15,1024]{1,0:T(8,128)(2,1)S(1)} %get-tuple-element.68), channel_id=1, source_target_pairs={{4,0},{8,4},{12,8},{16,12},{20,16},{24,20},{28,24},{32,28},{36,32}... | collective-permute-start | bytes 92168 | tf_op jit(solution)/shard_map/ppermute | solution.py:16
  2.8 19.6 %collective-permute-start = (bf16[15,1024]{1,0:T(8,128)(2,1)S(1)}, bf16[15,1024]{1,0:T(8,128)(2,1)S(1)}, u32[]{:S(2)}, u32[]{:S(2)}) collective-permute-start(bf16[15,1024]{1,0:T(8,128)(2,1)S(1)} %get-tuple-element.67), channel_id=1, source_target_pairs={{0,4},{4,8},{8,12},{12,16},{16,20},{20,24},{24,28},{28,32},{32,36}... | collective-permute-start | bytes 92168 | tf_op jit(solution)/shard_map/ppermute | solution.py:16
  7.5 27.4 %all-to-all-start = ((bf16[8,2,16,1024]{3,2,1,0:T(8,128)(2,1)}), bf16[8,2,16,1024]{3,2,1,0:T(8,128)(2,1)}, u32[]{:S(2)}, u32[]{:S(2)}) async-start(bf16[8,2,16,1024]{3,2,1,0:T(8,128)(2,1)} %broadcast_in_dim.40), calls=%async_computation | async-start | bytes 1048576 | tf_op jit(solution)/shard_map/all_to_all | solution.py:31
  17.0 5.6 %copy-start.7 = (f32[1,1024]{1,0:T(1,128)}, f32[1,1024]{1,0:T(1,128)S(1)}, u32[]{:S(2)}) copy-start(f32[1,1024]{1,0:T(1,128)S(1)} %get-tuple-element.93) | copy-start | bytes 12292
  17.1 5.6 %copy-start.9 = (f32[1,1024]{1,0:T(1,128)}, f32[1,1024]{1,0:T(1,128)S(1)}, u32[]{:S(2)}) copy-start(f32[1,1024]{1,0:T(1,128)S(1)} %get-tuple-element.94) | copy-start | bytes 12292
  17.1 5.6 %copy-start.10 = (f32[1,1024]{1,0:T(1,128)}, f32[1,1024]{1,0:T(1,128)S(1)}, u32[]{:S(2)}) copy-start(f32[1,1024]{1,0:T(1,128)S(1)} %get-tuple-element.95) | copy-start | bytes 12292
  17.1 5.6 %copy-start.11 = (f32[1,1024]{1,0:T(1,128)}, f32[1,1024]{1,0:T(1,128)S(1)}, u32[]{:S(2)}) copy-start(f32[1,1024]{1,0:T(1,128)S(1)} %get-tuple-element.96) | copy-start | bytes 12292
  17.1 5.6 %copy-start.12 = (f32[1,1024]{1,0:T(1,128)}, f32[1,1024]{1,0:T(1,128)S(1)}, u32[]{:S(2)}) copy-start(f32[1,1024]{1,0:T(1,128)S(1)} %get-tuple-element.97) | copy-start | bytes 12292
  17.1 5.6 %copy-start.13 = (f32[1,1024]{1,0:T(1,128)}, f32[1,1024]{1,0:T(1,128)S(1)}, u32[]{:S(2)}) copy-start(f32[1,1024]{1,0:T(1,128)S(1)} %get-tuple-element.98) | copy-start | bytes 12292
  17.1 5.6 %copy-start.14 = (f32[1,1024]{1,0:T(1,128)}, f32[1,1024]{1,0:T(1,128)S(1)}, u32[]{:S(2)}) copy-start(f32[1,1024]{1,0:T(1,128)S(1)} %get-tuple-element.99) | copy-start | bytes 12292
  17.1 5.6 %copy-start.15 = (f32[1,1024]{1,0:T(1,128)}, f32[1,1024]{1,0:T(1,128)S(1)}, u32[]{:S(2)}) copy-start(f32[1,1024]{1,0:T(1,128)S(1)} %get-tuple-element.100) | copy-start | bytes 12292
  17.1 5.6 %copy-start.16 = (f32[1,1024]{1,0:T(1,128)}, f32[1,1024]{1,0:T(1,128)S(1)}, u32[]{:S(2)}) copy-start(f32[1,1024]{1,0:T(1,128)S(1)} %get-tuple-element.101) | copy-start | bytes 12292
  18.5 4.2 %copy-start.17 = (f32[1,1024]{1,0:T(1,128)}, f32[1,1024]{1,0:T(1,128)S(1)}, u32[]{:S(2)}) copy-start(f32[1,1024]{1,0:T(1,128)S(1)} %get-tuple-element.71) | copy-start | bytes 12292
  18.5 4.2 %copy-start.18 = (f32[1,1024]{1,0:T(1,128)}, f32[1,1024]{1,0:T(1,128)S(1)}, u32[]{:S(2)}) copy-start(f32[1,1024]{1,0:T(1,128)S(1)} %get-tuple-element.72) | copy-start | bytes 12292
  18.5 4.2 %copy-start.19 = (f32[1,1024]{1,0:T(1,128)}, f32[1,1024]{1,0:T(1,128)S(1)}, u32[]{:S(2)}) copy-start(f32[1,1024]{1,0:T(1,128)S(1)} %get-tuple-element.73) | copy-start | bytes 12292
  18.5 4.2 %copy-start.20 = (f32[1,1024]{1,0:T(1,128)}, f32[1,1024]{1,0:T(1,128)S(1)}, u32[]{:S(2)}) copy-start(f32[1,1024]{1,0:T(1,128)S(1)} %get-tuple-element.74) | copy-start | bytes 12292
  18.5 4.2 %copy-start.21 = (f32[1,1024]{1,0:T(1,128)}, f32[1,1024]{1,0:T(1,128)S(1)}, u32[]{:S(2)}) copy-start(f32[1,1024]{1,0:T(1,128)S(1)} %get-tuple-element.75) | copy-start | bytes 12292
  18.5 4.2 %copy-start.22 = (f32[1,1024]{1,0:T(1,128)}, f32[1,1024]{1,0:T(1,128)S(1)}, u32[]{:S(2)}) copy-start(f32[1,1024]{1,0:T(1,128)S(1)} %get-tuple-element.76) | copy-start | bytes 12292
  18.5 4.2 %copy-start.23 = (f32[1,1024]{1,0:T(1,128)}, f32[1,1024]{1,0:T(1,128)S(1)}, u32[]{:S(2)}) copy-start(f32[1,1024]{1,0:T(1,128)S(1)} %get-tuple-element.77) | copy-start | bytes 12292
  18.6 4.2 %copy-start.24 = (f32[1,1024]{1,0:T(1,128)}, f32[1,1024]{1,0:T(1,128)S(1)}, u32[]{:S(2)}) copy-start(f32[1,1024]{1,0:T(1,128)S(1)} %get-tuple-element.78) | copy-start | bytes 12292
  18.6 4.2 %copy-start.25 = (f32[1,1024]{1,0:T(1,128)}, f32[1,1024]{1,0:T(1,128)S(1)}, u32[]{:S(2)}) copy-start(f32[1,1024]{1,0:T(1,128)S(1)} %get-tuple-element.79) | copy-start | bytes 12292
  18.6 4.2 %copy-start.26 = (f32[1,1024]{1,0:T(1,128)}, f32[1,1024]{1,0:T(1,128)S(1)}, u32[]{:S(2)}) copy-start(f32[1,1024]{1,0:T(1,128)S(1)} %get-tuple-element.80) | copy-start | bytes 12292
  18.6 4.2 %copy-start.27 = (f32[1,1024]{1,0:T(1,128)}, f32[1,1024]{1,0:T(1,128)S(1)}, u32[]{:S(2)}) copy-start(f32[1,1024]{1,0:T(1,128)S(1)} %get-tuple-element.81) | copy-start | bytes 12292
  18.6 4.2 %copy-start.28 = (f32[1,1024]{1,0:T(1,128)}, f32[1,1024]{1,0:T(1,128)S(1)}, u32[]{:S(2)}) copy-start(f32[1,1024]{1,0:T(1,128)S(1)} %get-tuple-element.82) | copy-start | bytes 12292
  18.6 4.2 %copy-start.29 = (f32[1,1024]{1,0:T(1,128)}, f32[1,1024]{1,0:T(1,128)S(1)}, u32[]{:S(2)}) copy-start(f32[1,1024]{1,0:T(1,128)S(1)} %get-tuple-element.83) | copy-start | bytes 12292
  18.6 4.2 %copy-start.30 = (f32[1,1024]{1,0:T(1,128)}, f32[1,1024]{1,0:T(1,128)S(1)}, u32[]{:S(2)}) copy-start(f32[1,1024]{1,0:T(1,128)S(1)} %get-tuple-element.84) | copy-start | bytes 12292
  18.6 4.2 %copy-start.31 = (f32[1,1024]{1,0:T(1,128)}, f32[1,1024]{1,0:T(1,128)S(1)}, u32[]{:S(2)}) copy-start(f32[1,1024]{1,0:T(1,128)S(1)} %get-tuple-element.85) | copy-start | bytes 12292
  18.6 4.2 %copy-start.32 = (f32[1,1024]{1,0:T(1,128)}, f32[1,1024]{1,0:T(1,128)S(1)}, u32[]{:S(2)}) copy-start(f32[1,1024]{1,0:T(1,128)S(1)} %get-tuple-element.86) | copy-start | bytes 12292
  18.6 4.2 %copy-start.33 = (f32[1,1024]{1,0:T(1,128)}, f32[1,1024]{1,0:T(1,128)S(1)}, u32[]{:S(2)}) copy-start(f32[1,1024]{1,0:T(1,128)S(1)} %get-tuple-element.87) | copy-start | bytes 12292
  18.7 4.2 %copy-start.34 = (f32[1,1024]{1,0:T(1,128)}, f32[1,1024]{1,0:T(1,128)S(1)}, u32[]{:S(2)}) copy-start(f32[1,1024]{1,0:T(1,128)S(1)} %get-tuple-element.88) | copy-start | bytes 12292
  18.7 4.2 %copy-start.35 = (f32[1,1024]{1,0:T(1,128)}, f32[1,1024]{1,0:T(1,128)S(1)}, u32[]{:S(2)}) copy-start(f32[1,1024]{1,0:T(1,128)S(1)} %get-tuple-element.89) | copy-start | bytes 12292
  18.7 3.7 %copy-start.40 = (s32[256,1]{0,1:T(1,128)}, s32[256,1]{0,1:T(1,128)S(1)}, u32[]{:S(2)}) copy-start(s32[256,1]{0,1:T(1,128)S(1)} %compare_select_fusion) | copy-start | bytes 3076
  20.6 21.7 %copy-start.41 = (pred[256]{0:T(512)(128)(4,1)}, pred[256]{0:T(512)(128)(4,1)S(1)}, u32[]{:S(2)}) copy-start(pred[256]{0:T(512)(128)(4,1)S(1)} %iota_compare_fusion) | copy-start | bytes 772
  37.5 37.3 %all-to-all-start.1 = ((bf16[4,8,2,16,1024]{4,3,2,1,0:T(8,128)(2,1)}), bf16[4,8,2,16,1024]{4,3,2,1,0:T(8,128)(2,1)}, u32[]{:S(2)}, u32[]{:S(2)}) async-start(bf16[4,8,2,16,1024]{4,3,2,1,0:T(8,128)(2,1)} %broadcast_in_dim.41), calls=%async_computation.1 | async-start | bytes 4194304 | tf_op jit(solution)/shard_map/all_to_all | solution.py:31
  42.5 32.7 %copy-start.6 = (f32[1024]{0:T(1024)S(1)}, f32[1024]{0:T(1024)}, u32[]{:S(2)}) copy-start(f32[1024]{0:T(1024)} %param.11) | copy-start | bytes 12292
  42.5 3.3 %collective-permute-start.2 = (bf16[2,128,1024]{2,1,0:T(8,128)(2,1)S(1)}, bf16[2,128,1024]{2,1,0:T(8,128)(2,1)S(1)}, u32[]{:S(2)}, u32[]{:S(2)}) collective-permute-start(bf16[2,128,1024]{2,1,0:T(8,128)(2,1)S(1)} %slice_select_fusion), channel_id=1, source_target_pairs={{0,4},{4,8},{8,12},{12,16},{16,20},{20,24},{24,28},{28,32},{32,36}... | collective-permute-start | bytes 1572872 | tf_op jit(solution)/shard_map/ppermute | solution.py:16
  46.0 29.3 %copy-start.36 = (f32[128]{0:T(128)}, f32[128]{0:T(128)S(1)}, u32[]{:S(2)}) copy-start(f32[128]{0:T(128)S(1)} %broadcast_multiply_fusion.2) | copy-start | bytes 1540
  74.8 28.3 %collective-permute-start.6 = (bf16[4,8,2,16,1024]{4,3,2,1,0:T(8,128)(2,1)}, bf16[4,8,2,16,1024]{4,3,2,1,0:T(8,128)(2,1)}, u32[]{:S(2)}, u32[]{:S(2)}) collective-permute-start(bf16[4,8,2,16,1024]{4,3,2,1,0:T(8,128)(2,1)} %all-to-all-done.1), channel_id=1, source_target_pairs={{0,4},{4,0},{1,5},{5,1},{2,6},{6,2},{3,7},{7,3},{8,12},{12,8},{9,1... | collective-permute-start | bytes 6291464 | tf_op jit(solution)/shard_map/ppermute | solution.py:21
  75.6 14.5 %collective-permute-start.5 = (bf16[2,128,1024]{2,1,0:T(8,128)(2,1)S(1)}, bf16[2,128,1024]{2,1,0:T(8,128)(2,1)}, u32[]{:S(2)}, u32[]{:S(2)}) collective-permute-start(bf16[2,128,1024]{2,1,0:T(8,128)(2,1)S(1)} %pad_maximum_fusion.7), channel_id=1, source_target_pairs={{0,3},{1,0},{2,1},{3,2},{4,7},{5,4},{6,5},{7,6},{8,11},{9,8},{10,9... | collective-permute-start | bytes 1572872 | tf_op jit(solution)/shard_map/ppermute | solution.py:21
  76.2 26.0 %collective-permute-start.4 = (bf16[2,128,1024]{2,1,0:T(8,128)(2,1)S(1)}, bf16[2,128,1024]{2,1,0:T(8,128)(2,1)S(1)}, u32[]{:S(2)}, u32[]{:S(2)}) collective-permute-start(bf16[2,128,1024]{2,1,0:T(8,128)(2,1)S(1)} %pad_maximum_fusion.7), channel_id=1, source_target_pairs={{0,2},{1,3},{2,0},{3,1},{4,6},{5,7},{6,4},{7,5},{8,10},{9,11},{10,... | collective-permute-start | bytes 1572872 | tf_op jit(solution)/shard_map/ppermute | solution.py:21
  78.6 24.4 %collective-permute-start.3 = (bf16[2,128,1024]{2,1,0:T(8,128)(2,1)S(1)}, bf16[2,128,1024]{2,1,0:T(8,128)(2,1)S(1)}, u32[]{:S(2)}, u32[]{:S(2)}) collective-permute-start(bf16[2,128,1024]{2,1,0:T(8,128)(2,1)S(1)} %pad_maximum_fusion.7), channel_id=1, source_target_pairs={{0,1},{1,2},{2,3},{3,0},{4,5},{5,6},{6,7},{7,4},{8,9},{9,10},{10,1... | collective-permute-start | bytes 1572872 | tf_op jit(solution)/shard_map/ppermute | solution.py:21
  111.7 9.9 %collective-permute-start.9 = (bf16[128,1024]{1,0:T(8,128)(2,1)S(1)}, bf16[128,1024]{1,0:T(8,128)(2,1)S(1)}, u32[]{:S(2)}, u32[]{:S(2)}) collective-permute-start(bf16[128,1024]{1,0:T(8,128)(2,1)S(1)} %get-tuple-element.57), channel_id=1, source_target_pairs={{0,1},{1,2},{2,3},{3,0},{4,5},{5,6},{6,7},{7,4},{8,9},{9,10},{10,1... | collective-permute-start | bytes 786440 | tf_op jit(solution)/shard_map/ppermute | solution.py:21
  113.2 10.7 %collective-permute-start.8 = (bf16[128,1024]{1,0:T(8,128)(2,1)S(1)}, bf16[128,1024]{1,0:T(8,128)(2,1)S(1)}, u32[]{:S(2)}, u32[]{:S(2)}) collective-permute-start(bf16[128,1024]{1,0:T(8,128)(2,1)S(1)} %get-tuple-element.58), channel_id=1, source_target_pairs={{0,2},{1,3},{2,0},{3,1},{4,6},{5,7},{6,4},{7,5},{8,10},{9,11},{10,... | collective-permute-start | bytes 786440 | tf_op jit(solution)/shard_map/ppermute | solution.py:21
  116.5 11.8 %collective-permute-start.7 = (bf16[128,1024]{1,0:T(8,128)(2,1)S(1)}, bf16[128,1024]{1,0:T(8,128)(2,1)S(1)}, u32[]{:S(2)}, u32[]{:S(2)}) collective-permute-start(bf16[128,1024]{1,0:T(8,128)(2,1)S(1)} %get-tuple-element.56), channel_id=1, source_target_pairs={{0,3},{1,0},{2,1},{3,2},{4,7},{5,4},{6,5},{7,6},{8,11},{9,8},{10,9... | collective-permute-start | bytes 786440 | tf_op jit(solution)/shard_map/ppermute | solution.py:21
  118.4 10.0 %copy-start.37 = (f32[128]{0:T(128)S(1)}, f32[128]{0:T(128)}, u32[]{:S(2)}) copy-start(f32[128]{0:T(128)} %copy-done.36) | copy-start | bytes 1540
  118.4 10.0 %copy-start.39 = (f32[128]{0:T(128)S(1)}, f32[128]{0:T(128)}, u32[]{:S(2)}) copy-start(f32[128]{0:T(128)} %copy-done.38) | copy-start | bytes 1540
  129.1 5.1 %collective-permute-start.10 = (bf16[128,1024]{1,0:T(8,128)(2,1)S(1)}, bf16[128,1024]{1,0:T(8,128)(2,1)S(1)}, u32[]{:S(2)}, u32[]{:S(2)}) collective-permute-start(bf16[128,1024]{1,0:T(8,128)(2,1)S(1)} %fusion.109), channel_id=1, source_target_pairs={{4,0},{8,4},{12,8},{16,12},{20,16},{24,20},{28,24},{32,28},{36,32}... | collective-permute-start | bytes 786440 | tf_op jit(solution)/shard_map/ppermute | solution.py:16
  131.5 2.7 %copy-start.42 = (pred[256]{0:T(512)(128)(4,1)S(1)}, pred[256]{0:T(512)(128)(4,1)}, u32[]{:S(2)}) copy-start(pred[256]{0:T(512)(128)(4,1)} %copy-done.41) | copy-start | bytes 772
  133.0 27.7 %collective-permute-start.13 = (bf16[4,16,16,1024]{3,2,1,0:T(8,128)(2,1)}, bf16[4,16,16,1024]{3,2,1,0:T(8,128)(2,1)}, u32[]{:S(2)}, u32[]{:S(2)}) collective-permute-start(bf16[4,16,16,1024]{3,2,1,0:T(8,128)(2,1)} %pad_maximum_fusion.2), channel_id=1, source_target_pairs={{0,4},{4,0},{1,5},{5,1},{2,6},{6,2},{3,7},{7,3},{8,12},{12,8},{9,1... | collective-permute-start | bytes 6291464 | tf_op jit(solution)/shard_map/ppermute | solution.py:21
  143.8 16.9 %copy-start.3 = (bf16[4,8,16,1024]{3,2,1,0:T(8,128)(2,1)S(1)}, bf16[4,8,16,1024]{3,2,1,0:T(8,128)(2,1)}, u32[]{:S(2)}) copy-start(bf16[4,8,16,1024]{3,2,1,0:T(8,128)(2,1)} %get-tuple-element.52) | copy-start | bytes 3145732
  156.8 21.2 %all-to-all-start.4 = ((f32[32,8,512]{2,1,0:T(8,128)}), f32[32,8,512]{2,1,0:T(8,128)S(1)}, u32[]{:S(2)}, u32[]{:S(2)}) async-start(f32[32,8,512]{2,1,0:T(8,128)} %broadcast_in_dim.43), calls=%async_computation.4 | async-start | bytes 1048576 | tf_op jit(solution)/shard_map/all_to_all | solution.py:31
  166.3 28.3 %collective-permute-start.16 = (bf16[16,16,1024]{2,1,0:T(8,128)(2,1)}, bf16[16,16,1024]{2,1,0:T(8,128)(2,1)}, u32[]{:S(2)}, u32[]{:S(2)}) collective-permute-start(bf16[16,16,1024]{2,1,0:T(8,128)(2,1)} %get-tuple-element.48), channel_id=1, source_target_pairs={{0,192},{64,0},{128,64},{192,128},{1,193},{65,1},{129,65},{193,129... | collective-permute-start | bytes 1572872 | tf_op jit(solution)/shard_map/ppermute | solution.py:21
  169.3 25.2 %collective-permute-start.15 = (bf16[16,16,1024]{2,1,0:T(8,128)(2,1)}, bf16[16,16,1024]{2,1,0:T(8,128)(2,1)}, u32[]{:S(2)}, u32[]{:S(2)}) collective-permute-start(bf16[16,16,1024]{2,1,0:T(8,128)(2,1)} %get-tuple-element.49), channel_id=1, source_target_pairs={{0,128},{64,192},{128,0},{192,64},{1,129},{65,193},{129,1},{193,65... | collective-permute-start | bytes 1572872 | tf_op jit(solution)/shard_map/ppermute | solution.py:21
  170.1 27.9 %collective-permute-start.14 = (bf16[16,16,1024]{2,1,0:T(8,128)(2,1)}, bf16[16,16,1024]{2,1,0:T(8,128)(2,1)}, u32[]{:S(2)}, u32[]{:S(2)}) collective-permute-start(bf16[16,16,1024]{2,1,0:T(8,128)(2,1)} %get-tuple-element.47), channel_id=1, source_target_pairs={{0,64},{64,128},{128,192},{192,0},{1,65},{65,129},{129,193},{193,1... | collective-permute-start | bytes 1572872 | tf_op jit(solution)/shard_map/ppermute | solution.py:21
  171.0 35.3 %collective-permute-start.12 = (f32[15,1024]{1,0:T(8,128)S(1)}, f32[15,1024]{1,0:T(8,128)S(1)}, u32[]{:S(2)}, u32[]{:S(2)}) collective-permute-start(f32[15,1024]{1,0:T(8,128)S(1)} %get-tuple-element.55), channel_id=1, source_target_pairs={{0,4},{4,8},{8,12},{12,16},{16,20},{20,24},{24,28},{28,32},{32,36}... | collective-permute-start | bytes 184328 | tf_op jit(solution)/shard_map/ppermute | solution.py:16
  172.3 34.0 %collective-permute-start.11 = (f32[15,1024]{1,0:T(8,128)S(1)}, f32[15,1024]{1,0:T(8,128)S(1)}, u32[]{:S(2)}, u32[]{:S(2)}) collective-permute-start(f32[15,1024]{1,0:T(8,128)S(1)} %get-tuple-element.54), channel_id=1, source_target_pairs={{4,0},{8,4},{12,8},{16,12},{20,16},{24,20},{28,24},{32,28},{36,32}... | collective-permute-start | bytes 184328 | tf_op jit(solution)/shard_map/ppermute | solution.py:16
  178.7 22.0 %all-to-all-start.5 = ((f32[8,8,512]{2,1,0:T(8,128)}), f32[8,8,512]{2,1,0:T(8,128)S(1)}, u32[]{:S(2)}, u32[]{:S(2)}) async-start(f32[8,8,512]{2,1,0:T(8,128)} %broadcast_in_dim.44), calls=%async_computation.5 | async-start | bytes 262144 | tf_op jit(solution)/shard_map/all_to_all | solution.py:31
  183.1 23.2 %copy-start.1 = (f32[256,1024]{1,0:T(8,128)S(1)}, f32[256,1024]{1,0:T(8,128)}, u32[]{:S(2)}) copy-start(f32[256,1024]{1,0:T(8,128)} %scatter_custom_fusion) | copy-start | bytes 3145732
  183.1 23.2 %copy-start.8 = (f32[1,1024]{1,0:T(1,128)S(1)}, f32[1,1024]{1,0:T(1,128)}, u32[]{:S(2)}) copy-start(f32[1,1024]{1,0:T(1,128)} %copy-done.7) | copy-start | bytes 12292
  200.7 23.2 %all-to-all-start.2 = ((bf16[8,2,16,1024]{3,2,1,0:T(8,128)(2,1)}), bf16[8,2,16,1024]{3,2,1,0:T(8,128)(2,1)S(1)}, u32[]{:S(2)}, u32[]{:S(2)}) async-start(bf16[8,2,16,1024]{3,2,1,0:T(8,128)(2,1)} %copy.14), calls=%async_computation.2 | async-start | bytes 1048576 | tf_op jit(solution)/shard_map/all_to_all | solution.py:31
  213.0 11.8 %copy-start.5 = (f32[32,1024]{1,0:T(8,128)}, f32[32,1024]{1,0:T(8,128)S(1)}, u32[]{:S(2)}) copy-start(f32[32,1024]{1,0:T(8,128)S(1)} %reshape.132) | copy-start | bytes 393220
  (3 other events, 3.1 us)

commit v5 on v4

--- a/solution.py
+++ b/solution.py
@@ -179,8 +179,13 @@
     part = jnp.sum(part, axis=0)
     part = spread(part, ("y", "z"))
     part = jnp.sum(part, axis=0)
-    full = spread(part, near)
-    full = full.reshape(small.shape)
+    me = lax.axis_index("utt")
+    ring = [part] + [turn(part, "utt", by) for by in range(1, utts)]
+    ring = jnp.stack(ring[::-1] * 2)
+    ring = lax.dynamic_slice_in_dim(ring, utts - 1 - me, utts, 0)
+    other = turn(ring, "core", 1)
+    full = [jnp.where(core == 0, ring, other), jnp.where(core == 0, other, ring)]
+    full = jnp.stack(full).reshape(small.shape)
     load = exchange(chip, "z")
     grad_weight_in, grad_weight_out = jnp.sum(load.astype(f32), axis=0)
     return (grad_x, grad_weight_in, grad_weight_out, full[:tap_count], full[tap_count])

time: 228 us -> 253 us (1.11)
  waiting for transfers between devices: 94.9 us -> 114 us
  blocking collectives: 11.8 us -> 0 us
  starting transfers between devices: 53.2 us -> 64.3 us
  matrix products: 6.94 us -> 11.3 us
    all_to_all x1 -> x0, blocking collectives: 11.8 us -> none  [exchange(): return lax.all_to_all(cells, axis, 0, 0, tiled=True)]
    ppermute x11 -> x15, waiting for transfers between devices: 44.1 us -> 54.4 us  [turn(): lax.ppermute(cells, axis, [(i, (i + by) % count) for i in range(count)])]
    ppermute x11 -> x15, starting transfers between devices: 16.1 us -> 24.2 us  [turn(): lax.ppermute(cells, axis, [(i, (i + by) % count) for i in range(count)])]
    all_to_all x5, waiting for transfers between devices: 49.3 us -> 55.6 us  [exchange(): return lax.all_to_all(cells, axis, 0, 0, tiled=True)]
    all_to_all x5, starting transfers between devices: 27.1 us -> 30.2 us  [exchange(): return lax.all_to_all(cells, axis, 0, 0, tiled=True)]
    dot_general x1, matrix products: 1.35 us -> 4.29 us  [per_device(): lax.dot_general(activation, grad_all, over_rows, preferred_element_type=f32)]
    another operation x1, local copies, waits for them, and re-layouts: 0.24 us -> 3.12 us  [per_device(): small = jnp.stack(kernel_term + [gain_term])]
  transfers between devices with their start and end apart: 22 -> 26, of which waited for: 13 -> 17; matrix products, arithmetic and copies ran while one was open for 21% -> 16% of each run, Pallas kernels for 0% -> 0%
where the time goes in v5:
time: 253 us; the launch traced here: 249 us
  waiting for transfers between devices  114 us (45%)
  starting transfers between devices  64.3 us (25%)
  other arithmetic  35.5 us (14%)
  local copies, waits for them, and re-layouts  21.2 us (8%)
  matrix products  11.3 us (4%)
  between operations  2.61 us (1%)
    all_to_all x5, waiting for transfers between devices, exchange(): return lax.all_to_all(cells, axis, 0, 0, tiled=True)  55.6 us
    ppermute x15, waiting for transfers between devices, turn(): lax.ppermute(cells, axis, [(i, (i + by) % count) for i in range(count)])  54.4 us
    all_to_all x5, starting transfers between devices, exchange(): return lax.all_to_all(cells, axis, 0, 0, tiled=True)  30.2 us
    ppermute x15, starting transfers between devices, turn(): lax.ppermute(cells, axis, [(i, (i + by) % count) for i in range(count)])  24.2 us
    ppermute x6, starting transfers between devices, shift(): lax.ppermute(cells, axis, [(i, i + by) for i in range(count) if 0 <= i +...  9.96 us
    reduce_sum x2, other arithmetic, per_device(): jnp.sum(conv_grad * wide32[offset:offset + length], axis=0)  7.03 us
    broadcast_in_dim x1, other arithmetic, per_device(): grad_x = (frame_grad + transposed).astype(bf16)[None]  6.6 us
    convert_element_type x1, other arithmetic, per_device(): hidden = (frames.astype(f32) + jax.nn.silu(conv_out)).astype(bf16)  5.13 us
  transfers between devices with their start and end apart: 26, of which 17 were waited for; matrix products, arithmetic and copies ran while one was open for 16% of the time, Pallas kernels for 0%

profile of v5, /device:TPU:2, one launch (start us, length us, event | category | flops | bytes accessed | tf_op | source)
XLA Modules:
  0.0 248.6 jit_solution(10573444393637181177)
XLA Ops:
  0.7 0.8 slice_bitcast_fusion.9
  1.5 1.3 collective-permute-start.1
  2.8 3.0 %collective-permute-start = (bf16[15,1024]{1,0:T(8,128)(2,1)S(1)}, bf16[15,1024]{1,0:T(8,128)(2,1)S(1)}, u32[]{:S(2)}, u32[]{:S(2)}) collective-permute-start(bf16[15,1024]{1,0:T(8,128)(2,1)S(1)} %get-tuple-element.67), channel_id=1, source_target_pairs={{0,4},{4,8},{8,12},{12,16},{16,20},{20,24},{24,28},{28,32},{32,36}... | collective-permute-start | bytes 92168 | tf_op jit(solution)/shard_map/ppermute | solution.py:16
  5.9 0.8 pad_maximum_fusion.13
  6.6 0.9 broadcast_in_dim.38
  7.5 8.5 %all-to-all-start = ((bf16[8,2,16,1024]{3,2,1,0:T(8,128)(2,1)}), bf16[8,2,16,1024]{3,2,1,0:T(8,128)(2,1)}, u32[]{:S(2)}, u32[]{:S(2)}) async-start(bf16[8,2,16,1024]{3,2,1,0:T(8,128)(2,1)} %broadcast_in_dim.38), calls=%async_computation | async-start | bytes 1048576 | tf_op jit(solution)/shard_map/all_to_all | solution.py:31
  16.0 1.1 fusion.130
  17.2 1.3 fusion.129
  21.3 1.2 gather_fusion.1
  23.0 5.1 %add_convert_fusion.1 = (bf16[256,1024]{1,0:T(8,128)(2,1)S(1)}, f32[256,1024]{1,0:T(8,128)}) fusion(bf16[1,256,1024]{2,1,0:T(8,128)(2,1)S(1)} %copy-done.2, f32[286,1024]{1,0:T(8,128)S(1)} %maximum_convert_fusion, f32[1024]{0:T(1024)S(1)} %bitcast.221, f32[1024]{0:T(1024)S(1)} %bitcast.223, f32[1024]{0:T(1024)S(1)} %bitcast.227, f32[1024]{0:T(1024)S(1)} %bitcast.229, ...), kind=kLoop, calls=%fused_computation.202 | loop fusion | flops 17825792 | bytes 34729984 | tf_op jit(solution)/shard_map/convert_element_type | solution.py:109
  28.1 1.2 gather_fusion
  29.3 5.6 %all-to-all-done = bf16[8,2,16,1024]{3,2,1,0:T(8,128)(2,1)} async-done(((bf16[8,2,16,1024]{3,2,1,0:T(8,128)(2,1)}), bf16[8,2,16,1024]{3,2,1,0:T(8,128)(2,1)}, u32[]{:S(2)}, u32[]{:S(2)}) %all-to-all-start) | async-done | bytes 524320 | tf_op jit(solution)/shard_map/all_to_all | solution.py:31
  34.9 2.6 %broadcast_in_dim.39 = bf16[4,8,2,16,1024]{4,3,2,1,0:T(8,128)(2,1)} broadcast(bf16[8,2,16,1024]{3,2,1,0:T(8,128)(2,1)} %all-to-all-done), dimensions={1,2,3,4} | broadcast | bytes 2621440 | tf_op jit(solution)/shard_map/broadcast_in_dim | solution.py:36
  37.5 4.7 %all-to-all-start.1 = ((bf16[4,8,2,16,1024]{4,3,2,1,0:T(8,128)(2,1)}), bf16[4,8,2,16,1024]{4,3,2,1,0:T(8,128)(2,1)}, u32[]{:S(2)}, u32[]{:S(2)}) async-start(bf16[4,8,2,16,1024]{4,3,2,1,0:T(8,128)(2,1)} %broadcast_in_dim.39), calls=%async_computation.1 | async-start | bytes 4194304 | tf_op jit(solution)/shard_map/all_to_all | solution.py:31
  42.5 1.8 collective-permute-start.2
  44.3 1.5 collective-permute-done.2
  46.0 28.8 %all-to-all-done.1 = bf16[4,8,2,16,1024]{4,3,2,1,0:T(8,128)(2,1)} async-done(((bf16[4,8,2,16,1024]{4,3,2,1,0:T(8,128)(2,1)}), bf16[4,8,2,16,1024]{4,3,2,1,0:T(8,128)(2,1)}, u32[]{:S(2)}, u32[]{:S(2)}) %all-to-all-start.1) | async-done | bytes 2097184 | tf_op jit(solution)/shard_map/all_to_all | solution.py:31
  76.0 2.4 collective-permute-start.4
  78.4 1.8 collective-permute-start.3
  80.5 9.4 %collective-permute-done.5 = bf16[2,128,1024]{2,1,0:T(8,128)(2,1)} collective-permute-done((bf16[2,128,1024]{2,1,0:T(8,128)(2,1)S(1)}, bf16[2,128,1024]{2,1,0:T(8,128)(2,1)}, u32[]{:S(2)}, u32[]{:S(2)}) %collective-permute-start.5) | collective-permute-done | bytes 524320 | tf_op jit(solution)/shard_map/ppermute | solution.py:21
  89.9 1.1 slice_bitcast_fusion.3
  91.0 11.1 %collective-permute-done.4 = bf16[2,128,1024]{2,1,0:T(8,128)(2,1)} collective-permute-done((bf16[2,128,1024]{2,1,0:T(8,128)(2,1)S(1)}, bf16[2,128,1024]{2,1,0:T(8,128)(2,1)}, u32[]{:S(2)}, u32[]{:S(2)}) %collective-permute-start.4) | collective-permute-done | bytes 524320 | tf_op jit(solution)/shard_map/ppermute | solution.py:21
  102.1 1.1 slice_bitcast_fusion.4
  103.2 2.7 %broadcast_select_fusion.3 = (bf16[4,8,1,16,1024]{4,3,2,1,0:T(8,128)(2,1)S(1)}, bf16[4,8,1,16,1024]{4,3,2,1,0:T(8,128)(2,1)S(1)}, bf16[4,8,1,16,1024]{4,3,2,1,0:T(8,128)(2,1)S(1)}, bf16[4,8,1,16,1024]{4,3,2,1,0:T(8,128)(2,1)S(1)}) fusion(pred[]{:T(512)S(6)} %eq.7, bf16[4,8,2,16,1024]{4,3,2,1,0:T(8,128)(2,1)} %collective-permute-done.6, ...), kind=kLoop, calls=%fused_computation.208 | loop fusion | flops 2097152 | bytes 8388609 | tf_op jit(solution)/shard_map/jit(_where)/select_n | solution.py:52
  106.4 1.3 fusion.119
  107.7 1.7 multiply_convert_fusion.2
  109.5 1.3 fusion.131
  110.8 1.1 collective-permute-start.9
  111.9 3.3 %collective-permute-start.8 = (bf16[128,1024]{1,0:T(8,128)(2,1)S(1)}, bf16[128,1024]{1,0:T(8,128)(2,1)S(1)}, u32[]{:S(2)}, u32[]{:S(2)}) collective-permute-start(bf16[128,1024]{1,0:T(8,128)(2,1)S(1)} %get-tuple-element.58), channel_id=1, source_target_pairs={{0,2},{1,3},{2,0},{3,1},{4,6},{5,7},{6,4},{7,5},{8,10},{9,11},{10,... | collective-permute-start | bytes 786440 | tf_op jit(solution)/shard_map/ppermute | solution.py:21
  115.3 2.0 collective-permute-start.7
  117.2 3.1 %collective-permute-done.9 = bf16[128,1024]{1,0:T(8,128)(2,1)S(1)} collective-permute-done((bf16[128,1024]{1,0:T(8,128)(2,1)S(1)}, bf16[128,1024]{1,0:T(8,128)(2,1)S(1)}, u32[]{:S(2)}, u32[]{:S(2)}) %collective-permute-start.9) | collective-permute-done | bytes 262176 | tf_op jit(solution)/shard_map/ppermute | solution.py:21
  120.4 2.3 collective-permute-done.8
  122.7 4.4 %collective-permute-done.7 = bf16[128,1024]{1,0:T(8,128)(2,1)S(1)} collective-permute-done((bf16[128,1024]{1,0:T(8,128)(2,1)S(1)}, bf16[128,1024]{1,0:T(8,128)(2,1)S(1)}, u32[]{:S(2)}, u32[]{:S(2)}) %collective-permute-start.7) | collective-permute-done | bytes 262176 | tf_op jit(solution)/shard_map/ppermute | solution.py:21
  127.8 1.3 collective-permute-start.10
  129.1 2.1 collective-permute-done.10
  131.2 3.9 %scatter_custom_fusion = f32[256,1024]{1,0:T(8,128)} fusion(s32[256]{0:T(256)} %bitcast.298, bf16[128,1024]{1,0:T(8,128)(2,1)S(1)} %collective-permute-done.10, bf16[]{:T(256)} %constant.136, bf16[128,1024]{1,0:T(8,128)(2,1)S(1)} %broadcast_select_fusion.5, f32[]{:T(128)} %constant.98.clone.1, pred[256]{0:T(512)(128)(4,1)S(1)} %copy-done.55), kind=kCustom, calls=%fused_computation.236 | custom fusion | flops 1572864 | bytes 1574656 | tf_op jit(solution)/shard_map/scatter-add | solution.py:162
  135.1 4.6 %multiply_reduce_fusion = (f32[1024]{0:T(1024)S(1)}, f32[1024]{0:T(1024)S(1)}, f32[1024]{0:T(1024)S(1)}, f32[1024]{0:T(1024)}, f32[1024]{0:T(1024)}, /*index=5*/...) fusion(f32[286,1024]{1,0:T(8,128)S(1)} %maximum_convert_fusion,, ...), kind=kLoop, calls=%fused_computation.163 | loop fusion | flops 11515904 | bytes 22093824 | tf_op jit(solution)/shard_map/reduce_sum | solution.py:167
  139.8 2.4 multiply_reduce_fusion.1
  142.2 3.1 %stack.200 = f32[32,1024]{1,0:T(8,128)S(1)} concatenate(f32[1,1024]{1,0:T(1,128)} %bitcast.296, f32[1,1024]{1,0:T(1,128)} %bitcast.295, f32[1,1024]{1,0:T(1,128)} %bitcast.294, f32[1,1024]{1,0:T(1,128)} %bitcast.293, f32[1,1024]{1,0:T(1,128)} %bitcast.292, f32[1,1024]{1,0:T(1,128)} %bitcast.291, f32[1,1024]{1,0:T(1,128)} %bitcast.290, f32[1,1024]{1,0:T(1,128)} %bitcast.289, ...), dimensions={0} | concatenate | bytes 262144 | tf_op jit(solution)/shard_map/stack | solution.py:176
  146.0 9.6 %all-to-all-start.3 = ((f32[8,8,512]{2,1,0:T(8,128)}), f32[8,8,512]{2,1,0:T(8,128)S(1)}, u32[]{:S(2)}, u32[]{:S(2)}) async-start(f32[8,8,512]{2,1,0:T(8,128)} %reshape.130), calls=%async_computation.3 | async-start | bytes 262144 | tf_op jit(solution)/shard_map/all_to_all | solution.py:31
  155.6 4.3 %multiply_convert_fusion = bf16[1024,1024]{1,0:T(8,128)(2,1)} fusion(f32[512,1024]{1,0:T(8,128)} %copy-done.59, bf16[128,1024]{1,0:T(8,128)(2,1)S(1)} %copy-done.12, bf16[128,1024]{1,0:T(8,128)(2,1)S(1)} %copy-done.14, bf16[128,1024]{1,0:T(8,128)(2,1)} %copy-done.15, bf16[128,1024]{1,0:T(8,128)(2,1)S(1)} %get-tuple-element.59), kind=kOutput, calls=%fused_computation.32 | convolution fusion | flops 1082654720 | bytes 5242880 | tf_op jit(solution)/shard_map/dot_general | solution.py:142
  160.0 0.9 broadcast_in_dim.41
  160.9 3.9 %all-to-all-start.4 = ((f32[32,8,512]{2,1,0:T(8,128)}), f32[32,8,512]{2,1,0:T(8,128)S(1)}, u32[]{:S(2)}, u32[]{:S(2)}) async-start(f32[32,8,512]{2,1,0:T(8,128)} %broadcast_in_dim.41), calls=%async_computation.4 | async-start | bytes 1048576 | tf_op jit(solution)/shard_map/all_to_all | solution.py:31
  164.8 2.7 %convolution_convert_fusion = bf16[1024,1024]{1,0:T(8,128)(2,1)S(1)} fusion(bf16[512,1024]{1,0:T(8,128)(2,1)} %copy-done.58, bf16[128,1024]{1,0:T(8,128)(2,1)S(1)} %copy-done.7, bf16[128,1024]{1,0:T(8,128)(2,1)S(1)} %copy-done.9, bf16[128,1024]{1,0:T(8,128)(2,1)} %copy-done.10, bf16[128,1024]{1,0:T(8,128)(2,1)S(1)} %copy-done.5), kind=kOutput, calls=%fused_computation.39 | convolution fusion | flops 1078984704 | bytes 4194304 | tf_op jit(solution)/shard_map/dot_general | solution.py:143
  167.8 1.3 dynamic-slice_bitcast_fusion.3
  169.0 1.5 pad_maximum_fusion.2
  170.6 11.5 %all-to-all-done.4 = f32[32,8,512]{2,1,0:T(8,128)S(1)} async-done(((f32[32,8,512]{2,1,0:T(8,128)}), f32[32,8,512]{2,1,0:T(8,128)S(1)}, u32[]{:S(2)}, u32[]{:S(2)}) %all-to-all-start.4) | async-done | bytes 524320 | tf_op jit(solution)/shard_map/all_to_all | solution.py:31
  182.1 1.2 collective-permute-start.17
  183.9 1.3 collective-permute-start.12
  185.2 1.3 collective-permute-start.11
  186.5 1.8 collective-permute-start.18
  188.3 1.8 collective-permute-start.19
  190.1 1.8 collective-permute-done.18
  192.1 2.9 %add_convert_fusion = bf16[4,16,16,1024]{3,2,1,0:T(8,128)(2,1)S(1)} fusion(bf16[4,16,16,1024]{3,2,1,0:T(8,128)(2,1)} %collective-permute-done.13, bf16[4,8,16,1024]{3,2,1,0:T(8,128)(2,1)S(1)} %get-tuple-element.52, bf16[4,8,16,1024]{3,2,1,0:T(8,128)(2,1)} %get-tuple-element.50), kind=kLoop, calls=%fused_computation.31 | loop fusion | flops 5242880 | bytes 6291456 | tf_op jit(solution)/shard_map/convert_element_type | solution.py:63
  195.1 6.4 %collective-permute-start.16 = (bf16[16,16,1024]{2,1,0:T(8,128)(2,1)S(1)}, bf16[16,16,1024]{2,1,0:T(8,128)(2,1)S(1)}, u32[]{:S(2)}, u32[]{:S(2)}) collective-permute-start(bf16[16,16,1024]{2,1,0:T(8,128)(2,1)S(1)} %get-tuple-element.48), channel_id=1, source_target_pairs={{0,192},{64,0},{128,64},{192,128},{1,193},{65,1},{129,65},{193,129... | collective-permute-start | bytes 1572872 | tf_op jit(solution)/shard_map/ppermute | solution.py:21
  201.6 1.4 collective-permute-start.15
  203.3 10.4 %collective-permute-done.16 = bf16[16,16,1024]{2,1,0:T(8,128)(2,1)S(1)} collective-permute-done((bf16[16,16,1024]{2,1,0:T(8,128)(2,1)S(1)}, bf16[16,16,1024]{2,1,0:T(8,128)(2,1)S(1)}, u32[]{:S(2)}, u32[]{:S(2)}) %collective-permute-start.16) | collective-permute-done | bytes 524320 | tf_op jit(solution)/shard_map/ppermute | solution.py:21
  213.7 4.2 %collective-permute-done.15 = bf16[16,16,1024]{2,1,0:T(8,128)(2,1)S(1)} collective-permute-done((bf16[16,16,1024]{2,1,0:T(8,128)(2,1)S(1)}, bf16[16,16,1024]{2,1,0:T(8,128)(2,1)S(1)}, u32[]{:S(2)}, u32[]{:S(2)}) %collective-permute-start.15) | collective-permute-done | bytes 524320 | tf_op jit(solution)/shard_map/ppermute | solution.py:21
  217.8 7.5 %collective-permute-done.14 = bf16[16,16,1024]{2,1,0:T(8,128)(2,1)S(1)} collective-permute-done((bf16[16,16,1024]{2,1,0:T(8,128)(2,1)S(1)}, bf16[16,16,1024]{2,1,0:T(8,128)(2,1)S(1)}, u32[]{:S(2)}, u32[]{:S(2)}) %collective-permute-start.14) | collective-permute-done | bytes 524320 | tf_op jit(solution)/shard_map/ppermute | solution.py:21
  225.7 0.8 copy.14
  226.5 3.5 %all-to-all-start.2 = ((bf16[8,2,16,1024]{3,2,1,0:T(8,128)(2,1)}), bf16[8,2,16,1024]{3,2,1,0:T(8,128)(2,1)S(1)}, u32[]{:S(2)}, u32[]{:S(2)}) async-start(bf16[8,2,16,1024]{3,2,1,0:T(8,128)(2,1)} %copy.14), calls=%async_computation.2 | async-start | bytes 1048576 | tf_op jit(solution)/shard_map/all_to_all | solution.py:31
  230.1 6.6 %fusion.118 = bf16[1,256,1024]{2,1,0:T(8,128)(2,1)} fusion(f32[256,1024]{1,0:T(8,128)S(1)} %copy-done.1, f32[256,1024]{1,0:T(8,128)S(1)} %get-tuple-element.39, f32[15,1024]{1,0:T(8,128)S(1)} %collective-permute-done.12, f32[1024]{0:T(1024)} %bitcast.222, f32[1024]{0:T(1024)} %bitcast.224, f32[1024]{0:T(1024)} %bitcast.228, f32[1024]{0:T(1024)} %bitcast.230, ...), kind=kLoop, calls=%fused_computation.244 | loop fusion | flops 24379392 | bytes 2871296 | tf_op jit(solution)/shard_map/broadcast_in_dim | solution.py:174
  236.7 0.9 select_bitcast_fusion.1
  238.3 9.6 %all-to-all-done.2 = bf16[8,2,16,1024]{3,2,1,0:T(8,128)(2,1)S(1)} async-done(((bf16[8,2,16,1024]{3,2,1,0:T(8,128)(2,1)}), bf16[8,2,16,1024]{3,2,1,0:T(8,128)(2,1)S(1)}, u32[]{:S(2)}, u32[]{:S(2)}) %all-to-all-start.2) | async-done | bytes 524320 | tf_op jit(solution)/shard_map/all_to_all | solution.py:31
  (182 shorter events, 9.5 us)
Async XLA Ops:
  0.6 20.7 %copy-start = (bf16[1,256,1024]{2,1,0:T(8,128)(2,1)S(1)}, bf16[1,256,1024]{2,1,0:T(8,128)(2,1)}, u32[]{:S(2)}) copy-start(bf16[1,256,1024]{2,1,0:T(8,128)(2,1)} %param.9) | copy-start | bytes 1572868
  0.6 18.0 %copy-start.56 = (s32[1,256]{1,0:T(1,128)S(1)}, s32[1,256]{1,0:T(1,128)}, u32[]{:S(2)}) copy-start(s32[1,256]{1,0:T(1,128)} %param.15) | copy-start | bytes 3076
  0.7 18.1 %copy-start.57 = (s32[1,64]{1,0:T(1,128)S(1)}, s32[1,64]{1,0:T(1,128)}, u32[]{:S(2)}) copy-start(s32[1,64]{1,0:T(1,128)} %param.14) | copy-start | bytes 772
  1.5 21.0 %collective-permute-start.1 = (bf16[15,1024]{1,0:T(8,128)(2,1)S(1)}, bf16[15,1024]{1,0:T(8,128)(2,1)S(1)}, u32[]{:S(2)}, u32[]{:S(2)}) collective-permute-start(bf16[15,1024]{1,0:T(8,128)(2,1)S(1)} %get-tuple-element.68), channel_id=1, source_target_pairs={{4,0},{8,4},{12,8},{16,12},{20,16},{24,20},{28,24},{32,28},{36,32}... | collective-permute-start | bytes 92168 | tf_op jit(solution)/shard_map/ppermute | solution.py:16
  2.8 19.7 %collective-permute-start = (bf16[15,1024]{1,0:T(8,128)(2,1)S(1)}, bf16[15,1024]{1,0:T(8,128)(2,1)S(1)}, u32[]{:S(2)}, u32[]{:S(2)}) collective-permute-start(bf16[15,1024]{1,0:T(8,128)(2,1)S(1)} %get-tuple-element.67), channel_id=1, source_target_pairs={{0,4},{4,8},{8,12},{12,16},{16,20},{20,24},{24,28},{28,32},{32,36}... | collective-permute-start | bytes 92168 | tf_op jit(solution)/shard_map/ppermute | solution.py:16
  7.5 27.4 %all-to-all-start = ((bf16[8,2,16,1024]{3,2,1,0:T(8,128)(2,1)}), bf16[8,2,16,1024]{3,2,1,0:T(8,128)(2,1)}, u32[]{:S(2)}, u32[]{:S(2)}) async-start(bf16[8,2,16,1024]{3,2,1,0:T(8,128)(2,1)} %broadcast_in_dim.38), calls=%async_computation | async-start | bytes 1048576 | tf_op jit(solution)/shard_map/all_to_all | solution.py:31
  17.1 5.6 %copy-start.18 = (f32[1,1024]{1,0:T(1,128)}, f32[1,1024]{1,0:T(1,128)S(1)}, u32[]{:S(2)}) copy-start(f32[1,1024]{1,0:T(1,128)S(1)} %get-tuple-element.92) | copy-start | bytes 12292
  17.1 5.6 %copy-start.20 = (f32[1,1024]{1,0:T(1,128)}, f32[1,1024]{1,0:T(1,128)S(1)}, u32[]{:S(2)}) copy-start(f32[1,1024]{1,0:T(1,128)S(1)} %get-tuple-element.93) | copy-start | bytes 12292
  17.1 5.6 %copy-start.22 = (f32[1,1024]{1,0:T(1,128)}, f32[1,1024]{1,0:T(1,128)S(1)}, u32[]{:S(2)}) copy-start(f32[1,1024]{1,0:T(1,128)S(1)} %get-tuple-element.94) | copy-start | bytes 12292
  17.1 5.6 %copy-start.24 = (f32[1,1024]{1,0:T(1,128)}, f32[1,1024]{1,0:T(1,128)S(1)}, u32[]{:S(2)}) copy-start(f32[1,1024]{1,0:T(1,128)S(1)} %get-tuple-element.95) | copy-start | bytes 12292
  17.1 5.6 %copy-start.26 = (f32[1,1024]{1,0:T(1,128)}, f32[1,1024]{1,0:T(1,128)S(1)}, u32[]{:S(2)}) copy-start(f32[1,1024]{1,0:T(1,128)S(1)} %get-tuple-element.96) | copy-start | bytes 12292
  17.2 5.6 %copy-start.27 = (f32[1,1024]{1,0:T(1,128)}, f32[1,1024]{1,0:T(1,128)S(1)}, u32[]{:S(2)}) copy-start(f32[1,1024]{1,0:T(1,128)S(1)} %get-tuple-element.97) | copy-start | bytes 12292
  17.2 5.6 %copy-start.28 = (f32[1,1024]{1,0:T(1,128)}, f32[1,1024]{1,0:T(1,128)S(1)}, u32[]{:S(2)}) copy-start(f32[1,1024]{1,0:T(1,128)S(1)} %get-tuple-element.98) | copy-start | bytes 12292
  17.2 5.6 %copy-start.29 = (f32[1,1024]{1,0:T(1,128)}, f32[1,1024]{1,0:T(1,128)S(1)}, u32[]{:S(2)}) copy-start(f32[1,1024]{1,0:T(1,128)S(1)} %get-tuple-element.99) | copy-start | bytes 12292
  17.2 5.6 %copy-start.30 = (f32[1,1024]{1,0:T(1,128)}, f32[1,1024]{1,0:T(1,128)S(1)}, u32[]{:S(2)}) copy-start(f32[1,1024]{1,0:T(1,128)S(1)} %get-tuple-element.100) | copy-start | bytes 12292
  17.2 5.6 %copy-start.31 = (f32[1,1024]{1,0:T(1,128)}, f32[1,1024]{1,0:T(1,128)S(1)}, u32[]{:S(2)}) copy-start(f32[1,1024]{1,0:T(1,128)S(1)} %get-tuple-element.101) | copy-start | bytes 12292
  17.2 5.6 %copy-start.32 = (f32[1,1024]{1,0:T(1,128)}, f32[1,1024]{1,0:T(1,128)S(1)}, u32[]{:S(2)}) copy-start(f32[1,1024]{1,0:T(1,128)S(1)} %get-tuple-element.102) | copy-start | bytes 12292
  17.2 5.6 %copy-start.33 = (f32[1,1024]{1,0:T(1,128)}, f32[1,1024]{1,0:T(1,128)S(1)}, u32[]{:S(2)}) copy-start(f32[1,1024]{1,0:T(1,128)S(1)} %get-tuple-element.103) | copy-start | bytes 12292
  18.5 4.3 %copy-start.34 = (f32[1,1024]{1,0:T(1,128)}, f32[1,1024]{1,0:T(1,128)S(1)}, u32[]{:S(2)}) copy-start(f32[1,1024]{1,0:T(1,128)S(1)} %get-tuple-element.73) | copy-start | bytes 12292
  18.5 4.3 %copy-start.35 = (f32[1,1024]{1,0:T(1,128)}, f32[1,1024]{1,0:T(1,128)S(1)}, u32[]{:S(2)}) copy-start(f32[1,1024]{1,0:T(1,128)S(1)} %get-tuple-element.74) | copy-start | bytes 12292
  18.5 4.3 %copy-start.36 = (f32[1,1024]{1,0:T(1,128)}, f32[1,1024]{1,0:T(1,128)S(1)}, u32[]{:S(2)}) copy-start(f32[1,1024]{1,0:T(1,128)S(1)} %get-tuple-element.75) | copy-start | bytes 12292
  18.5 4.3 %copy-start.37 = (f32[1,1024]{1,0:T(1,128)}, f32[1,1024]{1,0:T(1,128)S(1)}, u32[]{:S(2)}) copy-start(f32[1,1024]{1,0:T(1,128)S(1)} %get-tuple-element.76) | copy-start | bytes 12292
  18.5 4.3 %copy-start.38 = (f32[1,1024]{1,0:T(1,128)}, f32[1,1024]{1,0:T(1,128)S(1)}, u32[]{:S(2)}) copy-start(f32[1,1024]{1,0:T(1,128)S(1)} %get-tuple-element.77) | copy-start | bytes 12292
  20.6 21.6 %copy-start.54 = (pred[256]{0:T(512)(128)(4,1)}, pred[256]{0:T(512)(128)(4,1)S(1)}, u32[]{:S(2)}) copy-start(pred[256]{0:T(512)(128)(4,1)S(1)} %iota_compare_fusion) | copy-start | bytes 772
  37.5 37.3 %all-to-all-start.1 = ((bf16[4,8,2,16,1024]{4,3,2,1,0:T(8,128)(2,1)}), bf16[4,8,2,16,1024]{4,3,2,1,0:T(8,128)(2,1)}, u32[]{:S(2)}, u32[]{:S(2)}) async-start(bf16[4,8,2,16,1024]{4,3,2,1,0:T(8,128)(2,1)} %broadcast_in_dim.39), calls=%async_computation.1 | async-start | bytes 4194304 | tf_op jit(solution)/shard_map/all_to_all | solution.py:31
  42.4 32.7 %copy-start.17 = (f32[1024]{0:T(1024)S(1)}, f32[1024]{0:T(1024)}, u32[]{:S(2)}) copy-start(f32[1024]{0:T(1024)} %param.11) | copy-start | bytes 12292
  42.5 3.3 %collective-permute-start.2 = (bf16[2,128,1024]{2,1,0:T(8,128)(2,1)S(1)}, bf16[2,128,1024]{2,1,0:T(8,128)(2,1)S(1)}, u32[]{:S(2)}, u32[]{:S(2)}) collective-permute-start(bf16[2,128,1024]{2,1,0:T(8,128)(2,1)S(1)} %slice_select_fusion), channel_id=1, source_target_pairs={{0,4},{4,8},{8,12},{12,16},{16,20},{20,24},{24,28},{28,32},{32,36}... | collective-permute-start | bytes 1572872 | tf_op jit(solution)/shard_map/ppermute | solution.py:16
  74.8 28.4 %collective-permute-start.6 = (bf16[4,8,2,16,1024]{4,3,2,1,0:T(8,128)(2,1)}, bf16[4,8,2,16,1024]{4,3,2,1,0:T(8,128)(2,1)}, u32[]{:S(2)}, u32[]{:S(2)}) collective-permute-start(bf16[4,8,2,16,1024]{4,3,2,1,0:T(8,128)(2,1)} %all-to-all-done.1), channel_id=1, source_target_pairs={{0,4},{4,0},{1,5},{5,1},{2,6},{6,2},{3,7},{7,3},{8,12},{12,8},{9,1... | collective-permute-start | bytes 6291464 | tf_op jit(solution)/shard_map/ppermute | solution.py:21
  75.4 14.5 %collective-permute-start.5 = (bf16[2,128,1024]{2,1,0:T(8,128)(2,1)S(1)}, bf16[2,128,1024]{2,1,0:T(8,128)(2,1)}, u32[]{:S(2)}, u32[]{:S(2)}) collective-permute-start(bf16[2,128,1024]{2,1,0:T(8,128)(2,1)S(1)} %pad_maximum_fusion.7), channel_id=1, source_target_pairs={{0,3},{1,0},{2,1},{3,2},{4,7},{5,4},{6,5},{7,6},{8,11},{9,8},{10,9... | collective-permute-start | bytes 1572872 | tf_op jit(solution)/shard_map/ppermute | solution.py:21
  76.0 26.1 %collective-permute-start.4 = (bf16[2,128,1024]{2,1,0:T(8,128)(2,1)S(1)}, bf16[2,128,1024]{2,1,0:T(8,128)(2,1)}, u32[]{:S(2)}, u32[]{:S(2)}) collective-permute-start(bf16[2,128,1024]{2,1,0:T(8,128)(2,1)S(1)} %pad_maximum_fusion.7), channel_id=1, source_target_pairs={{0,2},{1,3},{2,0},{3,1},{4,6},{5,7},{6,4},{7,5},{8,10},{9,11},{10,... | collective-permute-start | bytes 1572872 | tf_op jit(solution)/shard_map/ppermute | solution.py:21
  78.4 24.7 %collective-permute-start.3 = (bf16[2,128,1024]{2,1,0:T(8,128)(2,1)S(1)}, bf16[2,128,1024]{2,1,0:T(8,128)(2,1)S(1)}, u32[]{:S(2)}, u32[]{:S(2)}) collective-permute-start(bf16[2,128,1024]{2,1,0:T(8,128)(2,1)S(1)} %pad_maximum_fusion.7), channel_id=1, source_target_pairs={{0,1},{1,2},{2,3},{3,0},{4,5},{5,6},{6,7},{7,4},{8,9},{9,10},{10,1... | collective-permute-start | bytes 1572872 | tf_op jit(solution)/shard_map/ppermute | solution.py:21
  80.5 25.9 %copy-start.4 = (bf16[128,1024]{1,0:T(8,128)(2,1)}, bf16[128,1024]{1,0:T(8,128)(2,1)S(1)}, u32[]{:S(2)}) copy-start(bf16[128,1024]{1,0:T(8,128)(2,1)S(1)} %fusion.104) | copy-start | bytes 786436
  91.0 15.4 %copy-start.6 = (bf16[128,1024]{1,0:T(8,128)(2,1)}, bf16[128,1024]{1,0:T(8,128)(2,1)S(1)}, u32[]{:S(2)}) copy-start(bf16[128,1024]{1,0:T(8,128)(2,1)S(1)} %get-tuple-element.66) | copy-start | bytes 786436
  91.0 16.7 %copy-start.11 = (bf16[128,1024]{1,0:T(8,128)(2,1)}, bf16[128,1024]{1,0:T(8,128)(2,1)S(1)}, u32[]{:S(2)}) copy-start(bf16[128,1024]{1,0:T(8,128)(2,1)S(1)} %get-tuple-element.65) | copy-start | bytes 786436
  103.1 4.5 %copy-start.13 = (bf16[128,1024]{1,0:T(8,128)(2,1)}, bf16[128,1024]{1,0:T(8,128)(2,1)S(1)}, u32[]{:S(2)}) copy-start(bf16[128,1024]{1,0:T(8,128)(2,1)S(1)} %get-tuple-element.63) | copy-start | bytes 786436
  103.2 4.5 %copy-start.15 = (bf16[128,1024]{1,0:T(8,128)(2,1)}, bf16[128,1024]{1,0:T(8,128)(2,1)S(1)}, u32[]{:S(2)}) copy-start(bf16[128,1024]{1,0:T(8,128)(2,1)S(1)} %get-tuple-element.61) | copy-start | bytes 786436
  110.8 9.5 %collective-permute-start.9 = (bf16[128,1024]{1,0:T(8,128)(2,1)S(1)}, bf16[128,1024]{1,0:T(8,128)(2,1)S(1)}, u32[]{:S(2)}, u32[]{:S(2)}) collective-permute-start(bf16[128,1024]{1,0:T(8,128)(2,1)S(1)} %get-tuple-element.57), channel_id=1, source_target_pairs={{0,1},{1,2},{2,3},{3,0},{4,5},{5,6},{6,7},{7,4},{8,9},{9,10},{10,1... | collective-permute-start | bytes 786440 | tf_op jit(solution)/shard_map/ppermute | solution.py:21
  111.9 10.7 %collective-permute-start.8 = (bf16[128,1024]{1,0:T(8,128)(2,1)S(1)}, bf16[128,1024]{1,0:T(8,128)(2,1)S(1)}, u32[]{:S(2)}, u32[]{:S(2)}) collective-permute-start(bf16[128,1024]{1,0:T(8,128)(2,1)S(1)} %get-tuple-element.58), channel_id=1, source_target_pairs={{0,2},{1,3},{2,0},{3,1},{4,6},{5,7},{6,4},{7,5},{8,10},{9,11},{10,... | collective-permute-start | bytes 786440 | tf_op jit(solution)/shard_map/ppermute | solution.py:21
  115.3 11.8 %collective-permute-start.7 = (bf16[128,1024]{1,0:T(8,128)(2,1)S(1)}, bf16[128,1024]{1,0:T(8,128)(2,1)S(1)}, u32[]{:S(2)}, u32[]{:S(2)}) collective-permute-start(bf16[128,1024]{1,0:T(8,128)(2,1)S(1)} %get-tuple-element.56), channel_id=1, source_target_pairs={{0,3},{1,0},{2,1},{3,2},{4,7},{5,4},{6,5},{7,6},{8,11},{9,8},{10,9... | collective-permute-start | bytes 786440 | tf_op jit(solution)/shard_map/ppermute | solution.py:21
  127.8 3.4 %collective-permute-start.10 = (bf16[128,1024]{1,0:T(8,128)(2,1)S(1)}, bf16[128,1024]{1,0:T(8,128)(2,1)S(1)}, u32[]{:S(2)}, u32[]{:S(2)}) collective-permute-start(bf16[128,1024]{1,0:T(8,128)(2,1)S(1)} %fusion.109), channel_id=1, source_target_pairs={{4,0},{8,4},{12,8},{16,12},{20,16},{24,20},{28,24},{32,28},{36,32}... | collective-permute-start | bytes 786440 | tf_op jit(solution)/shard_map/ppermute | solution.py:16
  139.8 15.8 %copy-start.12 = (bf16[128,1024]{1,0:T(8,128)(2,1)S(1)}, bf16[128,1024]{1,0:T(8,128)(2,1)}, u32[]{:S(2)}) copy-start(bf16[128,1024]{1,0:T(8,128)(2,1)} %copy-done.11) | copy-start | bytes 786436
  139.8 15.8 %copy-start.14 = (bf16[128,1024]{1,0:T(8,128)(2,1)S(1)}, bf16[128,1024]{1,0:T(8,128)(2,1)}, u32[]{:S(2)}) copy-start(bf16[128,1024]{1,0:T(8,128)(2,1)} %copy-done.13) | copy-start | bytes 786436
  146.0 14.0 %all-to-all-start.3 = ((f32[8,8,512]{2,1,0:T(8,128)}), f32[8,8,512]{2,1,0:T(8,128)S(1)}, u32[]{:S(2)}, u32[]{:S(2)}) async-start(f32[8,8,512]{2,1,0:T(8,128)} %reshape.130), calls=%async_computation.3 | async-start | bytes 262144 | tf_op jit(solution)/shard_map/all_to_all | solution.py:31
  155.5 9.2 %copy-start.5 = (bf16[128,1024]{1,0:T(8,128)(2,1)S(1)}, bf16[128,1024]{1,0:T(8,128)(2,1)}, u32[]{:S(2)}) copy-start(bf16[128,1024]{1,0:T(8,128)(2,1)} %copy-done.4) | copy-start | bytes 786436
  155.6 9.2 %copy-start.7 = (bf16[128,1024]{1,0:T(8,128)(2,1)S(1)}, bf16[128,1024]{1,0:T(8,128)(2,1)}, u32[]{:S(2)}) copy-start(bf16[128,1024]{1,0:T(8,128)(2,1)} %copy-done.6) | copy-start | bytes 786436
  155.6 9.2 %copy-start.9 = (bf16[128,1024]{1,0:T(8,128)(2,1)S(1)}, bf16[128,1024]{1,0:T(8,128)(2,1)}, u32[]{:S(2)}) copy-start(bf16[128,1024]{1,0:T(8,128)(2,1)} %copy-done.8) | copy-start | bytes 786436
  160.9 21.2 %all-to-all-start.4 = ((f32[32,8,512]{2,1,0:T(8,128)}), f32[32,8,512]{2,1,0:T(8,128)S(1)}, u32[]{:S(2)}, u32[]{:S(2)}) async-start(f32[32,8,512]{2,1,0:T(8,128)} %broadcast_in_dim.41), calls=%async_computation.4 | async-start | bytes 1048576 | tf_op jit(solution)/shard_map/all_to_all | solution.py:31
  170.5 21.6 %collective-permute-start.13 = (bf16[4,16,16,1024]{3,2,1,0:T(8,128)(2,1)}, bf16[4,16,16,1024]{3,2,1,0:T(8,128)(2,1)}, u32[]{:S(2)}, u32[]{:S(2)}) collective-permute-start(bf16[4,16,16,1024]{3,2,1,0:T(8,128)(2,1)} %pad_maximum_fusion.2), channel_id=1, source_target_pairs={{0,4},{4,0},{1,5},{5,1},{2,6},{6,2},{3,7},{7,3},{8,12},{12,8},{9,1... | collective-permute-start | bytes 6291464 | tf_op jit(solution)/shard_map/ppermute | solution.py:21
  182.1 6.2 %collective-permute-start.17 = (f32[8,512]{1,0:T(8,128)S(1)}, f32[8,512]{1,0:T(8,128)S(1)}, u32[]{:S(2)}, u32[]{:S(2)}) collective-permute-start(f32[8,512]{1,0:T(8,128)S(1)} %reduce_sum.399), channel_id=1, source_target_pairs={{0,3},{1,0},{2,1},{3,2},{4,7},{5,4},{6,5},{7,6},{8,11},{9,8},{10,9... | collective-permute-start | bytes 49160 | tf_op jit(solution)/shard_map/ppermute | solution.py:21
  183.9 46.1 %collective-permute-start.12 = (f32[15,1024]{1,0:T(8,128)}, f32[15,1024]{1,0:T(8,128)S(1)}, u32[]{:S(2)}, u32[]{:S(2)}) collective-permute-start(f32[15,1024]{1,0:T(8,128)} %get-tuple-element.55), channel_id=1, source_target_pairs={{0,4},{4,8},{8,12},{12,16},{16,20},{20,24},{24,28},{28,32},{32,36}... | collective-permute-start | bytes 184328 | tf_op jit(solution)/shard_map/ppermute | solution.py:16
  185.2 44.8 %collective-permute-start.11 = (f32[15,1024]{1,0:T(8,128)S(1)}, f32[15,1024]{1,0:T(8,128)S(1)}, u32[]{:S(2)}, u32[]{:S(2)}) collective-permute-start(f32[15,1024]{1,0:T(8,128)S(1)} %get-tuple-element.54), channel_id=1, source_target_pairs={{4,0},{8,4},{12,8},{16,12},{20,16},{24,20},{28,24},{32,28},{36,32}... | collective-permute-start | bytes 184328 | tf_op jit(solution)/shard_map/ppermute | solution.py:16
  186.5 5.3 %collective-permute-start.18 = (f32[8,512]{1,0:T(8,128)S(1)}, f32[8,512]{1,0:T(8,128)S(1)}, u32[]{:S(2)}, u32[]{:S(2)}) collective-permute-start(f32[8,512]{1,0:T(8,128)S(1)} %reduce_sum.399), channel_id=1, source_target_pairs={{0,2},{1,3},{2,0},{3,1},{4,6},{5,7},{6,4},{7,5},{8,10},{9,11},{10,... | collective-permute-start | bytes 49160 | tf_op jit(solution)/shard_map/ppermute | solution.py:21
  188.3 3.7 %collective-permute-start.19 = (f32[8,512]{1,0:T(8,128)S(1)}, f32[8,512]{1,0:T(8,128)S(1)}, u32[]{:S(2)}, u32[]{:S(2)}) collective-permute-start(f32[8,512]{1,0:T(8,128)S(1)} %reduce_sum.399), channel_id=1, source_target_pairs={{0,1},{1,2},{2,3},{3,0},{4,5},{5,6},{6,7},{7,4},{8,9},{9,10},{10,1... | collective-permute-start | bytes 49160 | tf_op jit(solution)/shard_map/ppermute | solution.py:21
  195.1 18.6 %collective-permute-start.16 = (bf16[16,16,1024]{2,1,0:T(8,128)(2,1)S(1)}, bf16[16,16,1024]{2,1,0:T(8,128)(2,1)S(1)}, u32[]{:S(2)}, u32[]{:S(2)}) collective-permute-start(bf16[16,16,1024]{2,1,0:T(8,128)(2,1)S(1)} %get-tuple-element.48), channel_id=1, source_target_pairs={{0,192},{64,0},{128,64},{192,128},{1,193},{65,1},{129,65},{193,129... | collective-permute-start | bytes 1572872 | tf_op jit(solution)/shard_map/ppermute | solution.py:21
  201.6 16.3 %collective-permute-start.15 = (bf16[16,16,1024]{2,1,0:T(8,128)(2,1)S(1)}, bf16[16,16,1024]{2,1,0:T(8,128)(2,1)S(1)}, u32[]{:S(2)}, u32[]{:S(2)}) collective-permute-start(bf16[16,16,1024]{2,1,0:T(8,128)(2,1)S(1)} %get-tuple-element.49), channel_id=1, source_target_pairs={{0,128},{64,192},{128,0},{192,64},{1,129},{65,193},{129,1},{193,65... | collective-permute-start | bytes 1572872 | tf_op jit(solution)/shard_map/ppermute | solution.py:21
  203.0 22.4 %collective-permute-start.14 = (bf16[16,16,1024]{2,1,0:T(8,128)(2,1)S(1)}, bf16[16,16,1024]{2,1,0:T(8,128)(2,1)S(1)}, u32[]{:S(2)}, u32[]{:S(2)}) collective-permute-start(bf16[16,16,1024]{2,1,0:T(8,128)(2,1)S(1)} %get-tuple-element.47), channel_id=1, source_target_pairs={{0,64},{64,128},{128,192},{192,0},{1,65},{65,129},{129,193},{193,1... | collective-permute-start | bytes 1572872 | tf_op jit(solution)/shard_map/ppermute | solution.py:21
  203.2 26.8 %copy-start.1 = (f32[256,1024]{1,0:T(8,128)S(1)}, f32[256,1024]{1,0:T(8,128)}, u32[]{:S(2)}) copy-start(f32[256,1024]{1,0:T(8,128)} %scatter_custom_fusion) | copy-start | bytes 3145732
  203.2 26.8 %copy-start.19 = (f32[1,1024]{1,0:T(1,128)S(1)}, f32[1,1024]{1,0:T(1,128)}, u32[]{:S(2)}) copy-start(f32[1,1024]{1,0:T(1,128)} %copy-done.18) | copy-start | bytes 12292
  203.2 26.8 %copy-start.21 = (f32[1,1024]{1,0:T(1,128)S(1)}, f32[1,1024]{1,0:T(1,128)}, u32[]{:S(2)}) copy-start(f32[1,1024]{1,0:T(1,128)} %copy-done.20) | copy-start | bytes 12292
  203.3 26.8 %copy-start.23 = (f32[1,1024]{1,0:T(1,128)S(1)}, f32[1,1024]{1,0:T(1,128)}, u32[]{:S(2)}) copy-start(f32[1,1024]{1,0:T(1,128)} %copy-done.22) | copy-start | bytes 12292
  203.3 26.8 %copy-start.25 = (f32[1,1024]{1,0:T(1,128)S(1)}, f32[1,1024]{1,0:T(1,128)}, u32[]{:S(2)}) copy-start(f32[1,1024]{1,0:T(1,128)} %copy-done.24) | copy-start | bytes 12292
  213.7 23.0 %collective-permute-start.20 = (f32[4,8,512]{2,1,0:T(8,128)S(1)}, f32[4,8,512]{2,1,0:T(8,128)}, u32[]{:S(2)}, u32[]{:S(2)}) collective-permute-start(f32[4,8,512]{2,1,0:T(8,128)S(1)} %constant_dynamic-slice_fusion), channel_id=1, source_target_pairs={{0,4},{4,0},{1,5},{5,1},{2,6},{6,2},{3,7},{7,3},{8,12},{12,8},{9,1... | collective-permute-start | bytes 196616 | tf_op jit(solution)/shard_map/ppermute | solution.py:21
  226.5 21.4 %all-to-all-start.2 = ((bf16[8,2,16,1024]{3,2,1,0:T(8,128)(2,1)}), bf16[8,2,16,1024]{3,2,1,0:T(8,128)(2,1)S(1)}, u32[]{:S(2)}, u32[]{:S(2)}) async-start(bf16[8,2,16,1024]{3,2,1,0:T(8,128)(2,1)} %copy.14), calls=%async_computation.2 | async-start | bytes 1048576 | tf_op jit(solution)/shard_map/all_to_all | solution.py:31
  237.6 11.0 %copy-start.16 = (f32[32,1024]{1,0:T(8,128)}, f32[32,1024]{1,0:T(8,128)S(1)}, u32[]{:S(2)}) copy-start(f32[32,1024]{1,0:T(8,128)S(1)} %reshape.131) | copy-start | bytes 393220
  (22 other events, 81.6 us)

commit v6 on v5

--- a/solution.py
+++ b/solution.py
@@ -38,6 +38,13 @@
 
 def pick(cells, which, axis):
     return lax.dynamic_index_in_dim(cells, which, axis, keepdims=False)
+
+
+def pick_one(cells, flags):
+    chosen = cells[0]
+    for cell, flag in zip(cells[1:], flags[1:]):
+        chosen = jnp.where(flag, cell, chosen)
+    return chosen
 
 
 def gather_weights(pair, core):
@@ -94,7 +101,8 @@
     late = before - shard > 0
     local_index = keep_index[0]
     valid = jnp.arange(length, dtype=jnp.int32) < counts[shard]
-    zero_bf = jnp.zeros((), bf16)
+    slots = jnp.arange(length, dtype=jnp.int32)
+    chosen = ((local_index[:, None] == slots[None, :]) & valid[:, None]).astype(bf16)
 
     def place(rows):
         going = jnp.where(late, rows[:, :BLOCK], rows[:, BLOCK:])
@@ -107,8 +115,13 @@
     for offset in range(tap_count):
         conv_out = conv_out + conv_kernel[offset] * wide32[offset : offset + length]
     hidden = (frames.astype(f32) + jax.nn.silu(conv_out)).astype(bf16)
-    kept = jnp.stack([hidden[local_index], cotangent[0][local_index]])
-    picked, picked_grad = place(jnp.where(valid[:, None], kept, zero_bf))
+    kept = jnp.stack(
+        [
+            jnp.dot(chosen, rows, preferred_element_type=f32).astype(bf16)
+            for rows in (hidden, cotangent[0])
+        ]
+    )
+    picked, picked_grad = place(kept)
     rows32 = picked.astype(f32)
     row_mean = jnp.mean(rows32, axis=1, keepdims=True)
     centred = rows32 - row_mean
@@ -155,11 +168,11 @@
     returned = shift(row_grad, SEQ, -1)
     low = jnp.where(late, returned, row_grad)
     high = returned
-    local_grad = jnp.concatenate([low, high]).astype(f32)
-    frame_grad = (
-        jnp.zeros((length, width), f32)
-        .at[local_index]
-        .add(jnp.where(valid[:, None], local_grad, 0.0))
+    frame_grad = lax.dot_general(
+        chosen,
+        jnp.concatenate([low, high]),
+        (((0,), (0,)), ((), ())),
+        preferred_element_type=f32,
     )
     conv_grad = frame_grad * silu_grad(conv_out)
     grad_wide = with_halo(conv_grad, half_width)
@@ -181,8 +194,9 @@
     part = jnp.sum(part, axis=0)
     me = lax.axis_index("utt")
     ring = [part] + [turn(part, "utt", by) for by in range(1, utts)]
-    ring = jnp.stack(ring[::-1] * 2)
-    ring = lax.dynamic_slice_in_dim(ring, utts - 1 - me, utts, 0)
+    ring = jnp.stack(
+        [pick_one(ring, [(me - j) % utts == k for k in range(utts)]) for j in range(utts)]
+    )
     other = turn(ring, "core", 1)
     full = [jnp.where(core == 0, ring, other), jnp.where(core == 0, other, ring)]
     full = jnp.stack(full).reshape(small.shape)

time: 253 us -> 232 us (0.917); the launches traced: 249 us -> 230 us
  starting transfers between devices: 64.3 us -> 51.3 us
  blocking collectives: 0 us -> 11.7 us
  other arithmetic: 35.5 us -> 26.1 us
  local copies, waits for them, and re-layouts: 21.2 us -> 13 us
    all_to_all x0 -> x1, blocking collectives: none -> 11.7 us  [exchange(): return lax.all_to_all(cells, axis, 0, 0, tiled=True)]
    all_to_all x5 -> x4, waiting for transfers between devices: 55.6 us -> 63.7 us  [exchange(): return lax.all_to_all(cells, axis, 0, 0, tiled=True)]
    all_to_all x5 -> x4, starting transfers between devices: 30.2 us -> 22.6 us  [exchange(): return lax.all_to_all(cells, axis, 0, 0, tiled=True)]
    ppermute x15, waiting for transfers between devices: 54.4 us -> 48.1 us  [turn(): lax.ppermute(cells, axis, [(i, (i + by) % count) for i in range(count)])]
    ppermute x15, starting transfers between devices: 24.2 us -> 18.5 us  [turn(): lax.ppermute(cells, axis, [(i, (i + by) % count) for i in range(count)])]
    dot_general x0 -> x3, matrix products: none -> 5.54 us  [the longest x1 3.95 us: per_device(): lax.dot_general(chosen, jnp.concatenate([low, high]), (((0,), (0,)), ((),...]
    reduce_sum x2 -> x1, other arithmetic: 7.03 us -> 1.74 us  [per_device(): jnp.sum(conv_grad * wide32[offset:offset + length], axis=0)]
    convert_element_type x1 -> x0, other arithmetic: 5.13 us -> none  [per_device(): hidden = (frames.astype(f32) + jax.nn.silu(conv_out)).astype(bf16)]
  transfers between devices with their start and end apart: 26 -> 25, of which waited for: 17 -> 13; matrix products, arithmetic and copies ran while one was open for 16% -> 17% of each run, Pallas kernels for 0% -> 0%
where the time goes in v6:
time: 232 us; the launch traced here: 230 us
  waiting for transfers between devices  113 us (49%)
  starting transfers between devices  51.3 us (22%)
  other arithmetic  26.1 us (11%)
  local copies, waits for them, and re-layouts  13 us (6%)
  matrix products  12.5 us (5%)
  blocking collectives  11.7 us (5%)
  between operations  2.37 us (1%)
    all_to_all x4, waiting for transfers between devices, exchange(): return lax.all_to_all(cells, axis, 0, 0, tiled=True)  63.7 us
    ppermute x15, waiting for transfers between devices, turn(): lax.ppermute(cells, axis, [(i, (i + by) % count) for i in range(count)])  48.1 us
    all_to_all x4, starting transfers between devices, exchange(): return lax.all_to_all(cells, axis, 0, 0, tiled=True)  22.6 us
    ppermute x15, starting transfers between devices, turn(): lax.ppermute(cells, axis, [(i, (i + by) % count) for i in range(count)])  18.5 us
    all_to_all x1, blocking collectives, exchange(): return lax.all_to_all(cells, axis, 0, 0, tiled=True)  11.7 us
    ppermute x6, starting transfers between devices, shift(): lax.ppermute(cells, axis, [(i, i + by) for i in range(count) if 0 <= i +...  10.2 us
    broadcast_in_dim x1, other arithmetic, per_device(): grad_x = (frame_grad + transposed).astype(bf16)[None]  6.6 us
  transfers between devices with their start and end apart: 25, of which 13 were waited for; matrix products, arithmetic and copies ran while one was open for 17% of the time, Pallas kernels for 0%

profile of v6, /device:TPU:2, one launch (start us, length us, event | category | flops | bytes accessed | tf_op | source)
XLA Modules:
  0.0 230.2 jit_solution(3209355680067230939)
XLA Ops:
  0.7 0.9 slice_bitcast_fusion.9
  1.5 1.3 collective-permute-start.1
  2.8 3.0 %collective-permute-start = (bf16[15,1024]{1,0:T(8,128)(2,1)S(1)}, bf16[15,1024]{1,0:T(8,128)(2,1)S(1)}, u32[]{:S(2)}, u32[]{:S(2)}) collective-permute-start(bf16[15,1024]{1,0:T(8,128)(2,1)S(1)} %get-tuple-element.65), channel_id=1, source_target_pairs={{0,4},{4,8},{8,12},{12,16},{16,20},{20,24},{24,28},{28,32},{32,36}... | collective-permute-start | bytes 92168 | tf_op jit(solution)/shard_map/ppermute | solution.py:16
  5.9 0.8 pad_maximum_fusion.14
  6.7 0.9 broadcast_in_dim.10
  7.5 8.5 %all-to-all-start = ((bf16[8,2,16,1024]{3,2,1,0:T(8,128)(2,1)}), bf16[8,2,16,1024]{3,2,1,0:T(8,128)(2,1)S(1)}, u32[]{:S(2)}, u32[]{:S(2)}) async-start(bf16[8,2,16,1024]{3,2,1,0:T(8,128)(2,1)} %broadcast_in_dim.10), calls=%async_computation | async-start | bytes 1048576 | tf_op jit(solution)/shard_map/all_to_all | solution.py:31
  16.0 1.2 constant_dynamic-slice_fusion
  17.2 0.6 iota_compare_fusion.1
  17.9 1.0 fusion.1
  19.3 0.6 fusion.135
  20.6 1.2 maximum_convert_fusion
  21.9 13.0 %all-to-all-done = bf16[8,2,16,1024]{3,2,1,0:T(8,128)(2,1)S(1)} async-done(((bf16[8,2,16,1024]{3,2,1,0:T(8,128)(2,1)}), bf16[8,2,16,1024]{3,2,1,0:T(8,128)(2,1)S(1)}, u32[]{:S(2)}, u32[]{:S(2)}) %all-to-all-start) | async-done | bytes 524320 | tf_op jit(solution)/shard_map/all_to_all | solution.py:31
  34.8 1.6 broadcast_in_dim.11
  36.4 4.5 %all-to-all-start.1 = ((bf16[4,8,2,16,1024]{4,3,2,1,0:T(8,128)(2,1)}), bf16[4,8,2,16,1024]{4,3,2,1,0:T(8,128)(2,1)}, u32[]{:S(2)}, u32[]{:S(2)}) async-start(bf16[4,8,2,16,1024]{4,3,2,1,0:T(8,128)(2,1)} %broadcast_in_dim.11), calls=%async_computation.1 | async-start | bytes 4194304 | tf_op jit(solution)/shard_map/all_to_all | solution.py:31
  41.1 4.0 %multiply_add_fusion = f32[256,1024]{1,0:T(8,128)S(1)} fusion(f32[286,1024]{1,0:T(8,128)S(1)} %maximum_convert_fusion, f32[1024]{0:T(1024)S(1)} %bitcast.219, f32[1024]{0:T(1024)S(1)} %bitcast.221, f32[1024]{0:T(1024)S(1)} %bitcast.225, f32[1024]{0:T(1024)S(1)} %bitcast.227, f32[1024]{0:T(1024)S(1)} %bitcast.229, f32[1024]{0:T(1024)S(1)} %bitcast.231, ...), kind=kLoop, calls=%fused_computation.205 | loop fusion | flops 15990784 | bytes 33681408 | tf_op jit(solution)/shard_map/add | solution.py:116
  46.4 2.1 collective-permute-start.2
  48.4 1.5 collective-permute-done.2
  50.1 23.3 %all-to-all-done.1 = bf16[4,8,2,16,1024]{4,3,2,1,0:T(8,128)(2,1)} async-done(((bf16[4,8,2,16,1024]{4,3,2,1,0:T(8,128)(2,1)}), bf16[4,8,2,16,1024]{4,3,2,1,0:T(8,128)(2,1)}, u32[]{:S(2)}, u32[]{:S(2)}) %all-to-all-start.1) | async-done | bytes 2097184 | tf_op jit(solution)/shard_map/all_to_all | solution.py:31
  74.0 0.8 pad_maximum_fusion.8
  75.3 2.4 %collective-permute-start.4 = (bf16[2,128,1024]{2,1,0:T(8,128)(2,1)}, bf16[2,128,1024]{2,1,0:T(8,128)(2,1)S(1)}, u32[]{:S(2)}, u32[]{:S(2)}) collective-permute-start(bf16[2,128,1024]{2,1,0:T(8,128)(2,1)} %pad_maximum_fusion.8), channel_id=1, source_target_pairs={{0,2},{1,3},{2,0},{3,1},{4,6},{5,7},{6,4},{7,5},{8,10},{9,11},{10,... | collective-permute-start | bytes 1572872 | tf_op jit(solution)/shard_map/ppermute | solution.py:21
  77.7 1.8 collective-permute-start.3
  79.8 9.7 %collective-permute-done.5 = bf16[2,128,1024]{2,1,0:T(8,128)(2,1)} collective-permute-done((bf16[2,128,1024]{2,1,0:T(8,128)(2,1)}, bf16[2,128,1024]{2,1,0:T(8,128)(2,1)}, u32[]{:S(2)}, u32[]{:S(2)}) %collective-permute-start.5) | collective-permute-done | bytes 524320 | tf_op jit(solution)/shard_map/ppermute | solution.py:21
  89.4 1.1 slice_bitcast_fusion.3
  90.5 11.0 %collective-permute-done.4 = bf16[2,128,1024]{2,1,0:T(8,128)(2,1)S(1)} collective-permute-done((bf16[2,128,1024]{2,1,0:T(8,128)(2,1)}, bf16[2,128,1024]{2,1,0:T(8,128)(2,1)S(1)}, u32[]{:S(2)}, u32[]{:S(2)}) %collective-permute-start.4) | collective-permute-done | bytes 524320 | tf_op jit(solution)/shard_map/ppermute | solution.py:21
  101.5 0.9 collective-permute-done.3
  102.5 2.5 %broadcast_select_fusion.3 = (bf16[4,8,1,16,1024]{4,3,2,1,0:T(8,128)(2,1)S(1)}, bf16[4,8,1,16,1024]{4,3,2,1,0:T(8,128)(2,1)S(1)}, bf16[4,8,1,16,1024]{4,3,2,1,0:T(8,128)(2,1)S(1)}, bf16[4,8,1,16,1024]{4,3,2,1,0:T(8,128)(2,1)S(1)}) fusion(pred[]{:T(512)S(6)} %eq.80, bf16[4,8,2,16,1024]{4,3,2,1,0:T(8,128)(2,1)} %collective-permute-done.6, ...), kind=kLoop, calls=%fused_computation.209 | loop fusion | flops 2097152 | bytes 8388609 | tf_op jit(solution)/shard_map/jit(_where)/select_n | solution.py:59
  105.3 1.3 fusion.128
  106.6 1.4 multiply_convert_fusion
  107.9 1.7 multiply_convert_fusion.2
  109.7 1.3 fusion.149
  111.0 1.5 collective-permute-start.9
  112.5 3.3 %collective-permute-start.8 = (bf16[128,1024]{1,0:T(8,128)(2,1)S(1)}, bf16[128,1024]{1,0:T(8,128)(2,1)S(1)}, u32[]{:S(2)}, u32[]{:S(2)}) collective-permute-start(bf16[128,1024]{1,0:T(8,128)(2,1)S(1)} %get-tuple-element.56), channel_id=1, source_target_pairs={{0,2},{1,3},{2,0},{3,1},{4,6},{5,7},{6,4},{7,5},{8,10},{9,11},{10,... | collective-permute-start | bytes 786440 | tf_op jit(solution)/shard_map/ppermute | solution.py:21
  115.9 0.6 collective-permute-start.7
  116.5 1.3 dynamic-slice_bitcast_fusion.2
  117.7 1.3 convolution_convert_fusion
  119.1 1.9 collective-permute-done.9
  121.0 2.3 collective-permute-done.8
  123.3 4.4 %collective-permute-done.7 = bf16[128,1024]{1,0:T(8,128)(2,1)S(1)} collective-permute-done((bf16[128,1024]{1,0:T(8,128)(2,1)S(1)}, bf16[128,1024]{1,0:T(8,128)(2,1)S(1)}, u32[]{:S(2)}, u32[]{:S(2)}) %collective-permute-start.7) | collective-permute-done | bytes 262176 | tf_op jit(solution)/shard_map/ppermute | solution.py:21
  128.4 1.3 collective-permute-start.10
  129.7 1.2 dynamic-slice_bitcast_fusion.3
  130.8 1.5 pad_maximum_fusion.2
  132.3 1.1 collective-permute-start.13
  133.5 4.0 %multiply_reduce_fusion = (f32[1024]{0:T(1024)S(1)}, f32[1024]{0:T(1024)S(1)}, f32[1024]{0:T(1024)S(1)}, f32[1024]{0:T(1024)S(1)}, f32[1024]{0:T(1024)S(1)}, /*i...) fusion(f32[286,1024]{1,0:T(8,128)S(1)} %maximum_convert_fusion,, ...), kind=kOutput, calls=%fused_computation.165 | convolution fusion | flops 146913280 | bytes 22619392 | tf_op jit(solution)/shard_map/dot_general | solution.py:171
  137.4 1.7 multiply_reduce_fusion.1
  139.5 11.7 %all_to_all.25 = f32[8,8,512]{2,1,0:T(8,128)S(1)} all-to-all(f32[8,8,512]{2,1,0:T(8,128)S(1)} %reshape.103), channel_id=1, replica_groups=mesh['y'=4,'z'=8,'core'=2,'utt'=4] {'core','utt'}, dimensions={0} | all-to-all | bytes 262144 | tf_op jit(solution)/shard_map/all_to_all | solution.py:31
  151.2 0.9 broadcast_in_dim.13
  152.1 3.9 %all-to-all-start.4 = ((f32[32,8,512]{2,1,0:T(8,128)}), f32[32,8,512]{2,1,0:T(8,128)S(1)}, u32[]{:S(2)}, u32[]{:S(2)}) async-start(f32[32,8,512]{2,1,0:T(8,128)} %broadcast_in_dim.13), calls=%async_computation.4 | async-start | bytes 1048576 | tf_op jit(solution)/shard_map/all_to_all | solution.py:31
  156.1 17.2 %all-to-all-done.4 = f32[32,8,512]{2,1,0:T(8,128)S(1)} async-done(((f32[32,8,512]{2,1,0:T(8,128)}), f32[32,8,512]{2,1,0:T(8,128)S(1)}, u32[]{:S(2)}, u32[]{:S(2)}) %all-to-all-start.4) | async-done | bytes 524320 | tf_op jit(solution)/shard_map/all_to_all | solution.py:31
  173.3 1.2 collective-permute-start.17
  175.1 2.0 collective-permute-start.19
  177.1 3.0 %add_convert_fusion = bf16[4,16,16,1024]{3,2,1,0:T(8,128)(2,1)S(1)} fusion(bf16[4,16,16,1024]{3,2,1,0:T(8,128)(2,1)} %collective-permute-done.13, bf16[4,8,16,1024]{3,2,1,0:T(8,128)(2,1)S(1)} %copy-done.1, bf16[4,8,16,1024]{3,2,1,0:T(8,128)(2,1)} %get-tuple-element.48), kind=kLoop, calls=%fused_computation.28 | loop fusion | flops 5242880 | bytes 6291456 | tf_op jit(solution)/shard_map/convert_element_type | solution.py:70
  180.3 1.7 collective-permute-start.16
  182.0 1.0 collective-permute-start.15
  183.6 0.6 fusion.145
  184.3 1.3 collective-permute-start.12
  185.6 1.3 collective-permute-start.11
  186.9 14.2 %collective-permute-done.16 = bf16[16,16,1024]{2,1,0:T(8,128)(2,1)S(1)} collective-permute-done((bf16[16,16,1024]{2,1,0:T(8,128)(2,1)S(1)}, bf16[16,16,1024]{2,1,0:T(8,128)(2,1)S(1)}, u32[]{:S(2)}, u32[]{:S(2)}) %collective-permute-start.16) | collective-permute-done | bytes 524320 | tf_op jit(solution)/shard_map/ppermute | solution.py:21
  201.2 3.7 %collective-permute-done.14 = bf16[16,16,1024]{2,1,0:T(8,128)(2,1)S(1)} collective-permute-done((bf16[16,16,1024]{2,1,0:T(8,128)(2,1)S(1)}, bf16[16,16,1024]{2,1,0:T(8,128)(2,1)S(1)}, u32[]{:S(2)}, u32[]{:S(2)}) %collective-permute-start.14) | collective-permute-done | bytes 524320 | tf_op jit(solution)/shard_map/ppermute | solution.py:21
  205.2 0.8 copy.14
  206.0 5.8 %all-to-all-start.2 = ((bf16[8,2,16,1024]{3,2,1,0:T(8,128)(2,1)}), bf16[8,2,16,1024]{3,2,1,0:T(8,128)(2,1)S(1)}, u32[]{:S(2)}, u32[]{:S(2)}) async-start(bf16[8,2,16,1024]{3,2,1,0:T(8,128)(2,1)} %copy.14), calls=%async_computation.2 | async-start | bytes 1048576 | tf_op jit(solution)/shard_map/all_to_all | solution.py:31
  211.8 6.6 %fusion.123 = bf16[1,256,1024]{2,1,0:T(8,128)(2,1)} fusion(f32[256,1024]{1,0:T(8,128)S(1)} %copy-done.4, f32[256,1024]{1,0:T(8,128)S(1)} %get-tuple-element.39, f32[15,1024]{1,0:T(8,128)S(1)} %collective-permute-done.12, f32[1024]{0:T(1024)} %bitcast.220, f32[1024]{0:T(1024)} %bitcast.222, f32[1024]{0:T(1024)} %bitcast.226, f32[1024]{0:T(1024)} %bitcast.228, ...), kind=kLoop, calls=%fused_computation.248 | loop fusion | flops 24379392 | bytes 2871296 | tf_op jit(solution)/shard_map/broadcast_in_dim | solution.py:187
  218.5 0.6 slice.670
  219.2 10.3 %all-to-all-done.2 = bf16[8,2,16,1024]{3,2,1,0:T(8,128)(2,1)S(1)} async-done(((bf16[8,2,16,1024]{3,2,1,0:T(8,128)(2,1)}), bf16[8,2,16,1024]{3,2,1,0:T(8,128)(2,1)S(1)}, u32[]{:S(2)}, u32[]{:S(2)}) %all-to-all-start.2) | async-done | bytes 524320 | tf_op jit(solution)/shard_map/all_to_all | solution.py:31
  229.6 0.7 slice_bitcast_fusion.6
  (126 shorter events, 6.3 us)
Async XLA Ops:
  0.6 17.2 %copy-start = (bf16[1,256,1024]{2,1,0:T(8,128)(2,1)S(1)}, bf16[1,256,1024]{2,1,0:T(8,128)(2,1)}, u32[]{:S(2)}) copy-start(bf16[1,256,1024]{2,1,0:T(8,128)(2,1)} %param.9) | copy-start | bytes 1572868
  0.6 18.5 %copy-start.37 = (s32[1,64]{1,0:T(1,128)S(1)}, s32[1,64]{1,0:T(1,128)}, u32[]{:S(2)}) copy-start(s32[1,64]{1,0:T(1,128)} %param.14) | copy-start | bytes 772
  0.7 18.3 %copy-start.7 = (f32[31,1024]{1,0:T(8,128)S(1)}, f32[31,1024]{1,0:T(8,128)}, u32[]{:S(2)}) copy-start(f32[31,1024]{1,0:T(8,128)} %param.10) | copy-start | bytes 380932
  1.5 19.1 %collective-permute-start.1 = (bf16[15,1024]{1,0:T(8,128)(2,1)S(1)}, bf16[15,1024]{1,0:T(8,128)(2,1)S(1)}, u32[]{:S(2)}, u32[]{:S(2)}) collective-permute-start(bf16[15,1024]{1,0:T(8,128)(2,1)S(1)} %get-tuple-element.66), channel_id=1, source_target_pairs={{4,0},{8,4},{12,8},{16,12},{20,16},{24,20},{28,24},{32,28},{36,32}... | collective-permute-start | bytes 92168 | tf_op jit(solution)/shard_map/ppermute | solution.py:16
  2.8 17.8 %collective-permute-start = (bf16[15,1024]{1,0:T(8,128)(2,1)S(1)}, bf16[15,1024]{1,0:T(8,128)(2,1)S(1)}, u32[]{:S(2)}, u32[]{:S(2)}) collective-permute-start(bf16[15,1024]{1,0:T(8,128)(2,1)S(1)} %get-tuple-element.65), channel_id=1, source_target_pairs={{0,4},{4,8},{8,12},{12,16},{16,20},{20,24},{24,28},{28,32},{32,36}... | collective-permute-start | bytes 92168 | tf_op jit(solution)/shard_map/ppermute | solution.py:16
  7.5 27.3 %all-to-all-start = ((bf16[8,2,16,1024]{3,2,1,0:T(8,128)(2,1)}), bf16[8,2,16,1024]{3,2,1,0:T(8,128)(2,1)S(1)}, u32[]{:S(2)}, u32[]{:S(2)}) async-start(bf16[8,2,16,1024]{3,2,1,0:T(8,128)(2,1)} %broadcast_in_dim.10), calls=%async_computation | async-start | bytes 1048576 | tf_op jit(solution)/shard_map/all_to_all | solution.py:31
  19.0 21.9 %copy-start.9 = (f32[1,1024]{1,0:T(1,128)}, f32[1,1024]{1,0:T(1,128)S(1)}, u32[]{:S(2)}) copy-start(f32[1,1024]{1,0:T(1,128)S(1)} %get-tuple-element.94) | copy-start | bytes 12292
  19.0 21.9 %copy-start.10 = (f32[1,1024]{1,0:T(1,128)}, f32[1,1024]{1,0:T(1,128)S(1)}, u32[]{:S(2)}) copy-start(f32[1,1024]{1,0:T(1,128)S(1)} %get-tuple-element.95) | copy-start | bytes 12292
  19.0 21.9 %copy-start.11 = (f32[1,1024]{1,0:T(1,128)}, f32[1,1024]{1,0:T(1,128)S(1)}, u32[]{:S(2)}) copy-start(f32[1,1024]{1,0:T(1,128)S(1)} %get-tuple-element.96) | copy-start | bytes 12292
  19.0 21.9 %copy-start.12 = (f32[1,1024]{1,0:T(1,128)}, f32[1,1024]{1,0:T(1,128)S(1)}, u32[]{:S(2)}) copy-start(f32[1,1024]{1,0:T(1,128)S(1)} %get-tuple-element.97) | copy-start | bytes 12292
  19.0 21.9 %copy-start.13 = (f32[1,1024]{1,0:T(1,128)}, f32[1,1024]{1,0:T(1,128)S(1)}, u32[]{:S(2)}) copy-start(f32[1,1024]{1,0:T(1,128)S(1)} %get-tuple-element.98) | copy-start | bytes 12292
  19.0 21.9 %copy-start.14 = (f32[1,1024]{1,0:T(1,128)}, f32[1,1024]{1,0:T(1,128)S(1)}, u32[]{:S(2)}) copy-start(f32[1,1024]{1,0:T(1,128)S(1)} %get-tuple-element.99) | copy-start | bytes 12292
  19.0 21.9 %copy-start.15 = (f32[1,1024]{1,0:T(1,128)}, f32[1,1024]{1,0:T(1,128)S(1)}, u32[]{:S(2)}) copy-start(f32[1,1024]{1,0:T(1,128)S(1)} %get-tuple-element.100) | copy-start | bytes 12292
  19.0 21.9 %copy-start.16 = (f32[1,1024]{1,0:T(1,128)}, f32[1,1024]{1,0:T(1,128)S(1)}, u32[]{:S(2)}) copy-start(f32[1,1024]{1,0:T(1,128)S(1)} %get-tuple-element.101) | copy-start | bytes 12292
  19.1 21.8 %copy-start.17 = (f32[1,1024]{1,0:T(1,128)}, f32[1,1024]{1,0:T(1,128)S(1)}, u32[]{:S(2)}) copy-start(f32[1,1024]{1,0:T(1,128)S(1)} %get-tuple-element.71) | copy-start | bytes 12292
  19.1 21.8 %copy-start.18 = (f32[1,1024]{1,0:T(1,128)}, f32[1,1024]{1,0:T(1,128)S(1)}, u32[]{:S(2)}) copy-start(f32[1,1024]{1,0:T(1,128)S(1)} %get-tuple-element.72) | copy-start | bytes 12292
  19.2 21.8 %copy-start.19 = (f32[1,1024]{1,0:T(1,128)}, f32[1,1024]{1,0:T(1,128)S(1)}, u32[]{:S(2)}) copy-start(f32[1,1024]{1,0:T(1,128)S(1)} %get-tuple-element.73) | copy-start | bytes 12292
  19.2 21.8 %copy-start.20 = (f32[1,1024]{1,0:T(1,128)}, f32[1,1024]{1,0:T(1,128)S(1)}, u32[]{:S(2)}) copy-start(f32[1,1024]{1,0:T(1,128)S(1)} %get-tuple-element.74) | copy-start | bytes 12292
  19.2 21.8 %copy-start.21 = (f32[1,1024]{1,0:T(1,128)}, f32[1,1024]{1,0:T(1,128)S(1)}, u32[]{:S(2)}) copy-start(f32[1,1024]{1,0:T(1,128)S(1)} %get-tuple-element.75) | copy-start | bytes 12292
  19.2 21.8 %copy-start.22 = (f32[1,1024]{1,0:T(1,128)}, f32[1,1024]{1,0:T(1,128)S(1)}, u32[]{:S(2)}) copy-start(f32[1,1024]{1,0:T(1,128)S(1)} %get-tuple-element.76) | copy-start | bytes 12292
  19.2 21.8 %copy-start.23 = (f32[1,1024]{1,0:T(1,128)}, f32[1,1024]{1,0:T(1,128)S(1)}, u32[]{:S(2)}) copy-start(f32[1,1024]{1,0:T(1,128)S(1)} %get-tuple-element.77) | copy-start | bytes 12292
  19.2 21.8 %copy-start.24 = (f32[1,1024]{1,0:T(1,128)}, f32[1,1024]{1,0:T(1,128)S(1)}, u32[]{:S(2)}) copy-start(f32[1,1024]{1,0:T(1,128)S(1)} %get-tuple-element.78) | copy-start | bytes 12292
  19.2 21.8 %copy-start.25 = (f32[1,1024]{1,0:T(1,128)}, f32[1,1024]{1,0:T(1,128)S(1)}, u32[]{:S(2)}) copy-start(f32[1,1024]{1,0:T(1,128)S(1)} %get-tuple-element.79) | copy-start | bytes 12292
  19.2 21.8 %copy-start.26 = (f32[1,1024]{1,0:T(1,128)}, f32[1,1024]{1,0:T(1,128)S(1)}, u32[]{:S(2)}) copy-start(f32[1,1024]{1,0:T(1,128)S(1)} %get-tuple-element.80) | copy-start | bytes 12292
  19.2 21.8 %copy-start.27 = (f32[1,1024]{1,0:T(1,128)}, f32[1,1024]{1,0:T(1,128)S(1)}, u32[]{:S(2)}) copy-start(f32[1,1024]{1,0:T(1,128)S(1)} %get-tuple-element.81) | copy-start | bytes 12292
  19.2 21.8 %copy-start.28 = (f32[1,1024]{1,0:T(1,128)}, f32[1,1024]{1,0:T(1,128)S(1)}, u32[]{:S(2)}) copy-start(f32[1,1024]{1,0:T(1,128)S(1)} %get-tuple-element.82) | copy-start | bytes 12292
  19.3 21.8 %copy-start.29 = (f32[1,1024]{1,0:T(1,128)}, f32[1,1024]{1,0:T(1,128)S(1)}, u32[]{:S(2)}) copy-start(f32[1,1024]{1,0:T(1,128)S(1)} %get-tuple-element.83) | copy-start | bytes 12292
  19.3 21.8 %copy-start.30 = (f32[1,1024]{1,0:T(1,128)}, f32[1,1024]{1,0:T(1,128)S(1)}, u32[]{:S(2)}) copy-start(f32[1,1024]{1,0:T(1,128)S(1)} %get-tuple-element.84) | copy-start | bytes 12292
  19.3 21.8 %copy-start.31 = (f32[1,1024]{1,0:T(1,128)}, f32[1,1024]{1,0:T(1,128)S(1)}, u32[]{:S(2)}) copy-start(f32[1,1024]{1,0:T(1,128)S(1)} %get-tuple-element.85) | copy-start | bytes 12292
  19.3 21.8 %copy-start.32 = (f32[1,1024]{1,0:T(1,128)}, f32[1,1024]{1,0:T(1,128)S(1)}, u32[]{:S(2)}) copy-start(f32[1,1024]{1,0:T(1,128)S(1)} %get-tuple-element.86) | copy-start | bytes 12292
  19.3 21.8 %copy-start.33 = (f32[1,1024]{1,0:T(1,128)}, f32[1,1024]{1,0:T(1,128)S(1)}, u32[]{:S(2)}) copy-start(f32[1,1024]{1,0:T(1,128)S(1)} %get-tuple-element.87) | copy-start | bytes 12292
  19.3 21.8 %copy-start.34 = (f32[1,1024]{1,0:T(1,128)}, f32[1,1024]{1,0:T(1,128)S(1)}, u32[]{:S(2)}) copy-start(f32[1,1024]{1,0:T(1,128)S(1)} %get-tuple-element.88) | copy-start | bytes 12292
  19.3 21.8 %copy-start.35 = (f32[1,1024]{1,0:T(1,128)}, f32[1,1024]{1,0:T(1,128)S(1)}, u32[]{:S(2)}) copy-start(f32[1,1024]{1,0:T(1,128)S(1)} %get-tuple-element.89) | copy-start | bytes 12292
  36.4 37.0 %all-to-all-start.1 = ((bf16[4,8,2,16,1024]{4,3,2,1,0:T(8,128)(2,1)}), bf16[4,8,2,16,1024]{4,3,2,1,0:T(8,128)(2,1)}, u32[]{:S(2)}, u32[]{:S(2)}) async-start(bf16[4,8,2,16,1024]{4,3,2,1,0:T(8,128)(2,1)} %broadcast_in_dim.11), calls=%async_computation.1 | async-start | bytes 4194304 | tf_op jit(solution)/shard_map/all_to_all | solution.py:31
  41.1 4.1 %copy-start.5 = (bf16[1,256,1024]{2,1,0:T(8,128)(2,1)S(1)}, bf16[1,256,1024]{2,1,0:T(8,128)(2,1)}, u32[]{:S(2)}) copy-start(bf16[1,256,1024]{2,1,0:T(8,128)(2,1)} %param.8) | copy-start | bytes 1572868
  41.1 4.1 %copy-start.36 = (s32[1,256]{1,0:T(1,128)S(1)}, s32[1,256]{1,0:T(1,128)}, u32[]{:S(2)}) copy-start(s32[1,256]{1,0:T(1,128)} %param.15) | copy-start | bytes 3076
  45.2 1.0 copy-start.2
  46.4 27.3 %copy-start.8 = (f32[1024]{0:T(1024)S(1)}, f32[1024]{0:T(1024)}, u32[]{:S(2)}) copy-start(f32[1024]{0:T(1024)} %param.11) | copy-start | bytes 12292
  46.4 3.5 %collective-permute-start.2 = (bf16[2,128,1024]{2,1,0:T(8,128)(2,1)S(1)}, bf16[2,128,1024]{2,1,0:T(8,128)(2,1)S(1)}, u32[]{:S(2)}, u32[]{:S(2)}) collective-permute-start(bf16[2,128,1024]{2,1,0:T(8,128)(2,1)S(1)} %fusion.117), channel_id=1, source_target_pairs={{0,4},{4,8},{8,12},{12,16},{16,20},{20,24},{24,28},{28,32},{32,36}... | collective-permute-start | bytes 1572872 | tf_op jit(solution)/shard_map/ppermute | solution.py:16
  73.4 29.0 %collective-permute-start.6 = (bf16[4,8,2,16,1024]{4,3,2,1,0:T(8,128)(2,1)}, bf16[4,8,2,16,1024]{4,3,2,1,0:T(8,128)(2,1)}, u32[]{:S(2)}, u32[]{:S(2)}) collective-permute-start(bf16[4,8,2,16,1024]{4,3,2,1,0:T(8,128)(2,1)} %all-to-all-done.1), channel_id=1, source_target_pairs={{0,4},{4,0},{1,5},{5,1},{2,6},{6,2},{3,7},{7,3},{8,12},{12,8},{9,1... | collective-permute-start | bytes 6291464 | tf_op jit(solution)/shard_map/ppermute | solution.py:21
  74.8 14.7 %collective-permute-start.5 = (bf16[2,128,1024]{2,1,0:T(8,128)(2,1)}, bf16[2,128,1024]{2,1,0:T(8,128)(2,1)}, u32[]{:S(2)}, u32[]{:S(2)}) collective-permute-start(bf16[2,128,1024]{2,1,0:T(8,128)(2,1)} %pad_maximum_fusion.8), channel_id=1, source_target_pairs={{0,3},{1,0},{2,1},{3,2},{4,7},{5,4},{6,5},{7,6},{8,11},{9,8},{10,9... | collective-permute-start | bytes 1572872 | tf_op jit(solution)/shard_map/ppermute | solution.py:21
  75.3 26.2 %collective-permute-start.4 = (bf16[2,128,1024]{2,1,0:T(8,128)(2,1)}, bf16[2,128,1024]{2,1,0:T(8,128)(2,1)S(1)}, u32[]{:S(2)}, u32[]{:S(2)}) collective-permute-start(bf16[2,128,1024]{2,1,0:T(8,128)(2,1)} %pad_maximum_fusion.8), channel_id=1, source_target_pairs={{0,2},{1,3},{2,0},{3,1},{4,6},{5,7},{6,4},{7,5},{8,10},{9,11},{10,... | collective-permute-start | bytes 1572872 | tf_op jit(solution)/shard_map/ppermute | solution.py:21
  77.7 24.7 %collective-permute-start.3 = (bf16[2,128,1024]{2,1,0:T(8,128)(2,1)}, bf16[2,128,1024]{2,1,0:T(8,128)(2,1)S(1)}, u32[]{:S(2)}, u32[]{:S(2)}) collective-permute-start(bf16[2,128,1024]{2,1,0:T(8,128)(2,1)} %pad_maximum_fusion.8), channel_id=1, source_target_pairs={{0,1},{1,2},{2,3},{3,0},{4,5},{5,6},{6,7},{7,4},{8,9},{9,10},{10,1... | collective-permute-start | bytes 1572872 | tf_op jit(solution)/shard_map/ppermute | solution.py:21
  111.0 9.9 %collective-permute-start.9 = (bf16[128,1024]{1,0:T(8,128)(2,1)S(1)}, bf16[128,1024]{1,0:T(8,128)(2,1)S(1)}, u32[]{:S(2)}, u32[]{:S(2)}) collective-permute-start(bf16[128,1024]{1,0:T(8,128)(2,1)S(1)} %get-tuple-element.55), channel_id=1, source_target_pairs={{0,1},{1,2},{2,3},{3,0},{4,5},{5,6},{6,7},{7,4},{8,9},{9,10},{10,1... | collective-permute-start | bytes 786440 | tf_op jit(solution)/shard_map/ppermute | solution.py:21
  112.5 10.7 %collective-permute-start.8 = (bf16[128,1024]{1,0:T(8,128)(2,1)S(1)}, bf16[128,1024]{1,0:T(8,128)(2,1)S(1)}, u32[]{:S(2)}, u32[]{:S(2)}) collective-permute-start(bf16[128,1024]{1,0:T(8,128)(2,1)S(1)} %get-tuple-element.56), channel_id=1, source_target_pairs={{0,2},{1,3},{2,0},{3,1},{4,6},{5,7},{6,4},{7,5},{8,10},{9,11},{10,... | collective-permute-start | bytes 786440 | tf_op jit(solution)/shard_map/ppermute | solution.py:21
  115.9 11.8 %collective-permute-start.7 = (bf16[128,1024]{1,0:T(8,128)(2,1)S(1)}, bf16[128,1024]{1,0:T(8,128)(2,1)S(1)}, u32[]{:S(2)}, u32[]{:S(2)}) collective-permute-start(bf16[128,1024]{1,0:T(8,128)(2,1)S(1)} %get-tuple-element.54), channel_id=1, source_target_pairs={{0,3},{1,0},{2,1},{3,2},{4,7},{5,4},{6,5},{7,6},{8,11},{9,8},{10,9... | collective-permute-start | bytes 786440 | tf_op jit(solution)/shard_map/ppermute | solution.py:21
  128.4 5.1 %collective-permute-start.10 = (bf16[128,1024]{1,0:T(8,128)(2,1)S(1)}, bf16[128,1024]{1,0:T(8,128)(2,1)S(1)}, u32[]{:S(2)}, u32[]{:S(2)}) collective-permute-start(bf16[128,1024]{1,0:T(8,128)(2,1)S(1)} %fusion.111), channel_id=1, source_target_pairs={{4,0},{8,4},{12,8},{16,12},{20,16},{24,20},{28,24},{32,28},{36,32}... | collective-permute-start | bytes 786440 | tf_op jit(solution)/shard_map/ppermute | solution.py:16
  130.8 2.6 %copy-start.3 = (f32[256,1024]{1,0:T(8,128)S(1)}, f32[256,1024]{1,0:T(8,128)}, u32[]{:S(2)}) copy-start(f32[256,1024]{1,0:T(8,128)} %copy-done.2) | copy-start | bytes 3145732
  132.3 44.8 %collective-permute-start.13 = (bf16[4,16,16,1024]{3,2,1,0:T(8,128)(2,1)}, bf16[4,16,16,1024]{3,2,1,0:T(8,128)(2,1)}, u32[]{:S(2)}, u32[]{:S(2)}) collective-permute-start(bf16[4,16,16,1024]{3,2,1,0:T(8,128)(2,1)} %pad_maximum_fusion.2), channel_id=1, source_target_pairs={{0,4},{4,0},{1,5},{5,1},{2,6},{6,2},{3,7},{7,3},{8,12},{12,8},{9,1... | collective-permute-start | bytes 6291464 | tf_op jit(solution)/shard_map/ppermute | solution.py:21
  139.2 37.9 %copy-start.1 = (bf16[4,8,16,1024]{3,2,1,0:T(8,128)(2,1)S(1)}, bf16[4,8,16,1024]{3,2,1,0:T(8,128)(2,1)}, u32[]{:S(2)}) copy-start(bf16[4,8,16,1024]{3,2,1,0:T(8,128)(2,1)} %get-tuple-element.50) | copy-start | bytes 3145732
  152.1 21.2 %all-to-all-start.4 = ((f32[32,8,512]{2,1,0:T(8,128)}), f32[32,8,512]{2,1,0:T(8,128)S(1)}, u32[]{:S(2)}, u32[]{:S(2)}) async-start(f32[32,8,512]{2,1,0:T(8,128)} %broadcast_in_dim.13), calls=%async_computation.4 | async-start | bytes 1048576 | tf_op jit(solution)/shard_map/all_to_all | solution.py:31
  173.3 9.7 %collective-permute-start.17 = (f32[8,512]{1,0:T(8,128)S(1)}, f32[8,512]{1,0:T(8,128)S(1)}, u32[]{:S(2)}, u32[]{:S(2)}) collective-permute-start(f32[8,512]{1,0:T(8,128)S(1)} %reduce_sum.399), channel_id=1, source_target_pairs={{0,3},{1,0},{2,1},{3,2},{4,7},{5,4},{6,5},{7,6},{8,11},{9,8},{10,9... | collective-permute-start | bytes 49160 | tf_op jit(solution)/shard_map/ppermute | solution.py:21
  174.5 9.8 %collective-permute-start.18 = (f32[8,512]{1,0:T(8,128)S(1)}, f32[8,512]{1,0:T(8,128)S(1)}, u32[]{:S(2)}, u32[]{:S(2)}) collective-permute-start(f32[8,512]{1,0:T(8,128)S(1)} %reduce_sum.399), channel_id=1, source_target_pairs={{0,2},{1,3},{2,0},{3,1},{4,6},{5,7},{6,4},{7,5},{8,10},{9,11},{10,... | collective-permute-start | bytes 49160 | tf_op jit(solution)/shard_map/ppermute | solution.py:21
  175.1 10.5 %collective-permute-start.19 = (f32[8,512]{1,0:T(8,128)S(1)}, f32[8,512]{1,0:T(8,128)S(1)}, u32[]{:S(2)}, u32[]{:S(2)}) collective-permute-start(f32[8,512]{1,0:T(8,128)S(1)} %reduce_sum.399), channel_id=1, source_target_pairs={{0,1},{1,2},{2,3},{3,0},{4,5},{5,6},{6,7},{7,4},{8,9},{9,10},{10,1... | collective-permute-start | bytes 49160 | tf_op jit(solution)/shard_map/ppermute | solution.py:21
  180.3 20.9 %collective-permute-start.16 = (bf16[16,16,1024]{2,1,0:T(8,128)(2,1)S(1)}, bf16[16,16,1024]{2,1,0:T(8,128)(2,1)S(1)}, u32[]{:S(2)}, u32[]{:S(2)}) collective-permute-start(bf16[16,16,1024]{2,1,0:T(8,128)(2,1)S(1)} %get-tuple-element.46), channel_id=1, source_target_pairs={{0,192},{64,0},{128,64},{192,128},{1,193},{65,1},{129,65},{193,129... | collective-permute-start | bytes 1572872 | tf_op jit(solution)/shard_map/ppermute | solution.py:21
  182.0 19.2 %collective-permute-start.15 = (bf16[16,16,1024]{2,1,0:T(8,128)(2,1)S(1)}, bf16[16,16,1024]{2,1,0:T(8,128)(2,1)S(1)}, u32[]{:S(2)}, u32[]{:S(2)}) collective-permute-start(bf16[16,16,1024]{2,1,0:T(8,128)(2,1)S(1)} %get-tuple-element.47), channel_id=1, source_target_pairs={{0,128},{64,192},{128,0},{192,64},{1,129},{65,193},{129,1},{193,65... | collective-permute-start | bytes 1572872 | tf_op jit(solution)/shard_map/ppermute | solution.py:21
  183.0 21.8 %collective-permute-start.14 = (bf16[16,16,1024]{2,1,0:T(8,128)(2,1)S(1)}, bf16[16,16,1024]{2,1,0:T(8,128)(2,1)S(1)}, u32[]{:S(2)}, u32[]{:S(2)}) collective-permute-start(bf16[16,16,1024]{2,1,0:T(8,128)(2,1)S(1)} %get-tuple-element.45), channel_id=1, source_target_pairs={{0,64},{64,128},{128,192},{192,0},{1,65},{65,129},{129,193},{193,1... | collective-permute-start | bytes 1572872 | tf_op jit(solution)/shard_map/ppermute | solution.py:21
  184.3 27.5 %collective-permute-start.12 = (f32[15,1024]{1,0:T(8,128)}, f32[15,1024]{1,0:T(8,128)S(1)}, u32[]{:S(2)}, u32[]{:S(2)}) collective-permute-start(f32[15,1024]{1,0:T(8,128)} %get-tuple-element.53), channel_id=1, source_target_pairs={{0,4},{4,8},{8,12},{12,16},{16,20},{20,24},{24,28},{28,32},{32,36}... | collective-permute-start | bytes 184328 | tf_op jit(solution)/shard_map/ppermute | solution.py:16
  185.6 26.2 %collective-permute-start.11 = (f32[15,1024]{1,0:T(8,128)S(1)}, f32[15,1024]{1,0:T(8,128)S(1)}, u32[]{:S(2)}, u32[]{:S(2)}) collective-permute-start(f32[15,1024]{1,0:T(8,128)S(1)} %get-tuple-element.52), channel_id=1, source_target_pairs={{4,0},{8,4},{12,8},{16,12},{20,16},{24,20},{28,24},{32,28},{36,32}... | collective-permute-start | bytes 184328 | tf_op jit(solution)/shard_map/ppermute | solution.py:16
  186.9 24.9 %copy-start.4 = (f32[256,1024]{1,0:T(8,128)S(1)}, f32[256,1024]{1,0:T(8,128)}, u32[]{:S(2)}) copy-start(f32[256,1024]{1,0:T(8,128)} %get-tuple-element.108) | copy-start | bytes 3145732
  201.2 17.3 %collective-permute-start.20 = (f32[4,8,512]{2,1,0:T(8,128)S(1)}, f32[4,8,512]{2,1,0:T(8,128)S(1)}, u32[]{:S(2)}, u32[]{:S(2)}) collective-permute-start(f32[4,8,512]{2,1,0:T(8,128)S(1)} %pad_maximum_fusion.15), channel_id=1, source_target_pairs={{0,4},{4,0},{1,5},{5,1},{2,6},{6,2},{3,7},{7,3},{8,12},{12,8},{9,1... | collective-permute-start | bytes 196616 | tf_op jit(solution)/shard_map/ppermute | solution.py:21
  206.0 23.4 %all-to-all-start.2 = ((bf16[8,2,16,1024]{3,2,1,0:T(8,128)(2,1)}), bf16[8,2,16,1024]{3,2,1,0:T(8,128)(2,1)S(1)}, u32[]{:S(2)}, u32[]{:S(2)}) async-start(bf16[8,2,16,1024]{3,2,1,0:T(8,128)(2,1)} %copy.14), calls=%async_computation.2 | async-start | bytes 1048576 | tf_op jit(solution)/shard_map/all_to_all | solution.py:31
  218.5 11.7 %copy-start.6 = (f32[32,1024]{1,0:T(8,128)}, f32[32,1024]{1,0:T(8,128)S(1)}, u32[]{:S(2)}) copy-start(f32[32,1024]{1,0:T(8,128)S(1)} %reshape.104) | copy-start | bytes 393220
